TPU v7x, 32 devices: a whole 2x2x4 slice. The times are simulated.
32 devices in a mesh: dp: 8 (over y, x, core), tensor: 4 (over z).
Axes of the slice: x: 2, y: 2, z: 4, core: 2. Of those that a mesh axis runs over, the one named last changes fastest.
Arguments:
- inputs: float32 [8192, 1536], P(('dp', 'tensor')), may hold values from -80 to 80
- norm_gains: float32 [1, 2, 1536], replicated, may hold values from 0.5 to 1.5
- w_qkv: bfloat16 [1, 1536, 3072], P(None, 'dp', 'tensor'), may hold values from -0.15625 to 0.15625
- w_gate_up: bfloat16 [1, 1536, 2, 4096], P(None, 'dp', None, 'tensor'), may hold values from -0.15625 to 0.15625
- w_out: bfloat16 [1, 1536, 1536], P(None, 'dp', 'tensor'), may hold values from -2.5 to 2.5
- w_down: bfloat16 [1, 1536, 4096], P(None, 'dp', 'tensor'), may hold values from -0.09375 to 0.09375
- segments: int32 [8192], P('dp'), may hold values from 0 to 8, as said below
- positions: int32 [8192], P('dp'), may hold values from 0 to 799, as said below
- cotangent: bfloat16 [8192, 1536], P(('dp', 'tensor')), may hold values from -6 to 6
Outputs:
- output: float32 [8192, 1536], P(('dp', 'tensor'))
- input_grad: float32 [8192, 1536], P(('dp', 'tensor'))
- grad_qkv: float32 [1, 1536, 3072], P(None, 'dp', 'tensor')
- grad_gate_up: float32 [1, 1536, 2, 4096], P(None, 'dp', None, 'tensor')
- grad_out: float32 [1, 1536, 1536], P(None, 'dp', 'tensor')
- grad_down: float32 [1, 1536, 4096], P(None, 'dp', 'tensor')
- grad_gains: float32 [1, 2, 1536], replicated
- rms_stats: float32 [1, 4], replicated
Inputs may be any that keep to these rules, and one draw needn't show every extreme that they name: `segments`: within each group of 1024 consecutive tokens (one index of dp), the tokens form blocks of 32: 24 prompt blocks with segment 0 and one block for each continuation 1 to 8, in a drawn order of blocks. Within a group the prompt's tokens have positions 0 to 767, rising along the group; each continuation's tokens have positions 768 to 799 in order.
All inputs are finite; a program needn't handle non-finite values.
Results may differ from a plain program's by a relative error of at most 0.012.
The roundings to bfloat16 on the way count: a program that leaves them out, or rounds other values in their place, can miss the bound.
Values may be sent and summed in bfloat16 or wider, within the bound.
A program may use at most 192 MiB of HBM per device.

v0:
```python
import jax
import jax.numpy as jnp
from jax import lax
from jax.sharding import PartitionSpec as P

HEADS = 16
KV_HEADS = 8
HEAD_WIDTH = 96


norm_eps = 1e-05
rope_base = 100000.0


def rope_tables(position, head_dim):
    freq_steps = jnp.arange(head_dim // 2, dtype=jnp.float32) * (2.0 / head_dim)
    inverse = jnp.power(rope_base, -freq_steps)
    angles = position.astype(jnp.float32)[:, None] * inverse[None, :]
    return (jnp.cos(angles), jnp.sin(angles))


def rotate(values, cosine_table, sine_table):
    half_dim = values.shape[-1] // 2
    first_half = values[..., :half_dim]
    second_half = values[..., half_dim:]
    return jnp.concatenate(
        [
            first_half * cosine_table - second_half * sine_table,
            second_half * cosine_table + first_half * sine_table,
        ],
        axis=-1,
    )


def visible(query_segment, query_position, key_segment, key_position):
    same_doc = (key_segment[None, :] == 0) | (key_segment[None, :] == query_segment[:, None])
    return same_doc & (key_position[None, :] <= query_position[:, None])


def normalize(values, gain):
    inverse = lax.rsqrt(jnp.mean(values * values, axis=-1, keepdims=True) + norm_eps)
    return (values * inverse * gain, inverse)


def norm_back(values, inverse, gain, grad_normed):
    scaled = grad_normed * gain
    grad_gain = jnp.sum(grad_normed * values * inverse, axis=0)
    grad_values = inverse * scaled - values * inverse**3 * jnp.mean(
        scaled * values, axis=-1, keepdims=True
    )
    return (grad_values, grad_gain)


def spread_rows(values):
    return lax.all_gather(values, "tensor", axis=0, tiled=True)


def collect_rows(values):
    return lax.psum_scatter(values, "tensor", scatter_dimension=0, tiled=True)


def spread_grads(values):
    return lax.all_gather(values, "tensor", axis=0, tiled=True)


def collect_grads(values):
    return lax.psum_scatter(values, "tensor", scatter_dimension=0, tiled=True)


def refold(normed_local, grad_rows):
    return jnp.einsum(
        "td,tc->dc",
        lax.all_gather(normed_local, "tensor", axis=0, tiled=True),
        grad_rows,
        preferred_element_type=jnp.float32,
    )


def per_device(inputs, norm_gains, w_qkv, w_gate_up, w_out, w_down, segments, positions, cotangent):
    layers = w_qkv.shape[0]
    head_dim = HEAD_WIDTH
    repeat = HEADS // KV_HEADS
    kv_local = w_out.shape[2] // (repeat * head_dim)
    ff_local = w_down.shape[2]
    group_len = segments.shape[0]
    blocks = 2
    block_len = group_len // blocks
    score_scale = head_dim ** (-0.5)
    cosine_table, sine_table = rope_tables(positions, head_dim)
    cosine_wide = cosine_table[:, None, None, :]
    sine_wide = sine_table[:, None, None, :]
    block_segments = segments.reshape(blocks, block_len)
    block_positions = positions.reshape(blocks, block_len)
    layer_index = 0
    gathered = (
        lax.all_gather(w_qkv[layer_index], "dp", axis=0, tiled=True),
        lax.all_gather(w_gate_up[layer_index], "dp", axis=0, tiled=True),
        lax.all_gather(w_out[layer_index], "dp", axis=0, tiled=True),
        lax.all_gather(w_down[layer_index], "dp", axis=0, tiled=True),
    )
    qkv_full, gate_up_full, out_full, down_full = gathered
    normed_one, inverse_one = normalize(inputs, norm_gains[layer_index, 0])
    normed_one = normed_one.astype(jnp.bfloat16)
    normed_rows = spread_rows(normed_one)
    joined_rows = jnp.dot(normed_rows, qkv_full, preferred_element_type=jnp.float32)
    joined_rows = joined_rows.reshape(group_len, kv_local, repeat + 2, head_dim)
    query_matrix = rotate(joined_rows[:, :, :repeat], cosine_wide, sine_wide).astype(jnp.bfloat16)
    key_matrix = rotate(joined_rows[:, :, repeat], cosine_wide[:, :, 0], sine_wide[:, :, 0]).astype(
        jnp.bfloat16
    )
    value_matrix = joined_rows[:, :, repeat + 1].astype(jnp.bfloat16)

    def attend_block(block_item):
        query_block, block_segment, block_position = block_item
        allowed = visible(block_segment, block_position, segments, positions)
        attention_scores = (
            jnp.einsum(
                "mely,cey->elmc", query_block, key_matrix, preferred_element_type=jnp.float32
            )
            * score_scale
        )
        attention_scores = jnp.where(allowed[None, None], attention_scores, -1e30)
        row_top = jnp.max(attention_scores, axis=-1, keepdims=True)
        weights = jnp.exp(attention_scores - row_top)
        row_total = jnp.sum(weights, axis=-1, keepdims=True)
        probability_lowered = (weights / row_total).astype(jnp.bfloat16)
        mixed_rows_block = jnp.einsum(
            "zbvq,qzo->vzbo", probability_lowered, value_matrix, preferred_element_type=jnp.float32
        )
        return (mixed_rows_block.astype(jnp.bfloat16), (row_top + jnp.log(row_total))[..., 0])

    mixed_all, log_sums = lax.map(
        attend_block,
        (
            query_matrix.reshape(blocks, block_len, kv_local, repeat, head_dim),
            block_segments,
            block_positions,
        ),
    )
    attended = mixed_all.reshape(group_len, kv_local * repeat * head_dim)
    branch = collect_rows(
        jnp.einsum("tk,dk->td", attended, out_full, preferred_element_type=jnp.float32)
    )
    middle = inputs + branch
    normed_two, inverse_two = normalize(middle, norm_gains[layer_index, 1])
    normed_two = normed_two.astype(jnp.bfloat16)
    ff_kept = None
    normed_rows_two = spread_rows(normed_two)
    gate_up = jnp.einsum(
        "td,dcf->tcf", normed_rows_two, gate_up_full, preferred_element_type=jnp.float32
    )
    product = (jax.nn.silu(gate_up[:, 0]) * gate_up[:, 1]).astype(jnp.bfloat16)
    branch_two = collect_rows(
        jnp.einsum("tf,df->td", product, down_full, preferred_element_type=jnp.float32)
    )
    output = middle + branch_two
    stat_rows = [
        jnp.stack(
            [
                jnp.sum(middle * middle),
                jnp.sum(output * output),
                jnp.sum(branch * branch),
                jnp.sum(branch_two * branch_two),
            ]
        )
    ]
    kept_items = [
        (
            inputs,
            inverse_one,
            normed_one,
            normed_rows,
            middle,
            inverse_two,
            normed_two,
            normed_rows_two,
            query_matrix,
            key_matrix,
            value_matrix,
            attended,
            log_sums,
            gate_up,
            product,
            gathered,
            ff_kept,
        )
    ]
    grad_hidden = cotangent.astype(jnp.float32)
    grad_qkv_list = [None] * layers
    grad_gu_list = [None] * layers
    grad_out_list = [None] * layers
    grad_down_list = [None] * layers
    gain_list = [None] * layers
    for layer_index in reversed(range(layers)):
        (
            hidden_in,
            inverse_one,
            normed_one,
            normed_rows,
            middle,
            inverse_two,
            normed_two,
            normed_rows_two,
            query_matrix,
            key_matrix,
            value_matrix,
            attended,
            log_sums,
            gate_up,
            product,
            gathered,
            ff_kept,
        ) = kept_items[layer_index]
        qkv_full, gate_up_full, out_full, down_full = (
            lax.all_gather(w_qkv[layer_index], "dp", axis=0, tiled=True),
            lax.all_gather(w_gate_up[layer_index], "dp", axis=0, tiled=True),
            lax.all_gather(w_out[layer_index], "dp", axis=0, tiled=True),
            lax.all_gather(w_down[layer_index], "dp", axis=0, tiled=True),
        )
        gate_rows = gate_up[:, 0]
        up_rows = gate_up[:, 1]
        sigmoid_gate = jax.nn.sigmoid(gate_rows)
        grad_two = spread_grads(grad_hidden.astype(jnp.bfloat16))
        grad_product = jnp.einsum(
            "td,df->tf", grad_two, down_full, preferred_element_type=jnp.float32
        )
        grad_down_w = jnp.einsum("td,tf->df", grad_two, product, preferred_element_type=jnp.float32)
        grad_gate = (
            grad_product * up_rows * (sigmoid_gate * (1.0 + gate_rows * (1.0 - sigmoid_gate)))
        )
        grad_up = grad_product * (gate_rows * sigmoid_gate)
        grad_gate_up = jnp.stack([grad_gate, grad_up], axis=1).astype(jnp.bfloat16)
        grad_gu_w = refold(normed_two, grad_gate_up.reshape(group_len, 2 * ff_local)).reshape(
            -1, 2, ff_local
        )
        grad_normed_two = collect_grads(
            jnp.einsum(
                "tcf,dcf->td", grad_gate_up, gate_up_full, preferred_element_type=jnp.float32
            )
        )
        grad_middle, grad_gain_two = norm_back(
            middle, inverse_two, norm_gains[layer_index, 1], grad_normed_two
        )
        grad_middle = grad_middle + grad_hidden
        grad_one = spread_grads(grad_middle.astype(jnp.bfloat16))
        grad_attended = jnp.einsum(
            "td,dk->tk", grad_one, out_full, preferred_element_type=jnp.float32
        ).astype(jnp.bfloat16)
        grad_out_w = jnp.einsum("td,tk->dk", grad_one, attended, preferred_element_type=jnp.float32)

        def back_block(running_grads, block_item):
            grad_keys, grad_values = running_grads
            query_block, block_gradient, block_sums, block_segment, block_position = block_item
            allowed = visible(block_segment, block_position, segments, positions)
            attention_scores = (
                jnp.einsum(
                    "mely,cey->elmc", query_block, key_matrix, preferred_element_type=jnp.float32
                )
                * score_scale
            )
            attention_scores = jnp.where(allowed[None, None], attention_scores, -1e30)
            probability_full = jnp.exp(attention_scores - block_sums[..., None])
            grad_probs = jnp.einsum(
                "mely,cey->elmc", block_gradient, value_matrix, preferred_element_type=jnp.float32
            )
            row_delta = jnp.sum(probability_full * grad_probs, axis=-1, keepdims=True)
            score_gradient = (probability_full * (grad_probs - row_delta)).astype(jnp.bfloat16)
            grad_query = (
                jnp.einsum(
                    "zbvq,qzo->vzbo", score_gradient, key_matrix, preferred_element_type=jnp.float32
                )
                * score_scale
            )
            grad_keys = (
                grad_keys
                + jnp.einsum(
                    "wqpv,pwqo->vwo",
                    score_gradient,
                    query_block,
                    preferred_element_type=jnp.float32,
                )
                * score_scale
            )
            grad_values = grad_values + jnp.einsum(
                "wqpv,pwqo->vwo",
                probability_full.astype(jnp.bfloat16),
                block_gradient,
                preferred_element_type=jnp.float32,
            )
            return ((grad_keys, grad_values), grad_query)

        zero_rows = jnp.zeros((group_len, kv_local, head_dim), jnp.float32)
        (grad_keys, grad_values), grad_query = lax.scan(
            back_block,
            (zero_rows, zero_rows),
            (
                query_matrix.reshape(blocks, block_len, kv_local, repeat, head_dim),
                grad_attended.reshape(blocks, block_len, kv_local, repeat, head_dim),
                log_sums,
                block_segments,
                block_positions,
            ),
        )
        grad_query = rotate(
            grad_query.reshape(group_len, kv_local, repeat, head_dim), cosine_wide, -sine_wide
        )
        grad_keys = rotate(grad_keys, cosine_wide[:, :, 0], -sine_wide[:, :, 0])
        grad_joined = jnp.concatenate(
            [grad_query, grad_keys[:, :, None], grad_values[:, :, None]], axis=2
        )
        grad_joined = grad_joined.reshape(group_len, kv_local * (repeat + 2) * head_dim).astype(
            jnp.bfloat16
        )
        grad_qkv_w = refold(normed_one, grad_joined)
        grad_normed_one = collect_grads(
            jnp.einsum("tc,dc->td", grad_joined, qkv_full, preferred_element_type=jnp.float32)
        )
        grad_input, grad_gain_one = norm_back(
            hidden_in, inverse_one, norm_gains[layer_index, 0], grad_normed_one
        )
        grad_hidden = grad_input + grad_middle
        shards = (
            lax.psum_scatter(grad_qkv_w, "dp", scatter_dimension=0, tiled=True),
            lax.psum_scatter(grad_gu_w, "dp", scatter_dimension=0, tiled=True),
            lax.psum_scatter(grad_out_w, "dp", scatter_dimension=0, tiled=True),
            lax.psum_scatter(grad_down_w, "dp", scatter_dimension=0, tiled=True),
        )
        grad_qkv_list[layer_index] = shards[0]
        grad_gu_list[layer_index] = shards[1]
        grad_out_list[layer_index] = shards[2]
        grad_down_list[layer_index] = shards[3]
        gain_list[layer_index] = jnp.stack([grad_gain_one, grad_gain_two])
    gain_total, stat_total = lax.psum(
        (jnp.stack(gain_list), jnp.stack(stat_rows)), ("dp", "tensor")
    )
    cell_count = inputs.shape[0] * inputs.shape[1] * lax.axis_size("dp") * lax.axis_size("tensor")
    rms_values = jnp.sqrt(stat_total / cell_count)
    return (
        output,
        grad_hidden,
        jnp.stack(grad_qkv_list),
        jnp.stack(grad_gu_list),
        jnp.stack(grad_out_list),
        jnp.stack(grad_down_list),
        gain_total,
        rms_values,
    )


def solution(mesh):
    placed = (
        P(("dp", "tensor"), None),
        P(),
        P(None, "dp", "tensor"),
        P(None, "dp", None, "tensor"),
        P(None, "dp", "tensor"),
        P(None, "dp", "tensor"),
        P("dp"),
        P("dp"),
        P(("dp", "tensor"), None),
    )
    return jax.shard_map(
        per_device,
        mesh=mesh,
        in_specs=placed,
        out_specs=(
            P(("dp", "tensor"), None),
            P(("dp", "tensor"), None),
            P(None, "dp", "tensor"),
            P(None, "dp", None, "tensor"),
            P(None, "dp", "tensor"),
            P(None, "dp", "tensor"),
            P(),
            P(),
        ),
        check_vma=False,
    )
```

profile of v0, /device:TPU:0, one launch (start us, length us, event | category | flops | bytes accessed | tf_op | source)
XLA Modules:
  0.0 1162.8 jit_solution(16583962716732105338)
XLA Ops:
  15.8 25.8 %all-gather.21.cloned.1.call-done = bf16[1,1536,768]{2,1,0:T(8,128)(2,1)} async-done(((bf16[1,192,768]{2,1,0:T(8,128)(2,1)}), bf16[1,1536,768]{2,1,0:T(8,128)(2,1)}) %all-gather.21.cloned.1.call-update) | async-done | bytes 2359312 | tf_op jit(solution)/shard_map/all_gather | solution.py:96
  41.7 65.7 %all-gather.13.cloned.1.call-done = bf16[1024,1536]{1,0:T(8,128)(2,1)} async-done(((bf16[256,1536]{1,0:T(8,128)(2,1)}), bf16[1024,1536]{1,0:T(8,128)(2,1)}) %all-gather.13.cloned.1.call-update) | async-done | bytes 3145744 | tf_op jit(solution)/shard_map/all_gather | solution.py:55
  107.3 5.3 fusion.69
  115.7 18.8 %while.27 = (s32[]{:T(128)}, bf16[2,512,2,2,96]{1,4,3,2,0:T(8,128)(2,1)S(1)}, f32[2,2,2,512]{3,2,1,0:T(2,128)}, s32[1024]{0:T(1024)S(1)}, s32[2,512]{1,0:T(2,128...) while((s32[]{:T(128)}, ...), condition=%wide.region_4.5_spmd, body=%wide.region_1.4_spmd.sunk | while | flops 832764928 | bytes 28928132 | solution.py:132
  135.5 6.0 fusion.72
  142.1 108.9 %reduce-scatter.11.cloned.1.call-done = f32[256,1536]{1,0:T(8,128)} async-done(((f32[1024,1536]{1,0:T(8,128)}), f32[256,1536]{1,0:T(8,128)}) %reduce-scatter.11.cloned.1.call-update) | async-done | bytes 1572880 | tf_op jit(solution)/shard_map/reduce_scatter | solution.py:59
  257.4 41.5 %all-gather.25.cloned.1.call-done = bf16[1,1536,2,1024]{3,2,0,1:T(2,128)(2,1)} async-done(((bf16[1,192,2,1024]{3,2,0,1:T(2,128)(2,1)}), bf16[1,1536,2,1024]{3,2,0,1:T(2,128)(2,1)}) %all-gather.25.cloned.1.call-update) | async-done | bytes 6291472 | tf_op jit(solution)/shard_map/all_gather | solution.py:97
  298.9 16.5 %copy.45 = bf16[1,1536,2,1024]{1,3,2,0:T(8,128)(2,1)} copy(bf16[1,1536,2,1024]{3,2,0,1:T(2,128)(2,1)} %all-gather.25.cloned.1.call-done) | data formatting | bytes 12582912 | tf_op jit(solution)/shard_map/all_gather | solution.py:97
  315.3 49.1 %all-gather.15.cloned.1.call-done = bf16[1024,1536]{1,0:T(8,128)(2,1)} async-done(((bf16[256,1536]{1,0:T(8,128)(2,1)}), bf16[1024,1536]{1,0:T(8,128)(2,1)}) %all-gather.15.cloned.1.call-update) | async-done | bytes 3145744 | tf_op jit(solution)/shard_map/all_gather | solution.py:55
  364.4 11.7 %fusion.53 = f32[1024,2,1024]{0,2,1:T(8,128)} fusion(bf16[1,1536,2,1024]{1,3,2,0:T(8,128)(2,1)} %copy.45, bf16[1024,1536]{1,0:T(8,128)(2,1)} %all-gather.15.cloned.1.call-done), kind=kOutput, calls=%fused_computation.68 | convolution fusion | flops 6442450944 | bytes 17825792 | tf_op jit(solution)/shard_map/td,dcf->tcf/dot_general | solution.py:149
  376.1 52.0 %all-gather.17.cloned.1.call-done = bf16[1024,1536]{1,0:T(8,128)(2,1)} async-done(((bf16[256,1536]{1,0:T(8,128)(2,1)}), bf16[1024,1536]{1,0:T(8,128)(2,1)}) %all-gather.17.cloned.1.call-update) | async-done | bytes 3145744 | tf_op jit(solution)/shard_map/all_gather | solution.py:63
  428.1 32.9 %all-gather.27.cloned.1.call-done = bf16[1,1536,1024]{2,1,0:T(8,128)(2,1)} async-done(((bf16[1,192,1024]{2,1,0:T(8,128)(2,1)}), bf16[1,1536,1024]{2,1,0:T(8,128)(2,1)}) %all-gather.27.cloned.1.call-update) | async-done | bytes 3145744 | tf_op jit(solution)/shard_map/all_gather | solution.py:99
  461.0 10.2 multiply_bitcast_fusion.1
  473.2 10.8 fusion.55
  484.3 5.0 multiply_convert_fusion
  490.7 5.4 fusion.63
  496.2 98.7 %reduce-scatter.15.cloned.1.call-done = f32[256,1536]{1,0:T(8,128)} async-done(((f32[1024,1536]{1,0:T(8,128)}), f32[256,1536]{1,0:T(8,128)}) %reduce-scatter.15.cloned.1.call-update) | async-done | bytes 1572880 | tf_op jit(solution)/shard_map/reduce_scatter | solution.py:67
  598.4 110.0 %reduce-scatter.13.cloned.1.call-done = f32[256,1536]{1,0:T(8,128)} async-done(((f32[1024,1536]{1,0:T(8,128)}), f32[256,1536]{1,0:T(8,128)}) %reduce-scatter.13.cloned.1.call-update) | async-done | bytes 1572880 | tf_op jit(solution)/shard_map/reduce_scatter | solution.py:59
  708.4 5.4 multiply_reduce_fusion.2
  713.9 8.6 convolution_bitcast_fusion.1
  722.4 6.7 copy.69
  730.7 11.7 %fusion.58 = f32[1536,2,1024]{2,0,1:T(8,128)} fusion(bf16[1024,1536]{1,0:T(8,128)(2,1)} %all-gather.15.cloned.1.call-done, bf16[1024,1,1024]{0,2,1:T(8,128)(2,1)} %copy-done.26, bf16[1024,1,1024]{0,2,1:T(8,128)(2,1)S(1)} %copy-done.25), kind=kOutput, calls=%fused_computation.74 | convolution fusion | flops 6450839552 | bytes 19922944 | tf_op jit(solution)/shard_map/td,tc->dc/dot_general | solution.py:71
  742.5 35.5 %all-gather.19.cloned.1.call-done = bf16[1024,1536]{1,0:T(8,128)(2,1)} async-done(((bf16[256,1536]{1,0:T(8,128)(2,1)}), bf16[1024,1536]{1,0:T(8,128)(2,1)}) %all-gather.19.cloned.1.call-update) | async-done | bytes 3145744 | tf_op jit(solution)/shard_map/all_gather | solution.py:63
  789.4 63.6 %while.28 = (s32[]{:T(128)}, f32[1024,2,96]{0,2,1:T(8,128)S(1)}, f32[1024,2,96]{0,2,1:T(8,128)}, f32[2,512,2,2,96]{1,0,4,3,2:T(2,128)}, bf16[2,512,2,2,96]{1,4,3...) while((s32[]{:T(128)}, f32[1024,2,96]{0,2,1:T(8,128)S(1)}, ...), condition=%wide.region_12.13_spmd.clone, body=%wide.region_10.12_spmd.clone.sunk | while | flops 2047998976 | bytes 74926256 | solution.py:293
  805.9 15.0 %dynamic_update_slice.20 = f32[2,512,2,2,96]{1,0,4,3,2:T(2,128)} dynamic-update-slice(f32[2,512,2,2,96]{1,0,4,3,2:T(2,128)} %get-tuple-element.557, f32[1,512,2,2,96]{1,0,4,3,2:T(1,128)S(1)} %copy.86, s32[]{:T(128)S(6)} %copy.103, s32[]{:T(128)} %constant.42.clone.1..sunk, s32[]{:T(128)} %constant.42.clone.1..sunk, s32[]{:T(128)} %constant.42.clone.1..sunk, s32[]{:T(128)} %constant.42.clone.1..sunk) | dynamic-update-slice | bytes 1572868 | tf_op jit(solution)/shard_map/while/body/jit(dynamic_update_index_in_dim)/dynamic_update_slice | solution.py:293
  838.0 15.0 %dynamic_update_slice.20 = f32[2,512,2,2,96]{1,0,4,3,2:T(2,128)} dynamic-update-slice(f32[2,512,2,2,96]{1,0,4,3,2:T(2,128)} %get-tuple-element.557, f32[1,512,2,2,96]{1,0,4,3,2:T(1,128)S(1)} %copy.86, s32[]{:T(128)S(6)} %copy.103, s32[]{:T(128)} %constant.42.clone.1..sunk, s32[]{:T(128)} %constant.42.clone.1..sunk, s32[]{:T(128)} %constant.42.clone.1..sunk, s32[]{:T(128)} %constant.42.clone.1..sunk) | dynamic-update-slice | bytes 1572868 | tf_op jit(solution)/shard_map/while/body/jit(dynamic_update_index_in_dim)/dynamic_update_slice | solution.py:293
  866.0 5.2 fusion.82
  871.3 6.8 fusion.81
  883.5 54.5 %reduce-scatter.21.cloned.1.call-done = f32[192,2,1024]{2,0,1:T(8,128)} async-done(((f32[1536,2,1024]{2,0,1:T(8,128)}), f32[192,2,1024]{2,0,1:T(8,128)}) %reduce-scatter.21.cloned.1.call-update) | async-done | bytes 1572880 | tf_op jit(solution)/shard_map/reduce_scatter | solution.py:324
  941.8 109.3 %reduce-scatter.17.cloned.1.call-done = f32[256,1536]{1,0:T(8,128)} async-done(((f32[1024,1536]{1,0:T(8,128)}), f32[256,1536]{1,0:T(8,128)}) %reduce-scatter.17.cloned.1.call-update) | async-done | bytes 1572880 | tf_op jit(solution)/shard_map/reduce_scatter | solution.py:67
  1052.9 41.0 %all-reduce = (f32[1,2,1536]{2,1,0:T(2,128)}, f32[1,4]{1,0:T(1,128)S(1)}) all-reduce(f32[1,2,1536]{2,1,0:T(2,128)S(1)} %maximum_bitcast_fusion.1, f32[1,4]{1,0:T(1,128)S(1)} %maximum_bitcast_fusion.2), channel_id=1, replica_groups=mesh['dp'=8,'tensor'=4] {'dp','tensor'}, use_global_device_ids=true, to_apply=%region_21.22 | all-reduce | flops 3076 | bytes 24608 | tf_op jit(solution)/shard_map/psum | solution.py:333
  1098.3 57.8 %reduce-scatter.19.cloned.1.call-done = f32[192,768]{1,0:T(8,128)} async-done(((f32[1536,768]{1,0:T(8,128)}), f32[192,768]{1,0:T(8,128)}) %reduce-scatter.19.cloned.1.call-update) | async-done | bytes 589840 | tf_op jit(solution)/shard_map/reduce_scatter | solution.py:323
  (176 shorter events, 119.2 us)
Async XLA Ops:
  7.2 7.1 copy-start.13
  7.2 7.2 copy-start.10
  7.2 34.5 %all-gather.21.cloned.1.call-start = ((), (), s32[]{:S(2)}) async-start(), calls=%async_computation.19 | async-start | bytes 2654208 | tf_op jit(solution)/shard_map/all_gather | solution.py:96
  7.9 99.4 %all-gather.13.cloned.1.call-start = ((), (), s32[]{:S(2)}) async-start(), calls=%async_computation.8 | async-start | bytes 3932160 | tf_op jit(solution)/shard_map/all_gather | solution.py:55
  8.8 245.4 %copy-start.16 = (f32[1536]{0:T(1024)}, f32[1536]{0:T(1024)S(1)}, u32[]{:S(2)}) copy-start(f32[1536]{0:T(1024)S(1)} %get-tuple-element.265) | copy-start | bytes 18436
  11.0 101.7 %copy-start.18 = (f32[256]{0:T(256)}, f32[256]{0:T(256)S(1)}, u32[]{:S(2)}) copy-start(f32[256]{0:T(256)S(1)} %get-tuple-element.347) | copy-start | bytes 3076
  13.5 122.0 %all-gather.23.cloned.1.call-start = ((), (), s32[]{:S(2)}) async-start(), calls=%async_computation.20 | async-start | bytes 1327104 | tf_op jit(solution)/shard_map/all_gather | solution.py:98
  14.2 236.8 %reduce-scatter.11.cloned.1.call-start = ((), (), s32[]{:S(2)}) async-start(), calls=%async_computation.9 | async-start | bytes 7864320 | tf_op jit(solution)/shard_map/reduce_scatter | solution.py:59
  15.8 98.0 %copy-start.4 = (f32[1024,48]{0,1:T(8,128)}, f32[1024,48]{0,1:T(8,128)S(1)}, u32[]{:S(2)}) copy-start(f32[1024,48]{0,1:T(8,128)S(1)} %get-tuple-element.345) | copy-start | bytes 589828
  135.4 6.0 copy-start.6
  141.5 109.6 %copy-start = (f32[256,1536]{1,0:T(8,128)S(1)}, f32[256,1536]{1,0:T(8,128)}, u32[]{:S(2)}) copy-start(f32[256,1536]{1,0:T(8,128)} %param.13) | copy-start | bytes 4718596
  141.5 157.4 %all-gather.25.cloned.1.call-start = ((), (), s32[]{:S(2)}) async-start(), calls=%async_computation.21 | async-start | bytes 7077888 | tf_op jit(solution)/shard_map/all_gather | solution.py:97
  142.1 222.3 %all-gather.15.cloned.1.call-start = ((), (), s32[]{:S(2)}) async-start(), calls=%async_computation.10 | async-start | bytes 3932160 | tf_op jit(solution)/shard_map/all_gather | solution.py:55
  254.2 61.1 %copy-start.20 = (f32[256]{0:T(256)}, f32[256]{0:T(256)S(1)}, u32[]{:S(2)}) copy-start(f32[256]{0:T(256)S(1)} %get-tuple-element.349) | copy-start | bytes 3076
  255.8 172.3 %all-gather.17.cloned.1.call-start = ((), (), s32[]{:S(2)}) async-start(), calls=%async_computation.12 | async-start | bytes 3932160 | tf_op jit(solution)/shard_map/all_gather | solution.py:63
  256.6 204.5 %all-gather.27.cloned.1.call-start = ((), (), s32[]{:S(2)}) async-start(), calls=%async_computation.22 | async-start | bytes 3538944 | tf_op jit(solution)/shard_map/all_gather | solution.py:99
  257.3 337.6 %reduce-scatter.15.cloned.1.call-start = ((), (), s32[]{:S(2)}) async-start(), calls=%async_computation.13 | async-start | bytes 7864320 | tf_op jit(solution)/shard_map/reduce_scatter | solution.py:67
  484.0 224.4 %reduce-scatter.13.cloned.1.call-start = ((), (), s32[]{:S(2)}) async-start(), calls=%async_computation.11 | async-start | bytes 7864320 | tf_op jit(solution)/shard_map/reduce_scatter | solution.py:59
  484.3 6.4 copy-start.22
  496.1 98.8 %copy-start.3 = (f32[256,1536]{1,0:T(8,128)S(1)}, f32[256,1536]{1,0:T(8,128)}, u32[]{:S(2)}) copy-start(f32[256,1536]{1,0:T(8,128)} %copy-done.2) | copy-start | bytes 4718596
  496.2 212.2 %copy-start.8 = (bf16[256,1536]{1,0:T(8,128)(2,1)S(1)}, bf16[256,1536]{1,0:T(8,128)(2,1)}, u32[]{:S(2)}) copy-start(bf16[256,1536]{1,0:T(8,128)(2,1)} %param.21) | copy-start | bytes 2359300
  496.2 281.8 %all-gather.19.cloned.1.call-start = ((), (), s32[]{:S(2)}) async-start(), calls=%async_computation.14 | async-start | bytes 3932160 | tf_op jit(solution)/shard_map/all_gather | solution.py:63
  713.8 164.3 %reduce-scatter.25.cloned.1.call-start = ((), (), s32[]{:S(2)}) async-start(), calls=%async_computation.23 | async-start | bytes 7077888
  729.1 208.9 %reduce-scatter.21.cloned.1.call-start = ((), (), s32[]{:S(2)}) async-start(), calls=%async_computation.17 | async-start | bytes 14155776 | tf_op jit(solution)/shard_map/reduce_scatter | solution.py:324
  742.4 35.6 %copy-start.12 = (bf16[1,1536,384]{2,1,0:T(8,128)(2,1)S(1)}, bf16[1,1536,384]{2,1,0:T(8,128)(2,1)}, u32[]{:S(2)}) copy-start(bf16[1,1536,384]{2,1,0:T(8,128)(2,1)} %all-gather.23.cloned.1.call-done) | copy-start | bytes 3538948
  742.4 308.6 %reduce-scatter.17.cloned.1.call-start = ((), (), s32[]{:S(2)}) async-start(), calls=%async_computation.15 | async-start | bytes 7864320 | tf_op jit(solution)/shard_map/reduce_scatter | solution.py:67
  864.8 233.5 %reduce-scatter.23.cloned.1.call-start = ((), (), s32[]{:S(2)}) async-start(), calls=%async_computation.18 | async-start | bytes 2654208 | tf_op jit(solution)/shard_map/reduce_scatter | solution.py:325
  871.2 284.9 %reduce-scatter.19.cloned.1.call-start = ((), (), s32[]{:S(2)}) async-start(), calls=%async_computation.16 | async-start | bytes 5308416 | tf_op jit(solution)/shard_map/reduce_scatter | solution.py:323
  878.1 172.9 %copy-start.1 = (f32[256,1536]{1,0:T(8,128)S(1)}, f32[256,1536]{1,0:T(8,128)}, u32[]{:S(2)}) copy-start(f32[256,1536]{1,0:T(8,128)} %param.13) | copy-start | bytes 4718596
  878.1 172.9 %copy-start.15 = (f32[1536]{0:T(1024)S(1)}, f32[1536]{0:T(1024)}, u32[]{:S(2)}) copy-start(f32[1536]{0:T(1024)} %copy-done.14) | copy-start | bytes 18436
  878.1 172.9 %copy-start.19 = (f32[256]{0:T(256)S(1)}, f32[256]{0:T(256)}, u32[]{:S(2)}) copy-start(f32[256]{0:T(256)} %copy-done.18) | copy-start | bytes 3076
  938.0 156.4 %copy-start.21 = (f32[256]{0:T(256)S(1)}, f32[256]{0:T(256)}, u32[]{:S(2)}) copy-start(f32[256]{0:T(256)} %get-tuple-element.346) | copy-start | bytes 3076
  (11 other events, 25.7 us)
Sparse Core Ops, SparseCore 0:
  9.9 31.7 all-gather.20
  43.8 63.4 all-gather.12
  109.2 22.7 all-gather.22
  141.6 109.3 reduce-scatter.10
  252.8 46.0 all-gather.24
  300.9 63.4 all-gather.14
  366.0 62.1 all-gather.16
  430.0 30.9 all-gather.26
  484.2 110.7 reduce-scatter.14
  597.1 111.2 reduce-scatter.12
  713.9 64.0 all-gather.18
  781.2 60.3 reduce-scatter.24
  845.6 92.3 reduce-scatter.20
  940.2 110.7 reduce-scatter.16
  1055.2 43.1 reduce-scatter.22
  1102.2 53.8 reduce-scatter.18
where the time goes:
time: 1170 us; the launch traced here: 1160 us
  waiting for transfers between devices  846 us (72%)
  matrix products  126 us (11%)
  local copies, waits for them, and re-layouts  84.5 us (7%)
  other arithmetic  49.1 us (4%)
  blocking collectives  41 us (4%)
  between operations  14.6 us (1%)
    reduce_scatter x2, waiting for transfers between devices, collect_rows(): return lax.psum_scatter(values, 'tensor', scatter_dimension=0, tiled=True)  219 us
    reduce_scatter x2, waiting for transfers between devices, collect_grads(): return lax.psum_scatter(values, 'tensor', scatter_dimension=0, tiled=True)  208 us
    all_gather x2, waiting for transfers between devices, spread_rows(): return lax.all_gather(values, 'tensor', axis=0, tiled=True)  115 us
    all_gather x2, waiting for transfers between devices, spread_grads(): return lax.all_gather(values, 'tensor', axis=0, tiled=True)  87.5 us
    reduce_scatter x1, waiting for transfers between devices, per_device(): lax.psum_scatter(grad_qkv_w, 'dp', scatter_dimension=0, tiled=True)  57.8 us
    reduce_scatter x1, waiting for transfers between devices, per_device(): lax.psum_scatter(grad_gu_w, 'dp', scatter_dimension=0, tiled=True)  54.5 us
    all_gather x1, waiting for transfers between devices, per_device(): lax.all_gather(w_gate_up[layer_index], 'dp', axis=0, tiled=True)  41.5 us
    psum x1, blocking collectives, per_device(): lax.psum((jnp.stack(gain_list), jnp.stack(stat_rows)), ('dp', 'tensor'))  41 us
  transfers between devices with their start and end apart: 16, of which 14 were waited for; matrix products, arithmetic and copies ran while one was open for 19% of the time, Pallas kernels for 0%

commit v1 on v0

v1 whole, which is shorter than its diff:
```python
import functools

import jax
import jax.numpy as jnp
from jax import lax
from jax.experimental import pallas as pl
from jax.experimental.pallas import tpu as pltpu
from jax.sharding import PartitionSpec as P

HEADS = 16
KV_HEADS = 8
HEAD_WIDTH = 96
REPEAT = HEADS // KV_HEADS
LANES = 128

norm_eps = 1e-05
rope_base = 100000.0
MESH = pl.DeviceIdType.MESH
BF = jnp.bfloat16
F32 = jnp.float32
VMEM_LIMIT = 60 * 2**20


def nn(a, b):
    return lax.dot_general(a, b, (((1,), (0,)), ((), ())), preferred_element_type=F32)


def nt(a, b):
    return lax.dot_general(a, b, (((1,), (1,)), ((), ())), preferred_element_type=F32)


def tn(a, b):
    return lax.dot_general(a, b, (((0,), (0,)), ((), ())), preferred_element_type=F32)


def rows_at(index, size):
    return pl.ds(pl.multiple_of(index * size, size), size)


def entry_barrier(n, others=()):
    z = lax.axis_index("tensor")
    barrier = pltpu.get_barrier_semaphore()

    @pl.when(z > 0)
    def _():
        pl.semaphore_signal(barrier, inc=1, device_id={"tensor": z - 1}, device_id_type=MESH)

    @pl.when(z < n - 1)
    def _():
        pl.semaphore_signal(barrier, inc=1, device_id={"tensor": z + 1}, device_id_type=MESH)

    for other in others:
        pl.semaphore_signal(barrier, inc=1, device_id=other, device_id_type=MESH)

    @pl.when((z > 0) & (z < n - 1))
    def _():
        pl.semaphore_wait(barrier, 2 + len(others))

    @pl.when((z == 0) | (z == n - 1))
    def _():
        pl.semaphore_wait(barrier, 1 + len(others))


def bit_of(index, bit):
    return (index // (1 << bit)) % 2


def across(index, bit):
    return index + (1 << bit) * (1 - 2 * bit_of(index, bit))


class Gather:
    def __init__(self, n, at, send_sem, recv_sem):
        self.n, self.at, self.send_sem, self.recv_sem = n, at, send_sem, recv_sem
        self.z = lax.axis_index("tensor")

    def copy(self, slot, step, side, source=None):
        block = self.at(slot)
        return pltpu.make_async_remote_copy(
            src_ref=block if source is None else source,
            dst_ref=block,
            send_sem=self.send_sem.at[side, step],
            recv_sem=self.recv_sem.at[side, step],
            device_id={"tensor": self.z + 1 - 2 * side},
            device_id_type=MESH,
        )

    def sends(self, step, side):
        z, n = self.z, self.n
        slot = z - (1 - 2 * side) * (step - 1)
        target = z + 1 - 2 * side
        return slot, (slot >= 0) & (slot < n) & (target >= 0) & (target < n)

    def send(self, step, side, source=None):
        slot, valid = self.sends(step, side)

        @pl.when(valid)
        def _():
            self.copy(slot, step, side, source).start()

    def begin(self, source=None):
        self.send(1, 0, source)
        self.send(1, 1, source)

    def arrive(self, step, side, forward=True):
        z, n = self.z, self.n
        slot = z - (1 - 2 * side) * step

        @pl.when((slot >= 0) & (slot < n))
        def _():
            self.copy(slot, step, side).wait_recv()

        if forward is True:
            self.send(step + 1, side)
        return slot, (slot >= 0) & (slot < n)

    def drain(self, source=None):
        for step in range(1, self.n):
            for side in range(2):
                slot, valid = self.sends(step, side)

                @pl.when(valid)
                def _(slot=slot, step=step, side=side):
                    self.copy(slot, step, side, source if step == 1 else None).wait_send()


class Scatter:
    def __init__(self, n, buffer, send_sem, recv_sem):
        self.n, self.buffer, self.send_sem, self.recv_sem = n, buffer, send_sem, recv_sem
        self.z = lax.axis_index("tensor")

    def copy(self, step, side):
        return pltpu.make_async_remote_copy(
            src_ref=self.buffer.at[side, step - 1],
            dst_ref=self.buffer.at[side, step],
            send_sem=self.send_sem.at[side, step],
            recv_sem=self.recv_sem.at[side, step],
            device_id={"tensor": self.z + 1 - 2 * side},
            device_id_type=MESH,
        )

    def turn(self, step, side):
        z, n = self.z, self.n
        return z + (1 - 2 * side) * (n - step), step >= 1 + z + side * (n - 1 - 2 * z)

    def has_source(self, side):
        source = self.z - (1 - 2 * side)
        return (source >= 0) & (source < self.n)

    def push(self, step, side, part):
        slot = self.buffer.at[side, step - 1]
        has_source = self.has_source(side)

        @pl.when(has_source)
        def _():
            self.copy(step - 1, side).wait_recv()
            slot[...] = (part() + slot[...].astype(F32)).astype(BF)

        @pl.when(jnp.logical_not(has_source))
        def _():
            slot[...] = part().astype(BF)

        self.copy(step, side).start()

    def settle(self, total_ref):
        for side in range(2):

            @pl.when(self.has_source(side))
            def _(side=side):
                self.copy(self.n - 1, side).wait_recv()
                total_ref[...] += self.buffer[side, self.n - 1].astype(F32)

    def drain(self):
        for step in range(1, self.n):
            for side in range(2):

                @pl.when(self.turn(step, side)[1])
                def _(step=step, side=side):
                    self.copy(step, side).wait_send()


def by_rows(rows, body, block=32):
    def step(index, carry):
        body(rows_at(index, block))
        return carry

    lax.fori_loop(0, rows // block, step, 0)


def norm_rows(values, gain):
    inverse = lax.rsqrt(jnp.mean(values * values, axis=-1, keepdims=True) + norm_eps)
    return values * inverse * gain, inverse


def spread_kernel(n, x_ref, gain_ref, all_ref, own, send_sem, recv_sem, own_sem):
    z = lax.axis_index("tensor")
    tokens = x_ref.shape[0]
    gain = gain_ref[...]

    def normalize(rows):
        own[rows, :] = norm_rows(x_ref[rows, :], gain)[0].astype(BF)

    by_rows(tokens, normalize)
    entry_barrier(n)
    gather = Gather(n, lambda slot: all_ref.at[rows_at(slot, tokens)], send_sem, recv_sem)
    gather.begin(own)
    keep = pltpu.make_async_copy(own, all_ref.at[rows_at(z, tokens)], own_sem)
    keep.start()
    for step in range(1, n):
        for side in range(2):
            gather.arrive(step, side, forward=step < n - 1)
    keep.wait()
    gather.drain(own)


def spread(n, x, gain):
    tokens, width = x.shape
    return pl.pallas_call(
        functools.partial(spread_kernel, n),
        out_shape=jax.ShapeDtypeStruct((n * tokens, width), BF),
        in_specs=[pl.BlockSpec(memory_space=pltpu.VMEM)] * 2,
        out_specs=pl.BlockSpec(memory_space=pl.ANY),
        scratch_shapes=[
            pltpu.VMEM((tokens, width), BF),
            pltpu.SemaphoreType.DMA((2, n)),
            pltpu.SemaphoreType.DMA((2, n)),
            pltpu.SemaphoreType.DMA,
        ],
        compiler_params=pltpu.CompilerParams(
            collective_id=1, has_side_effects=True, vmem_limit_bytes=VMEM_LIMIT
        ),
        cost_estimate=pl.CostEstimate(
            flops=10 * tokens * width, bytes_accessed=100 * tokens * width * 2, transcendentals=0
        ),
        name="spread_normed",
    )(x, gain)


def attend_kernel(
    n,
    kv_local,
    g1_ref,
    wqkv_hbm,
    wout_hbm,
    gf_ref,
    x_ref,
    gain_ref,
    cos_ref,
    sin_low_ref,
    sin_high_ref,
    key_seg_ref,
    key_pos_ref,
    query_seg_ref,
    query_pos_ref,
    q_ref,
    k_ref,
    v_ref,
    o_ref,
    prob_hbm,
    gf_all,
    m_ref,
    n2_ref,
    stat_ref,
    g1,
    wqkv,
    wout,
    v_t,
    bias,
    prob,
    part,
    sums,
    load_sem,
    chunk_sem,
    prob_sem,
    own_sem,
    ag_send,
    ag_recv,
    rs_send,
    rs_recv,
):
    z = lax.axis_index("tensor")
    tokens, width = x_ref.shape
    heads = REPEAT * kv_local
    load_w = pltpu.make_async_copy(wqkv_hbm, wqkv, load_sem.at[0])
    load_w.start()
    load_o = pltpu.make_async_copy(wout_hbm, wout, load_sem.at[1])

    def load_chunk(slot):
        rows = rows_at(slot, tokens)
        return pltpu.make_async_copy(g1_ref.at[rows], g1.at[rows], chunk_sem.at[slot])

    for slot in range(n):
        load_chunk(slot).start()
    load_o.start()
    entry_barrier(n)
    gather = Gather(n, lambda slot: gf_all.at[rows_at(slot, tokens)], ag_send, ag_recv)
    gather.begin(gf_ref)
    keep = pltpu.make_async_copy(gf_ref, gf_all.at[rows_at(z, tokens)], own_sem)
    keep.start()
    load_w.wait()

    group_width = (REPEAT + 2) * LANES

    def project(slot, carry):
        load_chunk(slot).wait()
        rows = rows_at(slot, tokens)
        cosine, low, high = cos_ref[rows, :], sin_low_ref[rows, :], sin_high_ref[rows, :]

        def turn(values):
            return (
                values * cosine
                + pltpu.roll(values, LANES - HEAD_WIDTH // 2, 1) * low
                + pltpu.roll(values, HEAD_WIDTH // 2, 1) * high
            ).astype(BF)

        for group in range(kv_local):
            joined = nn(g1[rows, :], wqkv[:, group * group_width : (group + 1) * group_width])
            for member in range(REPEAT):
                q_ref[group * REPEAT + member, rows, :] = turn(
                    joined[:, member * LANES : (member + 1) * LANES]
                )
            k_ref[group, rows, :] = turn(joined[:, REPEAT * LANES : (REPEAT + 1) * LANES])
            values = joined[:, (REPEAT + 1) * LANES :]
            v_ref[group, rows, :] = values.astype(BF)
        return carry

    lax.fori_loop(0, n, project, 0)
    for group in range(kv_local):
        v_t[group] = v_ref[group].astype(F32).T.astype(BF)
    load_o.wait()
    scatter = Scatter(n, sums, rs_send, rs_recv)
    log2_scale = HEAD_WIDTH ** (-0.5) * 1.4426950408889634

    def attend(target):
        rows = rows_at(target, tokens)
        key_seg, key_pos = key_seg_ref[...], key_pos_ref[...]
        seen = (key_seg == 0) | (key_seg == query_seg_ref[target])
        seen = seen & (key_pos <= query_pos_ref[target])
        bias[...] = jnp.where(seen, 0.0, -1e30)
        for head in range(heads):
            group = head // REPEAT
            scores = nt(k_ref[group], q_ref[head, rows, :]) * log2_scale + bias[...]
            top = jnp.max(scores, axis=0, keepdims=True)
            weights = jnp.exp2(scores - top)
            total = jnp.sum(weights, axis=0, keepdims=True)
            prob[head] = (weights * (1.0 / total)).astype(BF)
            mixed = nn(v_t[group], prob[head])
            o_ref[rows, head * LANES : (head + 1) * LANES] = mixed.T.astype(BF)
        out = pltpu.make_async_copy(prob, prob_hbm.at[target], prob_sem)
        out.start()
        for first in range(0, width, 512):
            part[:, first : first + 512] = nt(o_ref[rows, :], wout[first : first + 512, :])
        out.wait()

    def turn_of(index, carry):
        step, side = index // 2 + 1, index % 2
        target, valid = scatter.turn(step, side)

        @pl.when(valid)
        def _():
            attend(target)
            scatter.push(step, side, lambda: part[...])

        gather.arrive(step, side, forward=None)

        @pl.when(step < n - 1)
        def _():
            gather.send(step + 1, side)

        return carry

    lax.fori_loop(0, 2 * (n - 1), turn_of, 0)
    attend(z)
    scatter.settle(part)
    gain = gain_ref[...]
    stat_ref[...] = jnp.zeros_like(stat_ref)

    def finish(rows):
        branch = part[rows, :]
        middle = x_ref[rows, :] + branch
        m_ref[rows, :] = middle
        n2_ref[rows, :] = norm_rows(middle, gain)[0].astype(BF)
        stat_ref[0:1, :] += jnp.sum(middle * middle, axis=0, keepdims=True)
        stat_ref[1:2, :] += jnp.sum(branch * branch, axis=0, keepdims=True)

    by_rows(tokens, finish)
    keep.wait()
    gather.drain(gf_ref)
    scatter.drain()


def attend(n, kv_local, g1, wqkv, wout, gf, x, gain, tables, keys, queries):
    tokens, width = x.shape
    group_len = n * tokens
    heads = REPEAT * kv_local
    vmem = pl.BlockSpec(memory_space=pltpu.VMEM)
    hbm = pl.BlockSpec(memory_space=pl.ANY)
    flops = 2 * group_len * (
        width * wqkv.shape[1] + width * wout.shape[1] + 2 * heads * group_len * LANES
    )
    return pl.pallas_call(
        functools.partial(attend_kernel, n, kv_local),
        out_shape=(
            jax.ShapeDtypeStruct((heads, group_len, LANES), BF),
            jax.ShapeDtypeStruct((kv_local, group_len, LANES), BF),
            jax.ShapeDtypeStruct((kv_local, group_len, LANES), BF),
            jax.ShapeDtypeStruct((group_len, heads * LANES), BF),
            jax.ShapeDtypeStruct((n, heads, group_len, tokens), BF),
            jax.ShapeDtypeStruct((group_len, width), BF),
            jax.ShapeDtypeStruct((tokens, width), F32),
            jax.ShapeDtypeStruct((tokens, width), BF),
            jax.ShapeDtypeStruct((8, width), F32),
        ),
        in_specs=[hbm, hbm, hbm] + [vmem] * 10,
        out_specs=(vmem, vmem, vmem, vmem, hbm, hbm, vmem, vmem, vmem),
        scratch_shapes=[
            pltpu.VMEM((group_len, width), BF),
            pltpu.VMEM(wqkv.shape, BF),
            pltpu.VMEM(wout.shape, BF),
            pltpu.VMEM((kv_local, LANES, group_len), BF),
            pltpu.VMEM((group_len, tokens), F32),
            pltpu.VMEM((heads, group_len, tokens), BF),
            pltpu.VMEM((tokens, width), F32),
            pltpu.VMEM((2, n, tokens, width), BF),
            pltpu.SemaphoreType.DMA((2,)),
            pltpu.SemaphoreType.DMA((n,)),
            pltpu.SemaphoreType.DMA,
            pltpu.SemaphoreType.DMA,
            pltpu.SemaphoreType.DMA((2, n)),
            pltpu.SemaphoreType.DMA((2, n)),
            pltpu.SemaphoreType.DMA((2, n)),
            pltpu.SemaphoreType.DMA((2, n)),
        ],
        compiler_params=pltpu.CompilerParams(
            collective_id=2, has_side_effects=True, vmem_limit_bytes=VMEM_LIMIT
        ),
        cost_estimate=pl.CostEstimate(
            flops=flops, bytes_accessed=200 * tokens * width * 2, transcendentals=0
        ),
        name="attend_forward",
    )(g1, wqkv, wout, gf, x, gain, *tables, *keys, *queries)


def feed_kernel(
    n,
    chunks,
    n2_ref,
    gf_hbm,
    wgu_hbm,
    wd_hbm,
    m_ref,
    gain_ref,
    cot_ref,
    z_hbm,
    dm_ref,
    ga_ref,
    dgain_ref,
    dwgu_ref,
    n2_all,
    gf_all,
    z_all,
    dgu,
    wgu,
    wd,
    part,
    dn2,
    sums,
    load_sem,
    gf_sem,
    z_sem,
    ag_send,
    ag_recv,
    rs_send,
    rs_recv,
):
    z = lax.axis_index("tensor")
    tokens, width = n2_ref.shape
    ff = wd_hbm.shape[1]
    piece = tokens // chunks
    rows_chunk = n * piece
    load_gu = pltpu.make_async_copy(wgu_hbm, wgu, load_sem.at[0])
    load_d = pltpu.make_async_copy(wd_hbm, wd, load_sem.at[1])

    def load_gf(chunk, slot):
        return pltpu.make_async_copy(
            gf_hbm.at[pl.ds(pl.multiple_of(slot * tokens + chunk * piece, piece), piece)],
            gf_all.at[pl.ds(pl.multiple_of(chunk * rows_chunk + slot * piece, piece), piece)],
            gf_sem.at[chunk, slot],
        )

    load_gu.start()
    load_d.start()
    for chunk in range(chunks):
        for slot in range(n):
            load_gf(chunk, slot).start()
        n2_all[pl.ds(pl.multiple_of(chunk * rows_chunk + z * piece, piece), piece), :] = n2_ref[
            chunk * piece : (chunk + 1) * piece, :
        ]
    entry_barrier(n)

    def gather_of(chunk):
        return Gather(
            n,
            lambda slot: n2_all.at[
                pl.ds(pl.multiple_of(chunk * rows_chunk + slot * piece, piece), piece)
            ],
            ag_send.at[chunk],
            ag_recv.at[chunk],
        )

    def scatter_of(chunk):
        return Scatter(n, sums.at[chunk], rs_send.at[chunk], rs_recv.at[chunk])

    for chunk in range(chunks):
        gather_of(chunk).begin()

    def gather_step(chunk, step):
        gather = gather_of(chunk)
        for side in range(2):
            gather.arrive(step, side, forward=step < n - 1)

    def scatter_step(chunk, step):
        scatter = scatter_of(chunk)
        for side in range(2):
            target, valid = scatter.turn(step, side)

            @pl.when(valid)
            def _():
                scatter.push(
                    step, side, lambda: part[chunk % 2, rows_at(target, piece), :]
                )

    def scatter_end(chunk):
        own = dn2.at[rows_at(chunk, piece)]
        own[...] = part[chunk % 2, rows_at(z, piece), :]
        scatter_of(chunk).settle(own)

    for step in range(1, n):
        gather_step(0, step)
    load_gu.wait()
    load_d.wait()
    block = 256
    hidden_blocks = ff // block
    out_blocks = width // 512

    def hidden_block(chunk, index):
        rows = rows_at(chunk, rows_chunk)
        cols = rows_at(index, block)
        up_cols = pl.ds(pl.multiple_of(ff + index * block, block), block)
        gate = nn(n2_all[rows, :], wgu[:, cols])
        up = nn(n2_all[rows, :], wgu[:, up_cols])
        dz = nn(gf_all[rows, :], wd[:, cols])
        s = 1.0 / (1.0 + jnp.exp(-gate))
        act = gate * s
        z_all[rows, cols] = (act * up).astype(BF)
        dgu[rows, cols] = (dz * up * (s * (1.0 + gate * (1.0 - s)))).astype(BF)
        dgu[rows, up_cols] = (dz * act).astype(BF)

    def out_block(chunk, index):
        rows = rows_at(chunk, rows_chunk)
        cols = rows_at(index, 512)
        part[chunk % 2, :, cols] = nt(dgu[rows, :], wgu[cols, :])

    def z_out(chunk):
        rows = rows_at(chunk, rows_chunk)
        return pltpu.make_async_copy(z_all.at[rows], z_hbm.at[rows], z_sem.at[chunk])

    def stage(chunk, carry):
        for slot in range(n):
            load_gf(chunk, slot).wait()
        pieces = [functools.partial(hidden_block, chunk, i) for i in range(hidden_blocks)]
        pieces += [functools.partial(out_block, chunk, i) for i in range(out_blocks)]
        done = 0
        for step in range(1, n):
            until = len(pieces) * step // n
            for run in pieces[done:until]:
                run()
            done = until

            @pl.when(chunk + 1 < chunks)
            def _(step=step):
                gather_step(chunk + 1, step)

            @pl.when(chunk >= 1)
            def _(step=step):
                scatter_step(chunk - 1, step)

        for run in pieces[done:]:
            run()
        z_out(chunk).start()

        @pl.when(chunk >= 1)
        def _():
            scatter_end(chunk - 1)

        return carry

    lax.fori_loop(0, chunks, stage, 0)

    def grad_gu(first, last):
        def body(index, carry):
            cols = rows_at(index, 256)
            dwgu_ref[:, cols] = tn(n2_all[...], dgu[:, cols]).astype(BF)
            return carry

        lax.fori_loop(first, last, body, 0)

    blocks = 2 * ff // 256
    for step in range(1, n):
        scatter_step(chunks - 1, step)
        grad_gu(blocks * (step - 1) // (n - 1), blocks * step // (n - 1))
    scatter_end(chunks - 1)
    gain = gain_ref[...]
    dgain_ref[...] = jnp.zeros_like(dgain_ref)

    def finish(rows):
        middle = m_ref[rows, :]
        dn = dn2[rows, :]
        inverse = lax.rsqrt(jnp.mean(middle * middle, axis=-1, keepdims=True) + norm_eps)
        scaled = dn * gain
        dgain_ref[0:1, :] += jnp.sum(dn * middle * inverse, axis=0, keepdims=True)
        dm = (
            inverse * scaled
            - middle * inverse**3 * jnp.mean(scaled * middle, axis=-1, keepdims=True)
            + cot_ref[rows, :].astype(F32)
        )
        dm_ref[rows, :] = dm
        ga_ref[rows, :] = dm.astype(BF)

    by_rows(tokens, finish)
    for chunk in range(chunks):
        z_out(chunk).wait()
        gather_of(chunk).drain()
        scatter_of(chunk).drain()


def feed(n, chunks, n2, gf_all, wgu, wd, m, gain, cot):
    tokens, width = n2.shape
    group_len = n * tokens
    ff = wd.shape[1]
    vmem = pl.BlockSpec(memory_space=pltpu.VMEM)
    hbm = pl.BlockSpec(memory_space=pl.ANY)
    return pl.pallas_call(
        functools.partial(feed_kernel, n, chunks),
        out_shape=(
            jax.ShapeDtypeStruct((group_len, ff), BF),
            jax.ShapeDtypeStruct((tokens, width), F32),
            jax.ShapeDtypeStruct((tokens, width), BF),
            jax.ShapeDtypeStruct((8, width), F32),
            jax.ShapeDtypeStruct((width, 2 * ff), BF),
        ),
        in_specs=[vmem, hbm, hbm, hbm, vmem, vmem, vmem],
        out_specs=(hbm, vmem, vmem, vmem, vmem),
        scratch_shapes=[
            pltpu.VMEM((group_len, width), BF),
            pltpu.VMEM((group_len, width), BF),
            pltpu.VMEM((group_len, ff), BF),
            pltpu.VMEM((group_len, 2 * ff), BF),
            pltpu.VMEM((width, 2 * ff), BF),
            pltpu.VMEM((width, ff), BF),
            pltpu.VMEM((2, group_len // chunks, width), F32),
            pltpu.VMEM((tokens, width), F32),
            pltpu.VMEM((chunks, 2, n, tokens // chunks, width), BF),
            pltpu.SemaphoreType.DMA((2,)),
            pltpu.SemaphoreType.DMA((chunks, n)),
            pltpu.SemaphoreType.DMA((chunks,)),
            pltpu.SemaphoreType.DMA((chunks, 2, n)),
            pltpu.SemaphoreType.DMA((chunks, 2, n)),
            pltpu.SemaphoreType.DMA((chunks, 2, n)),
            pltpu.SemaphoreType.DMA((chunks, 2, n)),
        ],
        compiler_params=pltpu.CompilerParams(
            collective_id=3, has_side_effects=True, vmem_limit_bytes=VMEM_LIMIT
        ),
        cost_estimate=pl.CostEstimate(
            flops=18 * group_len * width * ff, bytes_accessed=250 * tokens * width * 2, transcendentals=0
        ),
        name="feed_both",
    )(n2, gf_all, wgu, wd, m, gain, cot)


def attend_back_kernel(
    n,
    kv_local,
    chunks,
    ga_ref,
    wout_hbm,
    wd_hbm,
    z_hbm,
    prob_hbm,
    g1_hbm,
    gf_hbm,
    m_ref,
    q_ref,
    k_ref,
    v_ref,
    o_ref,
    cos_ref,
    sin_low_ref,
    sin_high_ref,
    out_ref,
    stat_ref,
    dqkv_ref,
    dwd_ref,
    dw_ref,
    ga_all,
    g1,
    gf,
    wout,
    wd,
    z_all,
    k_t,
    prob,
    dk,
    dv,
    part,
    sums,
    load_sem,
    gf_sem,
    prob_sem,
    ag_send,
    ag_recv,
    rs_send,
    rs_recv,
):
    z = lax.axis_index("tensor")
    tokens, width = ga_ref.shape
    heads = REPEAT * kv_local
    group_len = n * tokens
    piece = tokens // chunks
    scale = HEAD_WIDTH ** (-0.5)
    loads = [
        pltpu.make_async_copy(source, target, load_sem.at[index])
        for index, (source, target) in enumerate(
            [(wout_hbm, wout), (z_hbm, z_all), (wd_hbm, wd), (g1_hbm, g1)]
        )
    ]
    for load in loads:
        load.start()
    load_out, load_z, load_d, load_g1 = loads

    def load_gf(chunk, slot):
        return pltpu.make_async_copy(
            gf_hbm.at[pl.ds(pl.multiple_of(slot * tokens + chunk * piece, piece), piece)],
            gf.at[pl.ds(pl.multiple_of((chunk * n + slot) * piece, piece), piece)],
            gf_sem.at[chunk, slot],
        )

    for chunk in range(chunks):
        for slot in range(n):
            load_gf(chunk, slot).start()

    def load_prob(slot, place):
        return pltpu.make_async_copy(prob_hbm.at[slot], prob.at[place], prob_sem.at[place])

    ga_all[rows_at(z, tokens), :] = ga_ref[...]
    entry_barrier(n)
    gather = Gather(n, lambda slot: ga_all.at[rows_at(slot, tokens)], ag_send, ag_recv)
    gather.begin()
    load_prob(z, 0).start()
    scatter = Scatter(n, sums, rs_send, rs_recv)
    for group in range(kv_local):
        k_t[group] = k_ref[group].astype(F32).T.astype(BF)
    dk[...] = jnp.zeros_like(dk)
    dv[...] = jnp.zeros_like(dv)
    load_out.wait()
    load_z.wait()
    load_d.wait()
    group_lanes = (REPEAT + 2) * LANES

    def turn_back(values, rows):
        return (
            values * cos_ref[rows, :]
            - pltpu.roll(values, LANES - HEAD_WIDTH // 2, 1) * sin_low_ref[rows, :]
            - pltpu.roll(values, HEAD_WIDTH // 2, 1) * sin_high_ref[rows, :]
        )

    def back(slot, place):
        rows = rows_at(slot, tokens)
        d_o = nn(ga_all[rows, :], wout[...])
        for head in range(heads):
            group = head // REPEAT
            lanes = slice(head * LANES, (head + 1) * LANES)
            do_h = d_o[:, lanes].astype(BF)
            both = do_h.astype(F32) * o_ref[rows, lanes].astype(F32)
            delta = jnp.sum(both.T, axis=0, keepdims=True)
            dprob = nt(v_ref[group], do_h)
            weights = prob[place, head]
            ds = (weights.astype(F32) * (dprob - delta)).astype(BF)
            dv[group] += nn(weights, do_h)
            dk[group] += nn(ds, q_ref[head, rows, :])
            dq = nn(k_t[group], ds).T * scale
            first = group * group_lanes + (head % REPEAT) * LANES
            dqkv_ref[rows, first : first + LANES] = turn_back(dq, rows).astype(BF)

    def feed_rows(target):
        pieces = [
            z_all[
                pl.ds(
                    pl.multiple_of(chunk * n * piece + target * piece, piece), piece
                ),
                :,
            ]
            for chunk in range(chunks)
        ]
        rows = jnp.concatenate(pieces, axis=0) if chunks > 1 else pieces[0]
        for first in range(0, width, 512):
            part[:, first : first + 512] = nt(rows, wd[first : first + 512, :])

    def turn_of(index, carry):
        step, side = index // 2 + 1, index % 2
        target, sends = scatter.turn(step, side)

        @pl.when(sends)
        def _():
            feed_rows(target)
            scatter.push(step, side, lambda: part[...])

        slot, valid = gather.arrive(step, side, forward=None)

        @pl.when(step < n - 1)
        def _():
            gather.send(step + 1, side)

        @pl.when(valid)
        def _():
            load_prob(slot, 1).start()
            load_prob(slot, 1).wait()
            back(slot, 1)

        return carry

    load_prob(z, 0).wait()
    back(z, 0)
    for chunk in range(chunks):
        for slot in range(n):
            load_gf(chunk, slot).wait()
    down_blocks = dwd_ref.shape[1] // 256

    def grad_down(first, last):
        def body(index, carry):
            cols = rows_at(index, 256)
            dwd_ref[:, cols] = tn(gf[...], z_all[:, cols]).astype(BF)
            return carry

        lax.fori_loop(first, last, body, 0)

    for step in range(1, n):
        lax.fori_loop(2 * (step - 1), 2 * step, turn_of, 0)
        grad_down(down_blocks * (step - 1) // (n - 1), down_blocks * step // (n - 1))

    def finish_keys(slot, carry):
        rows = rows_at(slot, tokens)
        for group in range(kv_local):
            first = group * group_lanes + REPEAT * LANES
            dqkv_ref[rows, first : first + LANES] = turn_back(
                dk[group, rows, :] * scale, rows
            ).astype(BF)
            dqkv_ref[rows, first + LANES : first + 2 * LANES] = dv[group, rows, :].astype(BF)
        return carry

    lax.fori_loop(0, n, finish_keys, 0)
    load_g1.wait()
    feed_rows(z)
    out_lanes = heads * LANES

    def grad_qkv(index, carry):
        cols = rows_at(index, 256)
        place = pl.ds(pl.multiple_of(out_lanes + index * 256, 256), 256)
        dw_ref[:, place] = tn(g1[...], dqkv_ref[:, cols]).astype(BF)
        return carry

    lax.fori_loop(0, dqkv_ref.shape[1] // 256, grad_qkv, 0)

    def grad_out(index, carry):
        cols = rows_at(index, 256)
        dw_ref[:, cols] = tn(ga_all[...], o_ref[:, cols]).astype(BF)
        return carry

    lax.fori_loop(0, out_lanes // 256, grad_out, 0)
    scatter.settle(part)
    stat_ref[...] = jnp.zeros_like(stat_ref)

    def finish(rows):
        branch = part[rows, :]
        result = m_ref[rows, :] + branch
        out_ref[rows, :] = result
        stat_ref[0:1, :] += jnp.sum(result * result, axis=0, keepdims=True)
        stat_ref[1:2, :] += jnp.sum(branch * branch, axis=0, keepdims=True)

    by_rows(tokens, finish)
    gather.drain()
    scatter.drain()


def attend_back(n, kv_local, chunks, ga, wout, wd, z_all, prob, g1, gf, m, q, k, v, o, tables):
    tokens, width = ga.shape
    group_len = n * tokens
    heads = REPEAT * kv_local
    ff = wd.shape[1]
    lanes = (REPEAT + 2) * kv_local * LANES
    vmem = pl.BlockSpec(memory_space=pltpu.VMEM)
    hbm = pl.BlockSpec(memory_space=pl.ANY)
    return pl.pallas_call(
        functools.partial(attend_back_kernel, n, kv_local, chunks),
        out_shape=(
            jax.ShapeDtypeStruct((tokens, width), F32),
            jax.ShapeDtypeStruct((8, width), F32),
            jax.ShapeDtypeStruct((group_len, lanes), BF),
            jax.ShapeDtypeStruct((width, ff), BF),
            jax.ShapeDtypeStruct((width, heads * LANES + lanes), BF),
        ),
        in_specs=[vmem] + [hbm] * 6 + [vmem] * 8,
        out_specs=(vmem,) * 5,
        scratch_shapes=[
            pltpu.VMEM((group_len, width), BF),
            pltpu.VMEM((group_len, width), BF),
            pltpu.VMEM((group_len, width), BF),
            pltpu.VMEM(wout.shape, BF),
            pltpu.VMEM(wd.shape, BF),
            pltpu.VMEM((group_len, ff), BF),
            pltpu.VMEM((kv_local, LANES, group_len), BF),
            pltpu.VMEM((2, heads, group_len, tokens), BF),
            pltpu.VMEM((kv_local, group_len, LANES), F32),
            pltpu.VMEM((kv_local, group_len, LANES), F32),
            pltpu.VMEM((tokens, width), F32),
            pltpu.VMEM((2, n, tokens, width), BF),
            pltpu.SemaphoreType.DMA((4,)),
            pltpu.SemaphoreType.DMA((chunks, n)),
            pltpu.SemaphoreType.DMA((2,)),
            pltpu.SemaphoreType.DMA((2, n)),
            pltpu.SemaphoreType.DMA((2, n)),
            pltpu.SemaphoreType.DMA((2, n)),
            pltpu.SemaphoreType.DMA((2, n)),
        ],
        compiler_params=pltpu.CompilerParams(
            collective_id=4, has_side_effects=True, vmem_limit_bytes=VMEM_LIMIT
        ),
        cost_estimate=pl.CostEstimate(
            flops=8 * group_len * width * ff, bytes_accessed=200 * tokens * width * 2, transcendentals=0
        ),
        name="attend_backward",
    )(ga, wout, wd, z_all, prob, g1, gf, m, q, k, v, o, *tables)


class Halving:
    def __init__(self, size, rows, grad, keep, buffer, keep_sem, send_sem, recv_sem):
        self.rows, self.grad, self.keep, self.buffer = rows, grad, keep, buffer
        self.keep_sem, self.send_sem, self.recv_sem = keep_sem, send_sem, recv_sem
        self.me = lax.axis_index("dp")
        self.bits = size.bit_length() - 1
        rest = list(range(1, self.bits))
        self.orders = ([0] + rest, [0] + rest[::-1])
        self.half = buffer.shape[-1]
        self.size = size

    def count(self, stage):
        return self.size >> (stage + 1)

    def offset(self, stage):
        return self.size - (self.size >> stage)

    def block_rows(self, half, number, mine):
        order = self.orders[half]
        first = bit_of(self.me, 0)
        index = first if mine else 1 - first
        later = order[1:]
        for place, bit in enumerate(later):
            index = index + ((number >> (len(later) - 1 - place)) & 1) * (1 << bit)
        return rows_at(index, self.rows)

    def columns(self, half):
        return slice(half * self.half, (half + 1) * self.half)

    def load(self, half, number):
        return pltpu.make_async_copy(
            self.grad.at[self.block_rows(half, number, True), self.columns(half)],
            self.keep.at[half, number],
            self.keep_sem.at[half, number],
        )

    def first_copy(self, half, number):
        return pltpu.make_async_remote_copy(
            src_ref=self.grad.at[self.block_rows(half, number, False), self.columns(half)],
            dst_ref=self.buffer.at[half, number],
            send_sem=self.send_sem.at[half, number],
            recv_sem=self.recv_sem.at[half, number],
            device_id={"dp": across(self.me, 0)},
            device_id_type=MESH,
        )

    def copy(self, half, stage):
        bit = self.orders[half][stage]
        count = self.count(stage)
        goes = (1 - bit_of(self.me, bit)) * count + self.offset(stage - 1)
        return pltpu.make_async_remote_copy(
            src_ref=self.buffer.at[half, pl.ds(goes, count)],
            dst_ref=self.buffer.at[half, pl.ds(self.offset(stage), count)],
            send_sem=self.send_sem.at[half, self.offset(stage)],
            recv_sem=self.recv_sem.at[half, self.offset(stage)],
            device_id={"dp": across(self.me, bit)},
            device_id_type=MESH,
        )

    def begin(self):
        for half in range(2):
            for number in range(self.count(0)):
                self.first_copy(half, number).start()
                self.load(half, number).start()

    def advance(self, stage):
        for half in range(2):
            if stage == 0:
                for number in range(self.count(0)):
                    self.first_copy(half, number).wait_recv()
                    self.load(half, number).wait()
            else:
                self.copy(half, stage).wait_recv()
            if stage == self.bits - 1:
                continue
            base = bit_of(self.me, self.orders[half][stage]) * self.count(stage)

            def add(number, carry, half=half, base=base):
                place = self.offset(stage) + number
                if stage == 0:
                    kept = self.keep[half, number]
                else:
                    kept = self.buffer[half, self.offset(stage - 1) + base + number]
                self.buffer[half, place] = (
                    self.buffer[half, place].astype(F32) + kept.astype(F32)
                ).astype(BF)
                return carry

            lax.fori_loop(0, self.count(stage), add, 0)
            self.copy(half, stage + 1).start()

    def result(self, half):
        stage = self.bits - 1
        base = bit_of(self.me, self.orders[half][stage])
        return self.buffer[half, self.offset(stage)].astype(F32) + self.buffer[
            half, self.offset(stage - 1) + base
        ].astype(F32)

    def drain(self):
        for half in range(2):
            for number in range(self.count(0)):
                self.first_copy(half, number).wait_send()
            for stage in range(1, self.bits):
                self.copy(half, stage).wait_send()


def last_kernel(
    n,
    dp,
    cells,
    out_heads,
    dqkv_ref,
    wqkv_ref,
    x_ref,
    dm_ref,
    gain_ref,
    dgain_two_ref,
    stat_one_ref,
    stat_two_ref,
    dw_hbm,
    dx_ref,
    gains_ref,
    rms_ref,
    grad_out_ref,
    grad_qkv_ref,
    part,
    sums,
    keep,
    blocks,
    vector,
    vectors,
    rs_send,
    rs_recv,
    keep_sem,
    dp_send,
    dp_recv,
    all_send,
    all_recv,
):
    z = lax.axis_index("tensor")
    me = lax.axis_index("dp")
    tokens, width = x_ref.shape
    dp_bits, z_bits = dp.bit_length() - 1, n.bit_length() - 1
    partners = [{"dp": across(me, bit)} for bit in range(dp_bits)]
    partners += [{"tensor": across(z, bit)} for bit in range(z_bits)]
    entry_barrier(n, partners[:dp_bits] + partners[dp_bits + 1 :])
    halving = Halving(dp, grad_out_ref.shape[0], dw_hbm, keep, blocks, keep_sem, dp_send, dp_recv)
    halving.begin()
    scatter = Scatter(n, sums, rs_send, rs_recv)

    def rows_of(target):
        rows = rows_at(target, tokens)
        for first in range(0, width, 512):
            part[:, first : first + 512] = nt(dqkv_ref[rows, :], wqkv_ref[first : first + 512, :])

    def turn_of(index, carry):
        step, side = index // 2 + 1, index % 2
        target, sends = scatter.turn(step, side)

        @pl.when(sends)
        def _():
            rows_of(target)
            scatter.push(step, side, lambda: part[...])

        return carry

    for step in range(1, n):
        lax.fori_loop(2 * (step - 1), 2 * step, turn_of, 0)
        if step <= dp_bits:
            halving.advance(step - 1)
    for stage in range(n - 1, dp_bits):
        halving.advance(stage)
    rows_of(z)
    for half in range(2):
        block = halving.result(half)
        first_head = half * (block.shape[1] // LANES)
        for index in range(block.shape[1] // LANES):
            values = block[:, index * LANES : index * LANES + HEAD_WIDTH]
            head = first_head + index
            if head < out_heads:
                grad_out_ref[:, head * HEAD_WIDTH : (head + 1) * HEAD_WIDTH] = values
            else:
                head -= out_heads
                grad_qkv_ref[:, head * HEAD_WIDTH : (head + 1) * HEAD_WIDTH] = values
    scatter.settle(part)
    gain = gain_ref[...]
    vector[...] = jnp.zeros_like(vector)
    vector[1:2, :] = dgain_two_ref[0:1, :]
    vector[2:3, :] = stat_one_ref[0:1, :]
    vector[3:4, :] = stat_two_ref[0:1, :]
    vector[4:5, :] = stat_one_ref[1:2, :]
    vector[5:6, :] = stat_two_ref[1:2, :]

    def finish(rows):
        values = x_ref[rows, :]
        dn = part[rows, :]
        inverse = lax.rsqrt(jnp.mean(values * values, axis=-1, keepdims=True) + norm_eps)
        scaled = dn * gain
        vector[0:1, :] += jnp.sum(dn * values * inverse, axis=0, keepdims=True)
        dx_ref[rows, :] = (
            inverse * scaled
            - values * inverse**3 * jnp.mean(scaled * values, axis=-1, keepdims=True)
            + dm_ref[rows, :]
        )

    by_rows(tokens, finish)

    def exchange(index):
        return pltpu.make_async_remote_copy(
            src_ref=vector if index == 0 else vectors.at[index - 1],
            dst_ref=vectors.at[index],
            send_sem=all_send.at[index],
            recv_sem=all_recv.at[index],
            device_id=partners[index],
            device_id_type=MESH,
        )

    for index in range(len(partners)):
        exchange(index).start()
        exchange(index).wait_recv()
        held = vector[...] if index == 0 else vectors[index - 1]
        vectors[index] += held
    for index in range(len(partners)):
        exchange(index).wait_send()
    total = vectors[len(partners) - 1]
    gains_ref[0] = total[0:2, :]
    squares = jnp.sqrt(jnp.sum(total, axis=1, keepdims=True) * (1.0 / cells))
    row = lax.broadcasted_iota(jnp.int32, (8, 4), 0)
    column = lax.broadcasted_iota(jnp.int32, (8, 4), 1)
    rms_ref[...] = jnp.sum(jnp.where(row == column + 2, squares, 0.0), axis=0, keepdims=True)
    halving.drain()
    scatter.drain()


def last(n, dqkv, wqkv, x, dm, gain, dgain_two, stat_one, stat_two, dw, out_columns, qkv_columns):
    tokens, width = x.shape
    dp = lax.axis_size("dp")
    owned = width // dp
    stages = (dp.bit_length() - 1) + (n.bit_length() - 1)
    half = dw.shape[1] // 2
    vmem = pl.BlockSpec(memory_space=pltpu.VMEM)
    return pl.pallas_call(
        functools.partial(last_kernel, n, dp, tokens * width * dp * n, out_columns // HEAD_WIDTH),
        out_shape=(
            jax.ShapeDtypeStruct((tokens, width), F32),
            jax.ShapeDtypeStruct((1, 2, width), F32),
            jax.ShapeDtypeStruct((1, 4), F32),
            jax.ShapeDtypeStruct((owned, out_columns), F32),
            jax.ShapeDtypeStruct((owned, qkv_columns), F32),
        ),
        in_specs=[vmem] * 8 + [pl.BlockSpec(memory_space=pl.ANY)],
        out_specs=(vmem,) * 5,
        scratch_shapes=[
            pltpu.VMEM((tokens, width), F32),
            pltpu.VMEM((2, n, tokens, width), BF),
            pltpu.VMEM((2, dp // 2, owned, half), BF),
            pltpu.VMEM((2, dp - 1, owned, half), BF),
            pltpu.VMEM((8, width), F32),
            pltpu.VMEM((stages, 8, width), F32),
            pltpu.SemaphoreType.DMA((2, n)),
            pltpu.SemaphoreType.DMA((2, n)),
            pltpu.SemaphoreType.DMA((2, dp // 2)),
            pltpu.SemaphoreType.DMA((2, dp)),
            pltpu.SemaphoreType.DMA((2, dp)),
            pltpu.SemaphoreType.DMA((stages,)),
            pltpu.SemaphoreType.DMA((stages,)),
        ],
        compiler_params=pltpu.CompilerParams(
            collective_id=5, has_side_effects=True, vmem_limit_bytes=VMEM_LIMIT
        ),
        cost_estimate=pl.CostEstimate(
            flops=2 * dqkv.size * width, bytes_accessed=150 * tokens * width * 2, transcendentals=0
        ),
        name="input_gradient",
    )(dqkv, wqkv, x, dm, gain, dgain_two, stat_one, stat_two, dw)


def pad_heads(values):
    rows, columns = values.shape
    heads = columns // HEAD_WIDTH
    padded = jnp.pad(
        values.reshape(rows, heads, HEAD_WIDTH), ((0, 0), (0, 0), (0, LANES - HEAD_WIDTH))
    )
    return padded.reshape(rows, heads * LANES)


def per_device(inputs, norm_gains, w_qkv, w_gate_up, w_out, w_down, segments, positions, cotangent):
    n = lax.axis_size("tensor")
    tokens, width = inputs.shape
    group_len = segments.shape[0]
    kv_local = w_out.shape[2] // (REPEAT * HEAD_WIDTH)
    ff_local = w_down.shape[2]
    chunks = 2
    half = HEAD_WIDTH // 2

    def whole(shard):
        return lax.all_gather(shard, "dp", axis=0, tiled=True)

    def owned(grad):
        return lax.psum_scatter(grad, "dp", scatter_dimension=0, tiled=True)

    wqkv = whole(pad_heads(w_qkv[0]))
    wout = whole(pad_heads(w_out[0]))
    wgu = whole(jnp.concatenate([w_gate_up[0, :, 0], w_gate_up[0, :, 1]], axis=1))
    wd = whole(w_down[0])

    lane = jnp.arange(LANES)
    freq_steps = jnp.arange(half, dtype=F32) * (2.0 / HEAD_WIDTH)
    inverse = jnp.power(rope_base, -freq_steps)
    lane_inverse = jnp.concatenate([inverse, inverse, jnp.zeros((LANES - HEAD_WIDTH,), F32)])
    angles = positions.astype(F32)[:, None] * lane_inverse[None, :]
    cosine, sine = jnp.cos(angles), jnp.sin(angles)
    tables = (
        cosine,
        jnp.where(lane < half, -sine, 0.0),
        jnp.where((lane >= half) & (lane < HEAD_WIDTH), sine, 0.0),
    )
    keys = (segments.reshape(group_len, 1), positions.reshape(group_len, 1))
    queries = (segments.reshape(n, 1, tokens), positions.reshape(n, 1, tokens))
    gain_one, gain_two = norm_gains[0, 0:1], norm_gains[0, 1:2]

    g1 = spread(n, inputs, gain_one)
    q, k, v, o, prob, gf_all, m, n2, stat_one = attend(
        n, kv_local, g1, wqkv, wout, cotangent, inputs, gain_two, tables, keys, queries
    )
    z_all, dm, ga, dgain_two, dwgu = feed(n, chunks, n2, gf_all, wgu, wd, m, gain_two, cotangent)
    grad_gu = owned(dwgu)
    output, stat_two, dqkv, dwd, dw = attend_back(
        n, kv_local, chunks, ga, wout, wd, z_all, prob, g1, gf_all, m, q, k, v, o, tables
    )
    dwd, grad_gu = lax.optimization_barrier((dwd, grad_gu))
    grad_down = owned(dwd)
    input_grad, gain_total, rms, grad_out, grad_qkv = last(
        n,
        dqkv,
        wqkv,
        inputs,
        dm,
        gain_one,
        dgain_two,
        stat_one,
        stat_two,
        dw,
        w_out.shape[2],
        w_qkv.shape[2],
    )
    return (
        output,
        input_grad,
        grad_qkv[None],
        grad_gu.reshape(-1, 2, ff_local)[None].astype(F32),
        grad_out[None],
        grad_down[None].astype(F32),
        gain_total,
        rms,
    )


def solution(mesh):
    rows = P(("dp", "tensor"), None)
    weights = P(None, "dp", "tensor")
    pairs = P(None, "dp", None, "tensor")
    return jax.shard_map(
        per_device,
        mesh=mesh,
        in_specs=(rows, P(), weights, pairs, weights, weights, P("dp"), P("dp"), rows),
        out_specs=(rows, rows, weights, pairs, weights, weights, P(), P()),
        check_vma=False,
    )
```

time: 1170 us -> 460 us (0.39)
  waiting for transfers between devices: 846 us -> 0.83 us
  Pallas kernels: 0 us -> 415 us
  matrix products: 126 us -> 0 us
  local copies, waits for them, and re-layouts: 84.5 us -> 16.9 us
  other arithmetic: 49.1 us -> 6.17 us
  blocking collectives: 41 us -> 0 us
    reduce_scatter x7 -> x2, waiting for transfers between devices: 540 us -> 0.02 us  [owned(): return lax.psum_scatter(grad, 'dp', scatter_dimension=0, tiled=True)]
    pallas_call x0 -> x5, Pallas kernels: none -> 415 us  [the longest x1 118 us: feed(): pl.pallas_call(functools.partial(feed_kernel, n, chunks), out_shape=(jax....]
    all_gather x8 -> x4, waiting for transfers between devices: 302 us -> 0.04 us  [whole(): return lax.all_gather(shard, 'dp', axis=0, tiled=True)]
    dot_general x26 -> x0, matrix products: 126 us -> none  [the longest x2 18.5 us: refold(): jnp.einsum('td,tc->dc', lax.all_gather(normed_local, 'tensor', axis=0, ti...]
    psum x1 -> x0, blocking collectives: 41 us -> none  [per_device(): lax.psum((jnp.stack(gain_list), jnp.stack(stat_rows)), ('dp', 'tensor'))]
    dynamic_update_slice x4 -> x0, local copies, waits for them, and re-layouts: 31.7 us -> none  [per_device(): lax.scan(back_block, (zero_rows, zero_rows), (query_matrix.reshape(blocks...]
    reduce_sum x7 -> x0, other arithmetic: 18.9 us -> none  [the longest x1 5.39 us: per_device(): jnp.sum(output * output)]
    all_gather x1 -> x0, local copies, waits for them, and re-layouts: 16.5 us -> none  [per_device(): lax.all_gather(w_gate_up[layer_index], 'dp', axis=0, tiled=True)]
  transfers between devices with their start and end apart: 16 -> 6, of which waited for: 14 -> 0; matrix products, arithmetic and copies ran while one was open for 19% -> 3% of each run, Pallas kernels for 0% -> 66%
where the time goes in v1:
time: 460 us; the launch traced here: 454 us
  Pallas kernels  415 us (90%)
  local copies, waits for them, and re-layouts  16.9 us (4%)
  between operations  14.5 us (3%)
  other arithmetic  6.17 us (1%)
    pallas_call x1, Pallas kernels, feed(): pl.pallas_call(functools.partial(feed_kernel, n, chunks), out_shape=(jax....  118 us
    pallas_call x1, Pallas kernels, attend_back(): pl.pallas_call(functools.partial(attend_back_kernel, n, kv_local, chunks)...  84 us
    pallas_call x1, Pallas kernels, attend(): pl.pallas_call(functools.partial(attend_kernel, n, kv_local), out_shape=(...  77.8 us
    pallas_call x1, Pallas kernels, last(): pl.pallas_call(functools.partial(last_kernel, n, dp, tokens * width * dp...  75.9 us
    pallas_call x1, Pallas kernels, spread(): pl.pallas_call(functools.partial(spread_kernel, n), out_shape=jax.ShapeDt...  59.9 us
  transfers between devices with their start and end apart: 6, of which 0 were waited for; matrix products, arithmetic and copies ran while one was open for 3% of the time, Pallas kernels for 66%

profile of v1, /device:TPU:0, one launch (start us, length us, event | category | flops | bytes accessed | tf_op | source)
XLA Modules:
  0.0 453.9 jit_solution(12173244925444774515)
XLA Ops:
  7.2 1.1 reshape_squeeze.7
  8.3 0.1 pad.9
  8.4 0.7 copy.32
  9.2 1.5 reshape_squeeze.6
  10.7 0.1 pad.8
  10.7 0.8 copy.31
  11.7 0.7 all-gather.12.cloned.1.call-update
  12.4 1.1 fusion.3
  13.5 0.3 copy_bitcast_fusion.1
  13.8 0.9 pad_maximum_fusion
  14.8 0.0 reduce-scatter.3.cloned.1.call-start
  14.9 1.0 copy.20.key_pos_ref
  15.9 1.0 copy.19.key_seg_ref
  16.9 0.6 slice_bitcast_fusion
  17.5 59.9 %spread_normed.1.g1_ref.g1_hbm = bf16[1024,1536]{1,0:T(8,128)(2,1)} custom-call(f32[256,1536]{1,0:T(8,128)} %x_ref.5, f32[1,1536]{1,0:T(1,128)} %get-tuple-element.63.gain_ref), custom_call_target="tpu_custom_call" | custom-call | flops 3932160 | bytes 78643200 | tf_op jit(solution)/shard_map/spread_normed/pallas_call | solution.py:218
  77.5 0.1 pad_maximum_fusion.1
  77.6 3.2 fusion
  80.8 77.8 %attend_forward.1 = (bf16[4,1024,128]{2,1,0:T(8,128)(2,1)}, bf16[2,1024,128]{2,1,0:T(8,128)(2,1)}, bf16[2,1024,128]{2,1,0:T(8,128)(2,1)}, bf16[1024,512]{1,0:T(8...) custom-call(bf16[1024,1536]{1,0:T(8,128)(2,1)} %spread_normed.1.g1_r, ...), custom_call_target="tpu_custom_call" | custom-call | flops 6979321856 | bytes 157286400 | tf_op jit(solution)/shard_map/attend_forward/pallas_call | solution.py:401
  158.7 117.6 %feed_both.1 = (bf16[1024,1024]{1,0:T(8,128)(2,1)}, f32[256,1536]{1,0:T(8,128)}, bf16[256,1536]{1,0:T(8,128)(2,1)}, f32[8,1536]{1,0:T(8,128)}, bf16[1536,2048]{1,0:T(8,128)(2,1)}) custom-call(bf16[256,1536]{1,0:T(8,128)(2,1)} %get-tuple-element.34.n2_ref, bf16[1024,1536]{1,0:T(8,128)(2,1)} %get-tuple-element.35.gf_hbm, ...), custom_call_target="tpu_custom_call" | custom-call | flops 28991029248 | bytes 196608000 | tf_op jit(solution)/shard_map/feed_both/pallas_call | solution.py:643
  276.4 0.0 reduce-scatter.5.cloned.1.call-start
  276.4 84.0 %attend_backward.1 = (f32[256,1536]{1,0:T(8,128)}, f32[8,1536]{1,0:T(8,128)}, bf16[1024,1024]{1,0:T(8,128)(2,1)}, bf16[1536,1024]{1,0:T(8,128)(2,1)}, bf16[1536,1536]{1,0:T(8,128)(2,1)}) custom-call(bf16[256,1536]{1,0:T(8,128)(2,1)} %get-tuple-element.37.ga_ref, bf16[1536,512]{1,0:T(8,128)(2,1)} %all-gather.8.cloned.1.call-done.wout_hbm, ...), custom_call_target="tpu_custom_call" | custom-call | flops 12884901888 | bytes 157286400 | tf_op jit(solution)/shard_map/attend_backward/pallas_call | solution.py:904
  360.5 75.9 %input_gradient.1 = (f32[256,1536]{1,0:T(8,128)}, f32[1,2,1536]{2,1,0:T(2,128)}, f32[1,4]{1,0:T(1,128)}, f32[192,384]{1,0:T(8,128)}, f32[192,768]{1,0:T(8,128)}) custom-call(bf16[1024,1024]{1,0:T(8,128)(2,1)} %get-tuple-element.45.dqkv_ref, bf16[1536,1024]{1,0:T(8,128)(2,1)} %all-gather.6.cloned.1.call-done.wqkv_hbm.wqkv_ref, f32[256,1536]{1,0:T(8,128)} %x_ref.5, ...), custom_call_target="tpu_custom_call" | custom-call | flops 3221225472 | bytes 117964800 | tf_op jit(solution)/shard_map/input_gradient/pallas_call | solution.py:1187
  436.3 2.5 reshape.58
  438.9 2.0 bitcast_convert_fusion
  440.8 1.1 copy.39
  442.0 0.8 copy-done.2
  442.8 1.1 copy.40
  443.9 0.3 copy-done.4
  444.2 0.8 copy.41
  445.1 0.7 copy.42
  445.8 0.6 copy.43
  446.4 0.5 copy.44
  (39 shorter events, 0.4 us)
Async XLA Ops:
  7.2 73.6 %all-gather.8.cloned.1.call-start = ((), (), s32[]{:S(2)}) async-start(), calls=%async_computation.3 | async-start | bytes 1769472 | tf_op jit(solution)/shard_map/all_gather | solution.py:1242
  9.1 3.3 copy-start
  9.1 71.7 %all-gather.6.cloned.1.call-start = ((), (), s32[]{:S(2)}) async-start(), calls=%async_computation.2 | async-start | bytes 3538944 | tf_op jit(solution)/shard_map/all_gather | solution.py:1242
  11.6 147.1 %all-gather.12.cloned.1.call-start = ((), (), s32[]{:S(2)}) async-start(), calls=%async_computation.7 | async-start | bytes 3538944 | tf_op jit(solution)/shard_map/all_gather | solution.py:1242
  12.3 146.3 %all-gather.10.cloned.1.call-start = ((), (), s32[]{:S(2)}) async-start(), calls=%async_computation.4 | async-start | bytes 7077888 | tf_op jit(solution)/shard_map/all_gather | solution.py:1242
  13.8 1.1 copy-start.6
  13.8 2.1 copy-start.9
  13.8 3.1 copy-start.7
  14.8 345.6 %reduce-scatter.3.cloned.1.call-start = ((), (), s32[]{:S(2)}) async-start(), calls=%async_computation.5 | async-start | bytes 7077888 | tf_op jit(solution)/shard_map/reduce_scatter | solution.py:1245
  276.4 162.5 %reduce-scatter.5.cloned.1.call-start = ((), (), s32[]{:S(2)}) async-start(), calls=%async_computation.6 | async-start | bytes 3538944 | tf_op jit(solution)/shard_map/reduce_scatter | solution.py:1245
  360.4 75.9 %copy-start.3 = (bf16[192,2048]{1,0:T(8,128)(2,1)S(1)}, bf16[192,2048]{1,0:T(8,128)(2,1)}, u32[]{:S(2)}) copy-start(bf16[192,2048]{1,0:T(8,128)(2,1)} %reduce-scatter.3.cloned.1.call-done) | copy-start | bytes 2359300
  436.3 4.5 copy-start.1
  440.8 2.0 copy-start.2
  442.8 1.4 copy-start.4
  442.8 2.3 copy-start.5
  444.2 1.5 copy-start.8
  444.2 2.1 copy-start.10
Sparse Core Ops, SparseCore 0:
  10.5 28.4 all-gather.7
  40.8 32.3 all-gather.5
  75.1 32.3 all-gather.11
  109.7 45.5 all-gather.9
  276.5 60.6 reduce-scatter.2
  360.6 50.1 reduce-scatter.4

commit v2 on v0

v2 whole, which is shorter than its diff:
```python
import functools

import jax
import jax.numpy as jnp
from jax import lax
from jax.experimental import pallas as pl
from jax.experimental.pallas import tpu as pltpu
from jax.sharding import PartitionSpec as P

HEADS = 16
KV_HEADS = 8
HEAD_WIDTH = 96
REPEAT = HEADS // KV_HEADS
LANES = 128

norm_eps = 1e-05
rope_base = 100000.0
MESH = pl.DeviceIdType.MESH
BF = jnp.bfloat16
F32 = jnp.float32
VMEM_LIMIT = 60 * 2**20


def nn(a, b):
    return lax.dot_general(a, b, (((1,), (0,)), ((), ())), preferred_element_type=F32)


def nt(a, b):
    return lax.dot_general(a, b, (((1,), (1,)), ((), ())), preferred_element_type=F32)


def tn(a, b):
    return lax.dot_general(a, b, (((0,), (0,)), ((), ())), preferred_element_type=F32)


def rows_at(index, size):
    return pl.ds(pl.multiple_of(index * size, size), size)


def entry_barrier(n, others=()):
    z = lax.axis_index("tensor")
    barrier = pltpu.get_barrier_semaphore()

    @pl.when(z > 0)
    def _():
        pl.semaphore_signal(barrier, inc=1, device_id={"tensor": z - 1}, device_id_type=MESH)

    @pl.when(z < n - 1)
    def _():
        pl.semaphore_signal(barrier, inc=1, device_id={"tensor": z + 1}, device_id_type=MESH)

    for other in others:
        pl.semaphore_signal(barrier, inc=1, device_id=other, device_id_type=MESH)

    @pl.when((z > 0) & (z < n - 1))
    def _():
        pl.semaphore_wait(barrier, 2 + len(others))

    @pl.when((z == 0) | (z == n - 1))
    def _():
        pl.semaphore_wait(barrier, 1 + len(others))


def bit_of(index, bit):
    return (index // (1 << bit)) % 2


def across(index, bit):
    return index + (1 << bit) * (1 - 2 * bit_of(index, bit))


class Gather:
    def __init__(self, n, at, send_sem, recv_sem):
        self.n, self.at, self.send_sem, self.recv_sem = n, at, send_sem, recv_sem
        self.z = lax.axis_index("tensor")

    def copy(self, slot, step, side, source=None):
        block = self.at(slot)
        return pltpu.make_async_remote_copy(
            src_ref=block if source is None else source,
            dst_ref=block,
            send_sem=self.send_sem.at[side, step],
            recv_sem=self.recv_sem.at[side, step],
            device_id={"tensor": self.z + 1 - 2 * side},
            device_id_type=MESH,
        )

    def sends(self, step, side):
        z, n = self.z, self.n
        slot = z - (1 - 2 * side) * (step - 1)
        target = z + 1 - 2 * side
        return slot, (slot >= 0) & (slot < n) & (target >= 0) & (target < n)

    def send(self, step, side, source=None):
        slot, valid = self.sends(step, side)

        @pl.when(valid)
        def _():
            self.copy(slot, step, side, source).start()

    def begin(self, source=None):
        self.send(1, 0, source)
        self.send(1, 1, source)

    def arrive(self, step, side, forward=True):
        z, n = self.z, self.n
        slot = z - (1 - 2 * side) * step

        @pl.when((slot >= 0) & (slot < n))
        def _():
            self.copy(slot, step, side).wait_recv()

        if forward is True:
            self.send(step + 1, side)
        return slot, (slot >= 0) & (slot < n)

    def drain(self, source=None):
        for step in range(1, self.n):
            for side in range(2):
                slot, valid = self.sends(step, side)

                @pl.when(valid)
                def _(slot=slot, step=step, side=side):
                    self.copy(slot, step, side, source if step == 1 else None).wait_send()


class Scatter:
    def __init__(self, n, buffer, send_sem, recv_sem):
        self.n, self.buffer, self.send_sem, self.recv_sem = n, buffer, send_sem, recv_sem
        self.z = lax.axis_index("tensor")

    def copy(self, step, side):
        return pltpu.make_async_remote_copy(
            src_ref=self.buffer.at[side, step - 1],
            dst_ref=self.buffer.at[side, step],
            send_sem=self.send_sem.at[side, step],
            recv_sem=self.recv_sem.at[side, step],
            device_id={"tensor": self.z + 1 - 2 * side},
            device_id_type=MESH,
        )

    def turn(self, step, side):
        z, n = self.z, self.n
        return z + (1 - 2 * side) * (n - step), step >= 1 + z + side * (n - 1 - 2 * z)

    def has_source(self, side):
        source = self.z - (1 - 2 * side)
        return (source >= 0) & (source < self.n)

    def push(self, step, side, part):
        slot = self.buffer.at[side, step - 1]
        has_source = self.has_source(side)

        @pl.when(has_source)
        def _():
            self.copy(step - 1, side).wait_recv()
            slot[...] = (part() + slot[...].astype(F32)).astype(BF)

        @pl.when(jnp.logical_not(has_source))
        def _():
            slot[...] = part().astype(BF)

        self.copy(step, side).start()

    def settle(self, total_ref):
        for side in range(2):

            @pl.when(self.has_source(side))
            def _(side=side):
                self.copy(self.n - 1, side).wait_recv()
                total_ref[...] += self.buffer[side, self.n - 1].astype(F32)

    def drain(self):
        for step in range(1, self.n):
            for side in range(2):

                @pl.when(self.turn(step, side)[1])
                def _(step=step, side=side):
                    self.copy(step, side).wait_send()


def by_rows(rows, body, block=32):
    def step(index, carry):
        body(rows_at(index, block))
        return carry

    lax.fori_loop(0, rows // block, step, 0)


def norm_rows(values, gain):
    inverse = lax.rsqrt(jnp.mean(values * values, axis=-1, keepdims=True) + norm_eps)
    return values * inverse * gain, inverse


class Doubling:
    def __init__(self, size, source, target, keep_sem, send_sem, recv_sem):
        self.source, self.target = source, target
        self.keep_sem, self.send_sem, self.recv_sem = keep_sem, send_sem, recv_sem
        self.rows, columns = source.shape
        self.half = columns // 2
        self.me = lax.axis_index("dp")
        self.bits = size.bit_length() - 1
        rest = list(range(1, self.bits))
        self.orders = (rest + [0], rest[::-1] + [0])

    def index(self, order, stage, number):
        index = self.me
        for place in range(stage):
            if (number >> place) & 1:
                index = across(index, order[place])
        return index

    def copy(self, half, stage, number):
        order = self.orders[half]
        columns = slice(half * self.half, (half + 1) * self.half)
        place = self.target.at[rows_at(self.index(order, stage, number), self.rows), columns]
        return pltpu.make_async_remote_copy(
            src_ref=self.source.at[:, columns] if number == 0 else place,
            dst_ref=place,
            send_sem=self.send_sem.at[half, (1 << stage) + number],
            recv_sem=self.recv_sem.at[half, (1 << stage) + number],
            device_id={"dp": across(self.me, order[stage])},
            device_id_type=MESH,
        )

    def arrival(self, half, stage, number):
        order = self.orders[half]
        columns = slice(half * self.half, (half + 1) * self.half)
        index = across(self.index(order, stage, number), order[stage])
        place = self.target.at[rows_at(index, self.rows), columns]
        return pltpu.make_async_remote_copy(
            src_ref=place,
            dst_ref=place,
            send_sem=self.send_sem.at[half, (1 << stage) + number],
            recv_sem=self.recv_sem.at[half, (1 << stage) + number],
            device_id={"dp": across(self.me, order[stage])},
            device_id_type=MESH,
        )

    def own(self):
        return pltpu.make_async_copy(
            self.source, self.target.at[rows_at(self.me, self.rows)], self.keep_sem
        )

    def start(self, stage):
        for half in range(2):
            for number in range(1 << stage):
                self.copy(half, stage, number).start()

    def begin(self):
        self.own().start()
        self.start(0)

    def advance(self, stage):
        for half in range(2):
            for number in range(1 << stage):
                self.arrival(half, stage, number).wait_recv()
        if stage + 1 < self.bits:
            self.start(stage + 1)

    def drain(self, own=True):
        if own:
            self.own().wait()
        for half in range(2):
            for stage in range(self.bits):
                for number in range(1 << stage):
                    self.copy(half, stage, number).wait_send()


class Halving:
    def __init__(self, size, rows, grad, keep, buffer, keep_sem, send_sem, recv_sem):
        self.rows, self.grad, self.keep, self.buffer = rows, grad, keep, buffer
        self.keep_sem, self.send_sem, self.recv_sem = keep_sem, send_sem, recv_sem
        self.me = lax.axis_index("dp")
        self.bits = size.bit_length() - 1
        rest = list(range(1, self.bits))
        self.orders = ([0] + rest, [0] + rest[::-1])
        self.half = buffer.shape[-1]
        self.size = size

    def count(self, stage):
        return self.size >> (stage + 1)

    def offset(self, stage):
        return self.size - (self.size >> stage)

    def block_rows(self, half, number, mine):
        order = self.orders[half]
        first = bit_of(self.me, 0)
        index = first if mine else 1 - first
        later = order[1:]
        for place, bit in enumerate(later):
            index = index + ((number >> (len(later) - 1 - place)) & 1) * (1 << bit)
        return rows_at(index, self.rows)

    def columns(self, half):
        return slice(half * self.half, (half + 1) * self.half)

    def load(self, half, number):
        return pltpu.make_async_copy(
            self.grad.at[self.block_rows(half, number, True), self.columns(half)],
            self.keep.at[half, number],
            self.keep_sem.at[half, number],
        )

    def first_copy(self, half, number):
        return pltpu.make_async_remote_copy(
            src_ref=self.grad.at[self.block_rows(half, number, False), self.columns(half)],
            dst_ref=self.buffer.at[half, number],
            send_sem=self.send_sem.at[half, number],
            recv_sem=self.recv_sem.at[half, number],
            device_id={"dp": across(self.me, 0)},
            device_id_type=MESH,
        )

    def copy(self, half, stage):
        bit = self.orders[half][stage]
        count = self.count(stage)
        goes = (1 - bit_of(self.me, bit)) * count + self.offset(stage - 1)
        return pltpu.make_async_remote_copy(
            src_ref=self.buffer.at[half, pl.ds(goes, count)],
            dst_ref=self.buffer.at[half, pl.ds(self.offset(stage), count)],
            send_sem=self.send_sem.at[half, self.offset(stage)],
            recv_sem=self.recv_sem.at[half, self.offset(stage)],
            device_id={"dp": across(self.me, bit)},
            device_id_type=MESH,
        )

    def begin(self):
        for half in range(2):
            for number in range(self.count(0)):
                self.first_copy(half, number).start()
                self.load(half, number).start()

    def advance(self, stage):
        for half in range(2):
            if stage == 0:
                for number in range(self.count(0)):
                    self.first_copy(half, number).wait_recv()
                    self.load(half, number).wait()
            else:
                self.copy(half, stage).wait_recv()
            if stage == self.bits - 1:
                continue
            base = bit_of(self.me, self.orders[half][stage]) * self.count(stage)

            def add(number, carry, half=half, base=base):
                place = self.offset(stage) + number
                if stage == 0:
                    kept = self.keep[half, number]
                else:
                    kept = self.buffer[half, self.offset(stage - 1) + base + number]
                self.buffer[half, place] = (
                    self.buffer[half, place].astype(F32) + kept.astype(F32)
                ).astype(BF)
                return carry

            lax.fori_loop(0, self.count(stage), add, 0)
            self.copy(half, stage + 1).start()

    def result(self, half):
        stage = self.bits - 1
        base = bit_of(self.me, self.orders[half][stage])
        return self.buffer[half, self.offset(stage)].astype(F32) + self.buffer[
            half, self.offset(stage - 1) + base
        ].astype(F32)

    def drain(self):
        for half in range(2):
            for number in range(self.count(0)):
                self.first_copy(half, number).wait_send()
            for stage in range(1, self.bits):
                self.copy(half, stage).wait_send()


def forward_kernel(
    n,
    dp,
    kv_local,
    x_ref,
    gains_ref,
    wq_ref,
    wgu_ref,
    wo_ref,
    wd_ref,
    cot_ref,
    seg_ref,
    pos_ref,
    freq_ref,
    wqkv_hbm,
    wout_hbm,
    wgu_hbm,
    wd_hbm,
    g1_hbm,
    q_hbm,
    k_hbm,
    v_hbm,
    o_hbm,
    cos_hbm,
    low_hbm,
    high_hbm,
    prob_hbm,
    gf_all,
    m_ref,
    n2_ref,
    stat_ref,
    g1,
    wqkv,
    wout,
    own_qkv,
    own_out,
    own_gu,
    q_ref,
    k_ref,
    v_ref,
    o_ref,
    cos_ref,
    low_ref,
    high_ref,
    v_t,
    key_seg,
    key_pos,
    bias,
    prob,
    part,
    sums,
    load_sem,
    out_sem,
    prob_sem,
    own_sem,
    n1_send,
    n1_recv,
    ag_send,
    ag_recv,
    rs_send,
    rs_recv,
    keep_sem,
    dp_send,
    dp_recv,
):
    z = lax.axis_index("tensor")
    me = lax.axis_index("dp")
    tokens, width = x_ref.shape
    heads = REPEAT * kv_local
    ff = wd_ref.shape[2]
    half_head = HEAD_WIDTH // 2
    dp_bits = dp.bit_length() - 1
    gain_one, gain_two = gains_ref[0, 0:1, :], gains_ref[0, 1:2, :]
    first_row = pl.multiple_of(z * tokens, tokens)

    def normalize(rows):
        place = pl.ds(pl.multiple_of(first_row + rows.start, rows.size), rows.size)
        g1[place, :] = norm_rows(x_ref[rows, :], gain_one)[0].astype(BF)

    by_rows(tokens, normalize)
    for padded, shard in ((own_qkv, wq_ref), (own_out, wo_ref)):
        padded[...] = jnp.zeros_like(padded)
        for head in range(padded.shape[1] // LANES):
            padded[:, head * LANES : head * LANES + HEAD_WIDTH] = shard[
                0, :, head * HEAD_WIDTH : (head + 1) * HEAD_WIDTH
            ]
    entry_barrier(n, [{"dp": across(me, bit)} for bit in range(dp_bits)])
    spread = Gather(n, lambda slot: g1.at[rows_at(slot, tokens)], n1_send, n1_recv)
    spread.begin()
    shards = [
        Doubling(dp, source, target, keep_sem.at[k], dp_send.at[k], dp_recv.at[k])
        for k, (source, target) in enumerate(
            [
                (own_qkv, wqkv_hbm),
                (own_out, wout_hbm),
                (own_gu, wgu_hbm),
                (wd_ref.at[0], wd_hbm),
            ]
        )
    ]
    early, late = shards[:2], shards[2:]
    for shard in early:
        shard.begin()
    own_gu[:, :ff] = wgu_ref[0, :, 0, :]
    own_gu[:, ff:] = wgu_ref[0, :, 1, :]

    def tables(slot, carry):
        rows = rows_at(slot, tokens)

        def column(row):
            return jnp.broadcast_to(row.astype(F32), (LANES, tokens)).T

        places = column(pos_ref[slot])
        key_pos[rows, :] = places
        key_seg[rows, :] = column(seg_ref[slot])
        angles = places * freq_ref[...]
        sine = jnp.sin(angles)
        lane = lax.broadcasted_iota(jnp.int32, sine.shape, 1)
        cos_ref[rows, :] = jnp.cos(angles)
        low_ref[rows, :] = jnp.where(lane < half_head, -sine, 0.0)
        high_ref[rows, :] = jnp.where((lane >= half_head) & (lane < HEAD_WIDTH), sine, 0.0)
        return carry

    lax.fori_loop(0, n, tables, 0)
    for shard in early:
        shard.advance(0)
    for shard in late:
        shard.begin()
    for stage in range(1, dp_bits):
        for shard in early:
            shard.advance(stage)
    for shard in early:
        shard.own().wait()
    loads = [
        pltpu.make_async_copy(wqkv_hbm, wqkv, load_sem.at[0]),
        pltpu.make_async_copy(wout_hbm, wout, load_sem.at[1]),
    ]
    for load in loads:
        load.start()
    gather = Gather(n, lambda slot: gf_all.at[rows_at(slot, tokens)], ag_send, ag_recv)
    keep = pltpu.make_async_copy(cot_ref, gf_all.at[rows_at(z, tokens)], own_sem)
    keep.start()
    loads[0].wait()
    group_width = (REPEAT + 2) * LANES

    def project(slot):
        rows = rows_at(slot, tokens)
        cosine, low, high = cos_ref[rows, :], low_ref[rows, :], high_ref[rows, :]

        def turn(values):
            return (
                values * cosine
                + pltpu.roll(values, LANES - half_head, 1) * low
                + pltpu.roll(values, half_head, 1) * high
            ).astype(BF)

        for group in range(kv_local):
            joined = nn(g1[rows, :], wqkv[:, group * group_width : (group + 1) * group_width])
            for member in range(REPEAT):
                q_ref[group * REPEAT + member, rows, :] = turn(
                    joined[:, member * LANES : (member + 1) * LANES]
                )
            k_ref[group, rows, :] = turn(joined[:, REPEAT * LANES : (REPEAT + 1) * LANES])
            values = joined[:, (REPEAT + 1) * LANES :]
            v_ref[group, rows, :] = values.astype(BF)

    def project_of(index, carry):
        came, near = (index + 1) // 2, (index + 1) % 2
        slot = z - (1 - 2 * near) * came

        @pl.when(index > 0)
        def _():
            spread.arrive(came, near, forward=None)

        @pl.when((index > 0) & (came < n - 1))
        def _():
            spread.send(came + 1, near)

        @pl.when(index == 2 * (n - 2))
        def _():
            gather.begin(cot_ref)

        for stage in range(min(2, dp_bits)):

            @pl.when(index == 3 + 2 * stage)
            def _(stage=stage):
                for shard in late:
                    shard.advance(stage)

        @pl.when((slot >= 0) & (slot < n))
        def _():
            project(slot)

        return carry

    lax.fori_loop(0, 2 * n - 1, project_of, 0)
    outs = [
        pltpu.make_async_copy(source, target, out_sem.at[k])
        for k, (source, target) in enumerate(
            [
                (q_ref, q_hbm),
                (k_ref, k_hbm),
                (v_ref, v_hbm),
                (cos_ref, cos_hbm),
                (low_ref, low_hbm),
                (high_ref, high_hbm),
                (g1, g1_hbm),
                (o_ref, o_hbm),
            ]
        )
    ]
    for out in outs[:-1]:
        out.start()
    for group in range(kv_local):
        v_t[group] = v_ref[group].astype(F32).T.astype(BF)
    loads[1].wait()
    scatter = Scatter(n, sums, rs_send, rs_recv)
    log2_scale = HEAD_WIDTH ** (-0.5) * 1.4426950408889634

    def attend(target):
        rows = rows_at(target, tokens)
        for first in range(0, tokens, LANES):
            lanes = slice(first, first + LANES)
            seen = (key_seg[...] == 0.0) | (
                key_seg[...] == seg_ref[target, :, lanes].astype(F32)
            )
            seen = seen & (key_pos[...] <= pos_ref[target, :, lanes].astype(F32))
            bias[:, lanes] = jnp.where(seen, 0.0, -1e30)

        def one_head(head, carry):
            group = head // REPEAT
            scores = nt(k_ref[group], q_ref[head, rows, :]) * log2_scale + bias[...]
            top = jnp.max(scores, axis=0, keepdims=True)
            weights = jnp.exp2(scores - top)
            total = jnp.sum(weights, axis=0, keepdims=True)
            prob[head] = (weights * (1.0 / total)).astype(BF)
            mixed = nn(v_t[group], prob[head])
            o_ref[rows, rows_at(head, LANES)] = mixed.T.astype(BF)
            return carry

        lax.fori_loop(0, heads, one_head, 0)
        out = pltpu.make_async_copy(prob, prob_hbm.at[target], prob_sem)
        out.start()
        for first in range(0, width, 512):
            part[:, first : first + 512] = nt(o_ref[rows, :], wout[first : first + 512, :])
        out.wait()

    def turn_of(index, carry):
        step, side = index // 2 + 1, index % 2
        target, valid = scatter.turn(step, side)

        @pl.when(valid)
        def _():
            attend(target)

            @pl.when(step < n)
            def _():
                scatter.push(step, side, lambda: part[...])

        for stage in range(2, dp_bits):

            @pl.when(index == 2 * (stage - 2) + 1)
            def _(stage=stage):
                for shard in late:
                    shard.advance(stage)

        @pl.when(step < n)
        def _():
            gather.arrive(step, side, forward=None)

        @pl.when(step < n - 1)
        def _():
            gather.send(step + 1, side)

        return carry

    lax.fori_loop(0, 2 * (n - 1) + 1, turn_of, 0)
    outs[-1].start()
    scatter.settle(part)
    stat_ref[...] = jnp.zeros_like(stat_ref)

    def finish(rows):
        branch = part[rows, :]
        middle = x_ref[rows, :] + branch
        m_ref[rows, :] = middle
        n2_ref[rows, :] = norm_rows(middle, gain_two)[0].astype(BF)
        stat_ref[0:1, :] += jnp.sum(middle * middle, axis=0, keepdims=True)
        stat_ref[1:2, :] += jnp.sum(branch * branch, axis=0, keepdims=True)

    by_rows(tokens, finish)
    keep.wait()
    for out in outs:
        out.wait()
    spread.drain()
    gather.drain(cot_ref)
    scatter.drain()
    for shard in early:
        shard.drain(own=False)
    for shard in late:
        shard.drain()


def forward(n, dp, kv_local, x, gains, w_qkv, w_gate_up, w_out, w_down, cot, seg, pos, freq):
    tokens, width = x.shape
    group_len = n * tokens
    heads = REPEAT * kv_local
    owned = w_qkv.shape[1]
    ff = w_down.shape[2]
    lanes, out_lanes = (REPEAT + 2) * kv_local * LANES, heads * LANES
    vmem = pl.BlockSpec(memory_space=pltpu.VMEM)
    hbm = pl.BlockSpec(memory_space=pl.ANY)
    kept = [
        ((heads, group_len, LANES), BF),
        ((kv_local, group_len, LANES), BF),
        ((kv_local, group_len, LANES), BF),
        ((group_len, out_lanes), BF),
        ((group_len, LANES), F32),
        ((group_len, LANES), F32),
        ((group_len, LANES), F32),
    ]
    flops = 2 * group_len * (
        width * lanes + width * out_lanes + 2 * heads * group_len * LANES
    )
    return pl.pallas_call(
        functools.partial(forward_kernel, n, dp, kv_local),
        out_shape=(
            jax.ShapeDtypeStruct((width, lanes), BF),
            jax.ShapeDtypeStruct((width, out_lanes), BF),
            jax.ShapeDtypeStruct((width, 2 * ff), BF),
            jax.ShapeDtypeStruct((width, ff), BF),
            jax.ShapeDtypeStruct((group_len, width), BF),
            *[jax.ShapeDtypeStruct(shape, kind) for shape, kind in kept],
            jax.ShapeDtypeStruct((n, heads, group_len, tokens), BF),
            jax.ShapeDtypeStruct((group_len, width), BF),
            jax.ShapeDtypeStruct((tokens, width), F32),
            jax.ShapeDtypeStruct((tokens, width), BF),
            jax.ShapeDtypeStruct((8, width), F32),
        ),
        in_specs=[vmem] * 10,
        out_specs=(hbm,) * 14 + (vmem,) * 3,
        scratch_shapes=[
            pltpu.VMEM((group_len, width), BF),
            pltpu.VMEM((width, lanes), BF),
            pltpu.VMEM((width, out_lanes), BF),
            pltpu.VMEM((owned, lanes), BF),
            pltpu.VMEM((owned, out_lanes), BF),
            pltpu.VMEM((owned, 2 * ff), BF),
            *[pltpu.VMEM(shape, kind) for shape, kind in kept],
            pltpu.VMEM((kv_local, LANES, group_len), BF),
            pltpu.VMEM((group_len, LANES), F32),
            pltpu.VMEM((group_len, LANES), F32),
            pltpu.VMEM((group_len, tokens), F32),
            pltpu.VMEM((heads, group_len, tokens), BF),
            pltpu.VMEM((tokens, width), F32),
            pltpu.VMEM((2, n, tokens, width), BF),
            pltpu.SemaphoreType.DMA((2,)),
            pltpu.SemaphoreType.DMA((8,)),
            pltpu.SemaphoreType.DMA,
            pltpu.SemaphoreType.DMA,
            *[pltpu.SemaphoreType.DMA((2, n))] * 6,
            pltpu.SemaphoreType.DMA((4,)),
            pltpu.SemaphoreType.DMA((4, 2, dp)),
            pltpu.SemaphoreType.DMA((4, 2, dp)),
        ],
        compiler_params=pltpu.CompilerParams(
            collective_id=1, has_side_effects=True, vmem_limit_bytes=VMEM_LIMIT
        ),
        cost_estimate=pl.CostEstimate(
            flops=flops, bytes_accessed=200 * tokens * width * 2, transcendentals=0
        ),
        name="attend_forward",
    )(x, gains, w_qkv, w_gate_up, w_out, w_down, cot, seg, pos, freq)


def feed_kernel(
    n,
    chunks,
    n2_ref,
    gf_hbm,
    wgu_hbm,
    wd_hbm,
    m_ref,
    gain_ref,
    cot_ref,
    z_hbm,
    dm_ref,
    ga_ref,
    dgain_ref,
    dwgu_hbm,
    dwgu_ref,
    n2_all,
    gf_all,
    z_all,
    dgu,
    wgu,
    wd,
    part,
    dn2,
    sums,
    load_sem,
    gf_sem,
    z_sem,
    dw_sem,
    ag_send,
    ag_recv,
    rs_send,
    rs_recv,
):
    z = lax.axis_index("tensor")
    tokens, width = n2_ref.shape
    ff = wd_hbm.shape[1]
    piece = tokens // chunks
    rows_chunk = n * piece
    load_gu = pltpu.make_async_copy(wgu_hbm, wgu, load_sem.at[0])
    load_d = pltpu.make_async_copy(wd_hbm, wd, load_sem.at[1])

    def load_gf(chunk, slot):
        return pltpu.make_async_copy(
            gf_hbm.at[pl.ds(pl.multiple_of(slot * tokens + chunk * piece, piece), piece)],
            gf_all.at[pl.ds(pl.multiple_of(chunk * rows_chunk + slot * piece, piece), piece)],
            gf_sem.at[chunk, slot],
        )

    load_gu.start()
    load_d.start()
    for chunk in range(chunks):
        for slot in range(n):
            load_gf(chunk, slot).start()
        n2_all[pl.ds(pl.multiple_of(chunk * rows_chunk + z * piece, piece), piece), :] = n2_ref[
            chunk * piece : (chunk + 1) * piece, :
        ]
    entry_barrier(n)

    def gather_of(chunk):
        return Gather(
            n,
            lambda slot: n2_all.at[
                pl.ds(pl.multiple_of(chunk * rows_chunk + slot * piece, piece), piece)
            ],
            ag_send.at[chunk],
            ag_recv.at[chunk],
        )

    def scatter_of(chunk):
        return Scatter(n, sums.at[chunk], rs_send.at[chunk], rs_recv.at[chunk])

    gather_of(0).begin()

    def scatter_end(chunk):
        own = dn2.at[rows_at(chunk, piece)]
        own[...] = part[chunk, rows_at(z, piece), :]
        scatter_of(chunk).settle(own)

    block = 256
    hidden_blocks = ff // block
    out_blocks = width // 512

    def hidden_block(chunk, index):
        rows = rows_at(chunk, rows_chunk)
        cols = rows_at(index, block)
        up_cols = pl.ds(pl.multiple_of(ff + index * block, block), block)
        gate = nn(n2_all[rows, :], wgu[:, cols])
        up = nn(n2_all[rows, :], wgu[:, up_cols])
        dz = nn(gf_all[rows, :], wd[:, cols])
        s = 1.0 / (1.0 + jnp.exp(-gate))
        act = gate * s
        z_all[rows, cols] = (act * up).astype(BF)
        dgu[rows, cols] = (dz * up * (s * (1.0 + gate * (1.0 - s)))).astype(BF)
        dgu[rows, up_cols] = (dz * act).astype(BF)

    def out_block(chunk, index):
        rows = rows_at(chunk, rows_chunk)
        cols = rows_at(index, 512)
        part[chunk, :, cols] = nt(dgu[rows, :], wgu[cols, :])

    def z_out(chunk):
        rows = rows_at(chunk, rows_chunk)
        return pltpu.make_async_copy(z_all.at[rows], z_hbm.at[rows], z_sem.at[chunk])

    def compute(chunk):
        for slot in range(n):
            load_gf(chunk, slot).wait()

        def hidden(index, carry):
            hidden_block(chunk, index)
            return carry

        def out(index, carry):
            out_block(chunk, index)
            return carry

        lax.fori_loop(0, hidden_blocks, hidden, 0)
        lax.fori_loop(0, out_blocks, out, 0)
        z_out(chunk).start()

    def grad_gu(index, carry):
        cols = rows_at(index, 256)
        dwgu_ref[:, cols] = tn(n2_all[...], dgu[:, cols]).astype(BF)
        dw_out(index).start()
        return carry

    def dw_out(index):
        cols = rows_at(index, 256)
        return pltpu.make_async_copy(dwgu_ref.at[:, cols], dwgu_hbm.at[:, cols], dw_sem.at[index])

    blocks = 2 * ff // 256

    def within(chunk):
        return (chunk >= 0) & (chunk < chunks)

    def stage(index, carry):
        for step in range(n - 1, 0, -1):
            chunk = index - (step - 1)

            @pl.when(within(chunk))
            def _(step=step, chunk=chunk):
                for side in range(2):
                    gather_of(chunk).arrive(step, side, forward=step < n - 1)

        @pl.when(index + 1 < chunks)
        def _():
            gather_of(index + 1).begin()

        ready = index - (n - 2)

        @pl.when(within(ready - (n - 1)))
        def _():
            scatter_end(ready - (n - 1))

        def push(chunk, step):
            scatter = scatter_of(chunk)
            for side in range(2):
                target, valid = scatter.turn(step, side)

                @pl.when(valid)
                def _(side=side, target=target):
                    scatter.push(step, side, lambda: part[chunk, rows_at(target, piece), :])

        for step in range(n - 1, 1, -1):
            chunk = ready - (step - 1)

            @pl.when(within(chunk))
            def _(step=step, chunk=chunk):
                push(chunk, step)

        @pl.when(ready == 0)
        def _():
            load_gu.wait()
            load_d.wait()

        @pl.when(within(ready))
        def _():
            compute(ready)
            push(ready, 1)

        @pl.when(ready >= chunks)
        def _():
            late = ready - chunks
            lax.fori_loop(blocks * late // (n - 1), blocks * (late + 1) // (n - 1), grad_gu, 0)

        return carry

    lax.fori_loop(0, chunks + 2 * n - 3, stage, 0)
    gain = gain_ref[0, 1:2, :]
    dgain_ref[...] = jnp.zeros_like(dgain_ref)

    def finish(rows):
        middle = m_ref[rows, :]
        dn = dn2[rows, :]
        inverse = lax.rsqrt(jnp.mean(middle * middle, axis=-1, keepdims=True) + norm_eps)
        scaled = dn * gain
        dgain_ref[0:1, :] += jnp.sum(dn * middle * inverse, axis=0, keepdims=True)
        dm = (
            inverse * scaled
            - middle * inverse**3 * jnp.mean(scaled * middle, axis=-1, keepdims=True)
            + cot_ref[rows, :].astype(F32)
        )
        dm_ref[rows, :] = dm
        ga_ref[rows, :] = dm.astype(BF)

    by_rows(tokens, finish)
    for index in range(blocks):
        dw_out(index).wait()
    for chunk in range(chunks):
        z_out(chunk).wait()
        gather_of(chunk).drain()
        scatter_of(chunk).drain()


def feed(n, chunks, n2, gf_all, wgu, wd, m, gain, cot):
    tokens, width = n2.shape
    group_len = n * tokens
    ff = wd.shape[1]
    vmem = pl.BlockSpec(memory_space=pltpu.VMEM)
    hbm = pl.BlockSpec(memory_space=pl.ANY)
    return pl.pallas_call(
        functools.partial(feed_kernel, n, chunks),
        out_shape=(
            jax.ShapeDtypeStruct((group_len, ff), BF),
            jax.ShapeDtypeStruct((tokens, width), F32),
            jax.ShapeDtypeStruct((tokens, width), BF),
            jax.ShapeDtypeStruct((8, width), F32),
            jax.ShapeDtypeStruct((width, 2 * ff), BF),
        ),
        in_specs=[vmem, hbm, hbm, hbm, vmem, vmem, vmem],
        out_specs=(hbm, vmem, vmem, vmem, hbm),
        scratch_shapes=[
            pltpu.VMEM((width, 2 * ff), BF),
            pltpu.VMEM((group_len, width), BF),
            pltpu.VMEM((group_len, width), BF),
            pltpu.VMEM((group_len, ff), BF),
            pltpu.VMEM((group_len, 2 * ff), BF),
            pltpu.VMEM((width, 2 * ff), BF),
            pltpu.VMEM((width, ff), BF),
            pltpu.VMEM((chunks, group_len // chunks, width), F32),
            pltpu.VMEM((tokens, width), F32),
            pltpu.VMEM((chunks, 2, n, tokens // chunks, width), BF),
            pltpu.SemaphoreType.DMA((2,)),
            pltpu.SemaphoreType.DMA((chunks, n)),
            pltpu.SemaphoreType.DMA((chunks,)),
            pltpu.SemaphoreType.DMA((2 * ff // 256,)),
            pltpu.SemaphoreType.DMA((chunks, 2, n)),
            pltpu.SemaphoreType.DMA((chunks, 2, n)),
            pltpu.SemaphoreType.DMA((chunks, 2, n)),
            pltpu.SemaphoreType.DMA((chunks, 2, n)),
        ],
        compiler_params=pltpu.CompilerParams(
            collective_id=3, has_side_effects=True, vmem_limit_bytes=VMEM_LIMIT
        ),
        cost_estimate=pl.CostEstimate(
            flops=18 * group_len * width * ff, bytes_accessed=250 * tokens * width * 2, transcendentals=0
        ),
        name="feed_both",
    )(n2, gf_all, wgu, wd, m, gain, cot)


def attend_back_kernel(
    n,
    dp,
    kv_local,
    chunks,
    ga_ref,
    wout_hbm,
    wd_hbm,
    z_hbm,
    prob_hbm,
    g1_hbm,
    gf_hbm,
    dwgu_hbm,
    m_ref,
    q_ref,
    k_ref,
    v_ref,
    o_ref,
    cos_ref,
    sin_low_ref,
    sin_high_ref,
    out_ref,
    stat_ref,
    dqkv_ref,
    dw_hbm,
    grad_gu_ref,
    dw_ref,
    keep,
    held,
    ga_all,
    g1,
    gf,
    wout,
    wd,
    z_all,
    k_t,
    prob,
    d_out,
    dk,
    dv,
    part,
    sums,
    load_sem,
    gf_sem,
    prob_sem,
    dw_sem,
    ag_send,
    ag_recv,
    rs_send,
    rs_recv,
    keep_sem,
    dp_send,
    dp_recv,
):
    z = lax.axis_index("tensor")
    tokens, width = ga_ref.shape
    heads = REPEAT * kv_local
    group_len = n * tokens
    piece = tokens // chunks
    scale = HEAD_WIDTH ** (-0.5)
    loads = [
        pltpu.make_async_copy(source, target, load_sem.at[index])
        for index, (source, target) in enumerate(
            [(wout_hbm, wout), (z_hbm, z_all), (wd_hbm, wd), (g1_hbm, g1)]
        )
    ]
    for load in loads:
        load.start()
    load_out, load_z, load_d, load_g1 = loads

    def load_gf(chunk, slot):
        return pltpu.make_async_copy(
            gf_hbm.at[pl.ds(pl.multiple_of(slot * tokens + chunk * piece, piece), piece)],
            gf.at[pl.ds(pl.multiple_of((chunk * n + slot) * piece, piece), piece)],
            gf_sem.at[chunk, slot],
        )

    for chunk in range(chunks):
        for slot in range(n):
            load_gf(chunk, slot).start()

    def load_prob(slot):
        return pltpu.make_async_copy(prob_hbm.at[slot], prob, prob_sem)

    ga_all[rows_at(z, tokens), :] = ga_ref[...]
    me = lax.axis_index("dp")
    dp_bits = dp.bit_length() - 1
    entry_barrier(n, [{"dp": across(me, bit)} for bit in range(dp_bits)])
    gather = Gather(n, lambda slot: ga_all.at[rows_at(slot, tokens)], ag_send, ag_recv)
    gather.begin()
    halving = Halving(
        dp, grad_gu_ref.shape[0], dwgu_hbm, keep, held, keep_sem, dp_send, dp_recv
    )
    halving.begin()
    scatter = Scatter(n, sums, rs_send, rs_recv)
    for group in range(kv_local):
        k_t[group] = k_ref[group].astype(F32).T.astype(BF)
    dk[...] = jnp.zeros_like(dk)
    dv[...] = jnp.zeros_like(dv)
    load_out.wait()
    load_z.wait()
    load_d.wait()
    group_lanes = (REPEAT + 2) * LANES

    def turn_back(values, rows):
        return (
            values * cos_ref[rows, :]
            - pltpu.roll(values, LANES - HEAD_WIDTH // 2, 1) * sin_low_ref[rows, :]
            - pltpu.roll(values, HEAD_WIDTH // 2, 1) * sin_high_ref[rows, :]
        )

    def back(slot):
        rows = rows_at(slot, tokens)
        d_o = nn(ga_all[rows, :], wout[...])
        d_out[...] = d_o.astype(BF)

        def one_head(head, carry):
            group = head // REPEAT
            lanes = rows_at(head, LANES)
            do_h = d_out[:, lanes]
            both = do_h.astype(F32) * o_ref[rows, lanes].astype(F32)
            delta = jnp.sum(both.T, axis=0, keepdims=True)
            dprob = nt(v_ref[group], do_h)
            weights = prob[head]
            ds = (weights.astype(F32) * (dprob - delta)).astype(BF)
            dv[group] += nn(weights, do_h)
            dk[group] += nn(ds, q_ref[head, rows, :])
            dq = nn(k_t[group], ds).T * scale
            first = group * (REPEAT + 2) + head % REPEAT
            dqkv_ref[rows, rows_at(first, LANES)] = turn_back(dq, rows).astype(BF)
            return carry

        lax.fori_loop(0, heads, one_head, 0)

    def feed_rows(target):
        pieces = [
            z_all[
                pl.ds(
                    pl.multiple_of(chunk * n * piece + target * piece, piece), piece
                ),
                :,
            ]
            for chunk in range(chunks)
        ]
        rows = jnp.concatenate(pieces, axis=0) if chunks > 1 else pieces[0]
        for first in range(0, width, 512):
            part[:, first : first + 512] = nt(rows, wd[first : first + 512, :])

    def turn_of(index, carry):
        came, near = (index + 1) // 2, (index + 1) % 2
        slot = z - (1 - 2 * near) * came
        valid = (slot >= 0) & (slot < n)

        @pl.when(valid)
        def _():
            load_prob(slot).start()

        @pl.when(index > 0)
        def _():
            gather.arrive(came, near, forward=None)

        @pl.when((index > 0) & (came < n - 1))
        def _():
            gather.send(came + 1, near)

        step, side = index // 2 + 1, index % 2
        target, sends = scatter.turn(step, side)

        @pl.when(sends & (step < n))
        def _():
            feed_rows(target)
            scatter.push(step, side, lambda: part[...])

        @pl.when(valid)
        def _():
            load_prob(slot).wait()
            back(slot)

        return carry

    for chunk in range(chunks):
        for slot in range(n):
            load_gf(chunk, slot).wait()
    ff = wd_hbm.shape[1]
    down_blocks = ff // 256
    down_first = heads * LANES + dqkv_ref.shape[1]

    def grad_down(first, last):
        def body(index, carry):
            cols = rows_at(index, 256)
            place = pl.ds(pl.multiple_of(down_first + index * 256, 256), 256)
            dw_ref[:, place] = tn(gf[...], z_all[:, cols]).astype(BF)
            return carry

        lax.fori_loop(first, last, body, 0)

    turns = 2 * n - 1

    def turn_and_grad(index, carry):
        turn_of(index, 0)
        grad_down(down_blocks * index // turns, down_blocks * (index + 1) // turns)
        for stage in range(dp_bits):

            @pl.when(index == 2 * stage + 1)
            def _(stage=stage):
                halving.advance(stage)

        return carry

    lax.fori_loop(0, turns, turn_and_grad, 0)

    def finish_keys(slot, carry):
        rows = rows_at(slot, tokens)
        for group in range(kv_local):
            first = group * group_lanes + REPEAT * LANES
            dqkv_ref[rows, first : first + LANES] = turn_back(
                dk[group, rows, :] * scale, rows
            ).astype(BF)
            dqkv_ref[rows, first + LANES : first + 2 * LANES] = dv[group, rows, :].astype(BF)
        return carry

    lax.fori_loop(0, n, finish_keys, 0)
    load_g1.wait()
    out_lanes = heads * LANES

    def dw_out(which):
        first, size = (
            (down_first, ff),
            (out_lanes, dqkv_ref.shape[1]),
            (0, out_lanes),
        )[which]
        cols = slice(first, first + size)
        return pltpu.make_async_copy(dw_ref.at[:, cols], dw_hbm.at[:, cols], dw_sem.at[which])

    dw_out(0).start()

    def grad_qkv(index, carry):
        cols = rows_at(index, 256)
        place = pl.ds(pl.multiple_of(out_lanes + index * 256, 256), 256)
        dw_ref[:, place] = tn(g1[...], dqkv_ref[:, cols]).astype(BF)
        return carry

    lax.fori_loop(0, dqkv_ref.shape[1] // 256, grad_qkv, 0)
    dw_out(1).start()

    def grad_out(index, carry):
        cols = rows_at(index, 256)
        dw_ref[:, cols] = tn(ga_all[...], o_ref[:, cols]).astype(BF)
        return carry

    lax.fori_loop(0, out_lanes // 256, grad_out, 0)
    dw_out(2).start()
    for half in range(2):
        grad_gu_ref[:, half, :] = halving.result(half)
    feed_rows(z)
    scatter.settle(part)
    stat_ref[...] = jnp.zeros_like(stat_ref)

    def finish(rows):
        branch = part[rows, :]
        result = m_ref[rows, :] + branch
        out_ref[rows, :] = result
        stat_ref[0:1, :] += jnp.sum(result * result, axis=0, keepdims=True)
        stat_ref[1:2, :] += jnp.sum(branch * branch, axis=0, keepdims=True)

    by_rows(tokens, finish)
    for which in range(3):
        dw_out(which).wait()
    gather.drain()
    scatter.drain()
    halving.drain()


def attend_back(n, dp, kv_local, chunks, ga, wout, wd, z_all, prob, g1, gf, dwgu, m, q, k, v, o, tables):
    tokens, width = ga.shape
    group_len = n * tokens
    heads = REPEAT * kv_local
    ff = wd.shape[1]
    owned = width // dp
    lanes = (REPEAT + 2) * kv_local * LANES
    vmem = pl.BlockSpec(memory_space=pltpu.VMEM)
    hbm = pl.BlockSpec(memory_space=pl.ANY)
    return pl.pallas_call(
        functools.partial(attend_back_kernel, n, dp, kv_local, chunks),
        out_shape=(
            jax.ShapeDtypeStruct((tokens, width), F32),
            jax.ShapeDtypeStruct((8, width), F32),
            jax.ShapeDtypeStruct((group_len, lanes), BF),
            jax.ShapeDtypeStruct((width, heads * LANES + lanes + ff), BF),
            jax.ShapeDtypeStruct((owned, 2, ff), F32),
        ),
        in_specs=[vmem] + [hbm] * 7 + [vmem] * 8,
        out_specs=(vmem, vmem, vmem, hbm, vmem),
        scratch_shapes=[
            pltpu.VMEM((width, heads * LANES + lanes + ff), BF),
            pltpu.VMEM((2, dp // 2, owned, ff), BF),
            pltpu.VMEM((2, dp - 1, owned, ff), BF),
            pltpu.VMEM((group_len, width), BF),
            pltpu.VMEM((group_len, width), BF),
            pltpu.VMEM((group_len, width), BF),
            pltpu.VMEM(wout.shape, BF),
            pltpu.VMEM(wd.shape, BF),
            pltpu.VMEM((group_len, ff), BF),
            pltpu.VMEM((kv_local, LANES, group_len), BF),
            pltpu.VMEM((heads, group_len, tokens), BF),
            pltpu.VMEM((tokens, heads * LANES), BF),
            pltpu.VMEM((kv_local, group_len, LANES), F32),
            pltpu.VMEM((kv_local, group_len, LANES), F32),
            pltpu.VMEM((tokens, width), F32),
            pltpu.VMEM((2, n, tokens, width), BF),
            pltpu.SemaphoreType.DMA((4,)),
            pltpu.SemaphoreType.DMA((chunks, n)),
            pltpu.SemaphoreType.DMA,
            pltpu.SemaphoreType.DMA((3,)),
            pltpu.SemaphoreType.DMA((2, n)),
            pltpu.SemaphoreType.DMA((2, n)),
            pltpu.SemaphoreType.DMA((2, n)),
            pltpu.SemaphoreType.DMA((2, n)),
            pltpu.SemaphoreType.DMA((2, dp // 2)),
            pltpu.SemaphoreType.DMA((2, dp)),
            pltpu.SemaphoreType.DMA((2, dp)),
        ],
        compiler_params=pltpu.CompilerParams(
            collective_id=4, has_side_effects=True, vmem_limit_bytes=VMEM_LIMIT
        ),
        cost_estimate=pl.CostEstimate(
            flops=8 * group_len * width * ff, bytes_accessed=200 * tokens * width * 2, transcendentals=0
        ),
        name="attend_backward",
    )(ga, wout, wd, z_all, prob, g1, gf, dwgu, m, q, k, v, o, *tables)


def last_kernel(
    n,
    dp,
    cells,
    out_heads,
    qkv_heads,
    dqkv_ref,
    wqkv_ref,
    x_ref,
    dm_ref,
    gain_ref,
    dgain_two_ref,
    stat_one_ref,
    stat_two_ref,
    g1_hbm,
    dw_hbm,
    dx_ref,
    gains_ref,
    rms_ref,
    grad_out_ref,
    grad_qkv_ref,
    grad_down_ref,
    g1,
    part,
    sums,
    keep,
    blocks,
    vector,
    vectors,
    rs_send,
    rs_recv,
    g1_sem,
    keep_sem,
    dp_send,
    dp_recv,
    all_send,
    all_recv,
):
    z = lax.axis_index("tensor")
    me = lax.axis_index("dp")
    tokens, width = x_ref.shape
    load_g1 = pltpu.make_async_copy(g1_hbm, g1, g1_sem)
    load_g1.start()
    dp_bits, z_bits = dp.bit_length() - 1, n.bit_length() - 1
    partners = [{"dp": across(me, bit)} for bit in range(dp_bits)]
    partners += [{"tensor": across(z, bit)} for bit in range(z_bits)]
    entry_barrier(n, partners[:dp_bits] + partners[dp_bits + 1 :])
    halving = Halving(dp, grad_out_ref.shape[0], dw_hbm, keep, blocks, keep_sem, dp_send, dp_recv)
    halving.begin()
    scatter = Scatter(n, sums, rs_send, rs_recv)
    gain = gain_ref[0, 0:1, :]
    vector[...] = jnp.zeros_like(vector)
    vector[1:2, :] = dgain_two_ref[0:1, :]
    vector[2:3, :] = stat_one_ref[0:1, :]
    vector[3:4, :] = stat_two_ref[0:1, :]
    vector[4:5, :] = stat_one_ref[1:2, :]
    vector[5:6, :] = stat_two_ref[1:2, :]
    load_g1.wait()

    def compute(index, carry):
        step, side = index // 2 + 1, index % 2
        target, due = scatter.turn(step, side)

        @pl.when(due)
        def _():
            rows = rows_at(target, tokens)

            def block(number, carry):
                cols = rows_at(number, 256)
                values = nt(dqkv_ref[rows, :], wqkv_ref[cols, :])
                part[rows, cols] = values
                vector[0:1, cols] += jnp.sum(
                    values * g1[rows, cols].astype(F32), axis=0, keepdims=True
                )
                return carry

            lax.fori_loop(0, width // 256, block, 0)

            @pl.when((step < n) & jnp.logical_not(scatter.has_source(side)))
            def _():
                scatter.push(step, side, lambda: part[rows, :])

        return carry

    lax.fori_loop(0, 2 * n - 1, compute, 0)
    vector[0:1, :] = vector[0:1, :] / gain

    def exchange(index):
        return pltpu.make_async_remote_copy(
            src_ref=vector if index == 0 else vectors.at[index - 1],
            dst_ref=vectors.at[index],
            send_sem=all_send.at[index],
            recv_sem=all_recv.at[index],
            device_id=partners[index],
            device_id_type=MESH,
        )

    def meet(index):
        exchange(index).wait_recv()
        held = vector[...] if index == 0 else vectors[index - 1]
        vectors[index] += held
        if index + 1 < len(partners):
            exchange(index + 1).start()

    exchange(0).start()
    stages = max(len(partners), dp_bits)
    for step in range(1, n):
        for side in range(2):
            target, sends = scatter.turn(step, side)

            @pl.when(sends & scatter.has_source(side))
            def _(step=step, side=side, target=target):
                rows = rows_at(target, tokens)
                scatter.push(step, side, lambda: part[rows, :])

        for index in range(stages * (step - 1) // (n - 1), stages * step // (n - 1)):
            if index < len(partners):
                meet(index)
        for index in range(dp_bits * (step - 1) // (n - 1), dp_bits * step // (n - 1)):
            halving.advance(index)
    place = 0
    for half in range(2):
        block = halving.result(half)
        for index in range(block.shape[1] // LANES):
            values = block[:, index * LANES : (index + 1) * LANES]
            if place < out_heads:
                grad_out_ref[:, place * HEAD_WIDTH : (place + 1) * HEAD_WIDTH] = values[
                    :, :HEAD_WIDTH
                ]
            elif place < out_heads + qkv_heads:
                head = place - out_heads
                grad_qkv_ref[:, head * HEAD_WIDTH : (head + 1) * HEAD_WIDTH] = values[
                    :, :HEAD_WIDTH
                ]
            else:
                first = (place - out_heads - qkv_heads) * LANES
                grad_down_ref[:, first : first + LANES] = values
            place += 1
    total = vectors[len(partners) - 1]
    gains_ref[0] = total[0:2, :]
    squares = jnp.sqrt(jnp.sum(total, axis=1, keepdims=True) * (1.0 / cells))
    row = lax.broadcasted_iota(jnp.int32, (8, 4), 0)
    column = lax.broadcasted_iota(jnp.int32, (8, 4), 1)
    rms_ref[...] = jnp.sum(jnp.where(row == column + 2, squares, 0.0), axis=0, keepdims=True)
    own = part.at[rows_at(z, tokens)]
    scatter.settle(own)

    def finish(rows):
        values = x_ref[rows, :]
        dn = own[rows, :]
        inverse = lax.rsqrt(jnp.mean(values * values, axis=-1, keepdims=True) + norm_eps)
        scaled = dn * gain
        dx_ref[rows, :] = (
            inverse * scaled
            - values * inverse**3 * jnp.mean(scaled * values, axis=-1, keepdims=True)
            + dm_ref[rows, :]
        )

    by_rows(tokens, finish)
    for index in range(len(partners)):
        exchange(index).wait_send()
    halving.drain()
    scatter.drain()


def last(n, dqkv, wqkv, x, dm, gain, dgain_two, stat_one, stat_two, g1, dw, out_columns, qkv_columns, ff):
    tokens, width = x.shape
    dp = lax.axis_size("dp")
    owned = width // dp
    stages = (dp.bit_length() - 1) + (n.bit_length() - 1)
    half = dw.shape[1] // 2
    vmem = pl.BlockSpec(memory_space=pltpu.VMEM)
    hbm = pl.BlockSpec(memory_space=pl.ANY)
    return pl.pallas_call(
        functools.partial(
            last_kernel,
            n,
            dp,
            tokens * width * dp * n,
            out_columns // HEAD_WIDTH,
            qkv_columns // HEAD_WIDTH,
        ),
        out_shape=(
            jax.ShapeDtypeStruct((tokens, width), F32),
            jax.ShapeDtypeStruct((1, 2, width), F32),
            jax.ShapeDtypeStruct((1, 4), F32),
            jax.ShapeDtypeStruct((owned, out_columns), F32),
            jax.ShapeDtypeStruct((owned, qkv_columns), F32),
            jax.ShapeDtypeStruct((owned, ff), F32),
        ),
        in_specs=[vmem] * 8 + [hbm] * 2,
        out_specs=(vmem,) * 6,
        scratch_shapes=[
            pltpu.VMEM((n * tokens, width), BF),
            pltpu.VMEM((n * tokens, width), F32),
            pltpu.VMEM((2, n, tokens, width), BF),
            pltpu.VMEM((2, dp // 2, owned, half), BF),
            pltpu.VMEM((2, dp - 1, owned, half), BF),
            pltpu.VMEM((8, width), F32),
            pltpu.VMEM((stages, 8, width), F32),
            pltpu.SemaphoreType.DMA((2, n)),
            pltpu.SemaphoreType.DMA((2, n)),
            pltpu.SemaphoreType.DMA,
            pltpu.SemaphoreType.DMA((2, dp // 2)),
            pltpu.SemaphoreType.DMA((2, dp)),
            pltpu.SemaphoreType.DMA((2, dp)),
            pltpu.SemaphoreType.DMA((stages,)),
            pltpu.SemaphoreType.DMA((stages,)),
        ],
        compiler_params=pltpu.CompilerParams(
            collective_id=5, has_side_effects=True, vmem_limit_bytes=VMEM_LIMIT
        ),
        cost_estimate=pl.CostEstimate(
            flops=2 * dqkv.size * width, bytes_accessed=150 * tokens * width * 2, transcendentals=0
        ),
        name="input_gradient",
    )(dqkv, wqkv, x, dm, gain, dgain_two, stat_one, stat_two, g1, dw)


def per_device(inputs, norm_gains, w_qkv, w_gate_up, w_out, w_down, segments, positions, cotangent):
    n, dp = lax.axis_size("tensor"), lax.axis_size("dp")
    tokens, width = inputs.shape
    kv_local = w_out.shape[2] // (REPEAT * HEAD_WIDTH)
    ff_local = w_down.shape[2]
    chunks = 4
    half = HEAD_WIDTH // 2
    freq_steps = jnp.arange(half, dtype=F32) * (2.0 / HEAD_WIDTH)
    inverse = jnp.power(rope_base, -freq_steps)
    freq = jnp.concatenate([inverse, inverse, jnp.zeros((LANES - HEAD_WIDTH,), F32)])[None]

    (
        wqkv,
        wout,
        wgu,
        wd,
        g1,
        q,
        k,
        v,
        o,
        cosine,
        low,
        high,
        prob,
        gf_all,
        m,
        n2,
        stat_one,
    ) = forward(
        n,
        dp,
        kv_local,
        inputs,
        norm_gains,
        w_qkv,
        w_gate_up,
        w_out,
        w_down,
        cotangent,
        segments.reshape(n, 1, tokens),
        positions.reshape(n, 1, tokens),
        freq,
    )
    z_all, dm, ga, dgain_two, dwgu = feed(n, chunks, n2, gf_all, wgu, wd, m, norm_gains, cotangent)
    output, stat_two, dqkv, dw, grad_gu = attend_back(
        n,
        dp,
        kv_local,
        chunks,
        ga,
        wout,
        wd,
        z_all,
        prob,
        g1,
        gf_all,
        dwgu,
        m,
        q,
        k,
        v,
        o,
        (cosine, low, high),
    )
    input_grad, gain_total, rms, grad_out, grad_qkv, grad_down = last(
        n,
        dqkv,
        wqkv,
        inputs,
        dm,
        norm_gains,
        dgain_two,
        stat_one,
        stat_two,
        g1,
        dw,
        w_out.shape[2],
        w_qkv.shape[2],
        ff_local,
    )
    return (
        output,
        input_grad,
        grad_qkv[None],
        grad_gu[None],
        grad_out[None],
        grad_down[None],
        gain_total,
        rms,
    )


def solution(mesh):
    rows = P(("dp", "tensor"), None)
    weights = P(None, "dp", "tensor")
    pairs = P(None, "dp", None, "tensor")
    return jax.shard_map(
        per_device,
        mesh=mesh,
        in_specs=(rows, P(), weights, pairs, weights, weights, P("dp"), P("dp"), rows),
        out_specs=(rows, rows, weights, pairs, weights, weights, P(), P()),
        check_vma=False,
    )
```

time: 1170 us -> 415 us (0.35)
  waiting for transfers between devices: 846 us -> 0 us
  Pallas kernels: 0 us -> 405 us
  matrix products: 126 us -> 0 us
  local copies, waits for them, and re-layouts: 84.5 us -> 8.09 us
  other arithmetic: 49.1 us -> 0.6 us
  blocking collectives: 41 us -> 0 us
  between operations: 14.6 us -> 0.72 us
    reduce_scatter x7 -> x0, waiting for transfers between devices: 540 us -> none  [the longest x2 219 us: collect_rows(): return lax.psum_scatter(values, 'tensor', scatter_dimension=0, tiled=True)]
    pallas_call x0 -> x4, Pallas kernels: none -> 405 us  [the longest x1 152 us: forward(): pl.pallas_call(functools.partial(forward_kernel, n, dp, kv_local), out_sh...]
    all_gather x8 -> x0, waiting for transfers between devices: 302 us -> none  [the longest x2 115 us: spread_rows(): return lax.all_gather(values, 'tensor', axis=0, tiled=True)]
    dot_general x26 -> x0, matrix products: 126 us -> none  [the longest x2 18.5 us: refold(): jnp.einsum('td,tc->dc', lax.all_gather(normed_local, 'tensor', axis=0, ti...]
    psum x1 -> x0, blocking collectives: 41 us -> none  [per_device(): lax.psum((jnp.stack(gain_list), jnp.stack(stat_rows)), ('dp', 'tensor'))]
    dynamic_update_slice x4 -> x0, local copies, waits for them, and re-layouts: 31.7 us -> none  [per_device(): lax.scan(back_block, (zero_rows, zero_rows), (query_matrix.reshape(blocks...]
    reduce_sum x7 -> x0, other arithmetic: 18.9 us -> none  [the longest x1 5.39 us: per_device(): jnp.sum(output * output)]
    all_gather x1 -> x0, local copies, waits for them, and re-layouts: 16.5 us -> none  [per_device(): lax.all_gather(w_gate_up[layer_index], 'dp', axis=0, tiled=True)]
  transfers between devices with their start and end apart: 16 -> 0, of which waited for: 14 -> 0; matrix products, arithmetic and copies ran while one was open for 19% -> 0% of each run, Pallas kernels for 0% -> 0%
where the time goes in v2:
time: 415 us; the launch traced here: 414 us
  Pallas kernels  405 us (98%)
  local copies, waits for them, and re-layouts  8.09 us (2%)
    pallas_call x1, Pallas kernels, forward(): pl.pallas_call(functools.partial(forward_kernel, n, dp, kv_local), out_sh...  152 us
    pallas_call x1, Pallas kernels, feed(): pl.pallas_call(functools.partial(feed_kernel, n, chunks), out_shape=(jax....  103 us
    pallas_call x1, Pallas kernels, attend_back(): pl.pallas_call(functools.partial(attend_back_kernel, n, dp, kv_local, chu...  83.4 us
    pallas_call x1, Pallas kernels, last(): pl.pallas_call(functools.partial(last_kernel, n, dp, tokens * width * dp...  66.6 us

profile of v2, /device:TPU:0, one launch (start us, length us, event | category | flops | bytes accessed | tf_op | source)
XLA Modules:
  0.0 414.3 jit_solution(14328516120384641762)
XLA Ops:
  0.7 0.6 maximum_bitcast_fusion.freq_ref
  1.2 151.9 %attend_forward.1 = (bf16[1536,1024]{1,0:T(8,128)(2,1)}, bf16[1536,512]{1,0:T(8,128)(2,1)}, bf16[1536,2048]{1,0:T(8,128)(2,1)}, bf16[1536,1024]{1,0:T(8,128)(2,1...) custom-call(f32[256,1536]{1,0:T(8,128)} %x_ref.3, ...), custom_call_target="tpu_custom_call" | custom-call | flops 6979321856 | bytes 157286400 | tf_op jit(solution)/shard_map/attend_forward/pallas_call | solution.py:699
  153.2 103.0 %feed_both.1 = (bf16[1024,1024]{1,0:T(8,128)(2,1)}, f32[256,1536]{1,0:T(8,128)}, bf16[256,1536]{1,0:T(8,128)(2,1)}, f32[8,1536]{1,0:T(8,128)}, bf16[1536,2048]{1,0:T(8,128)(2,1)}) custom-call(bf16[256,1536]{1,0:T(8,128)(2,1)} %get-tuple-element.41.n2_ref, bf16[1024,1536]{1,0:T(8,128)(2,1)} %get-tuple-element.42.gf_hbm, ...), custom_call_target="tpu_custom_call" | custom-call | flops 28991029248 | bytes 196608000 | tf_op jit(solution)/shard_map/feed_both/pallas_call | solution.py:971
  256.1 83.4 %attend_backward.1 = (f32[256,1536]{1,0:T(8,128)}, f32[8,1536]{1,0:T(8,128)}, bf16[1024,1024]{1,0:T(8,128)(2,1)}, bf16[1536,2560]{1,0:T(8,128)(2,1)}, f32[192,2,1024]{2,1,0:T(2,128)}) custom-call(bf16[256,1536]{1,0:T(8,128)(2,1)} %get-tuple-element.46.ga_ref, bf16[1536,512]{1,0:T(8,128)(2,1)} %get-tuple-element.47.wout_hbm, ...), custom_call_target="tpu_custom_call" | custom-call | flops 12884901888 | bytes 157286400 | tf_op jit(solution)/shard_map/attend_backward/pallas_call | solution.py:1294
  339.6 0.0 copy-start.1
  339.6 66.6 %input_gradient.1 = (f32[256,1536]{1,0:T(8,128)}, f32[1,2,1536]{2,1,0:T(2,128)}, f32[1,4]{1,0:T(1,128)}, f32[192,384]{1,0:T(8,128)}, f32[192,768]{1,0:T(8,128)}, /*index=5*/f32[192,1024]{1,0:T(8,128)}) custom-call(bf16[1024,1024]{1,0:T(8,128)(2,1)} %get-tuple-element.60.dqkv_ref, bf16[1536,1024]{1,0:T(8,128)(2,1)} %get-tuple-element.61.wqkv_ref, ...), custom_call_target="tpu_custom_call" | custom-call | flops 3221225472 | bytes 117964800 | tf_op jit(solution)/shard_map/input_gradient/pallas_call | solution.py:1517
  406.2 0.0 copy-start.2
  406.2 0.0 copy-done.1
  406.2 1.1 copy.25
  407.3 0.8 copy-done.2
  408.2 0.0 copy-start.4
  408.2 0.0 copy-start
  408.2 1.1 copy.26
  409.3 0.3 copy-done.4
  409.6 0.0 copy-start.5
  409.6 0.8 copy.27
  410.4 0.0 copy-done
  410.4 0.0 copy-start.3
  410.4 0.0 copy-start.6
  410.4 0.0 copy-start.7
  410.4 1.1 copy.28
  411.6 0.0 copy-done.5
  411.6 0.7 copy.29
  412.3 0.0 copy-done.3
  412.3 0.9 copy.30
  413.2 0.0 copy-done.6
  413.2 0.6 copy.31
  413.8 0.0 copy-done.7
  413.8 0.5 copy.32
  (2 shorter events, 0.0 us)
Async XLA Ops:
  339.6 66.6 %copy-start.1 = (f32[256,1536]{1,0:T(8,128)S(1)}, f32[256,1536]{1,0:T(8,128)}, u32[]{:S(2)}) copy-start(f32[256,1536]{1,0:T(8,128)} %get-tuple-element.82) | copy-start | bytes 4718596
  406.2 2.0 copy-start.2
  408.2 1.4 copy-start.4
  408.2 2.3 copy-start
  409.6 2.0 copy-start.5
  410.4 1.9 copy-start.3
  410.4 2.8 copy-start.6
  410.4 3.4 copy-start.7

commit v3 on v2

--- a/solution.py
+++ b/solution.py
@@ -19,6 +19,8 @@
 BF = jnp.bfloat16
 F32 = jnp.float32
 VMEM_LIMIT = 60 * 2**20
+PIECES = 1
+LAG = 2
 
 
 def nn(a, b):
@@ -37,7 +39,7 @@
     return pl.ds(pl.multiple_of(index * size, size), size)
 
 
-def entry_barrier(n, others=()):
+def greet(n, others=()):
     z = lax.axis_index("tensor")
     barrier = pltpu.get_barrier_semaphore()
 
@@ -51,6 +53,11 @@
 
     for other in others:
         pl.semaphore_signal(barrier, inc=1, device_id=other, device_id_type=MESH)
+
+
+def greeted(n, others=()):
+    z = lax.axis_index("tensor")
+    barrier = pltpu.get_barrier_semaphore()
 
     @pl.when((z > 0) & (z < n - 1))
     def _():
@@ -73,14 +80,17 @@
     def __init__(self, n, at, send_sem, recv_sem):
         self.n, self.at, self.send_sem, self.recv_sem = n, at, send_sem, recv_sem
         self.z = lax.axis_index("tensor")
-
-    def copy(self, slot, step, side, source=None):
+        self.pieces = send_sem.shape[-1]
+
+    def copy(self, slot, step, side, piece, source=None):
         block = self.at(slot)
+        size = block.shape[0] // self.pieces
+        rows = pl.ds(piece * size, size)
         return pltpu.make_async_remote_copy(
-            src_ref=block if source is None else source,
-            dst_ref=block,
-            send_sem=self.send_sem.at[side, step],
-            recv_sem=self.recv_sem.at[side, step],
+            src_ref=(block if source is None else source).at[rows],
+            dst_ref=block.at[rows],
+            send_sem=self.send_sem.at[side, step, piece],
+            recv_sem=self.recv_sem.at[side, step, piece],
             device_id={"tensor": self.z + 1 - 2 * side},
             device_id_type=MESH,
         )
@@ -91,50 +101,66 @@
         target = z + 1 - 2 * side
         return slot, (slot >= 0) & (slot < n) & (target >= 0) & (target < n)
 
-    def send(self, step, side, source=None):
+    def send(self, step, side, piece, source=None, where=True):
         slot, valid = self.sends(step, side)
 
-        @pl.when(valid)
+        @pl.when(valid if where is True else valid & where)
         def _():
-            self.copy(slot, step, side, source).start()
+            self.copy(slot, step, side, piece, source).start()
 
     def begin(self, source=None):
-        self.send(1, 0, source)
-        self.send(1, 1, source)
-
-    def arrive(self, step, side, forward=True):
+        for piece in range(self.pieces):
+            for side in range(2):
+                self.send(1, side, piece, source)
+
+    def begin_where(self, passes_on):
+        for side in range(2):
+            source = self.z - (1 - 2 * side)
+            other = (source >= 0) & (source < self.n)
+            for piece in range(self.pieces):
+                self.send(1, side, piece, where=other if passes_on else jnp.logical_not(other))
+
+    def arrive(self, step, side, forward):
         z, n = self.z, self.n
         slot = z - (1 - 2 * side) * step
-
-        @pl.when((slot >= 0) & (slot < n))
-        def _():
-            self.copy(slot, step, side).wait_recv()
-
-        if forward is True:
-            self.send(step + 1, side)
-        return slot, (slot >= 0) & (slot < n)
+        for piece in range(self.pieces):
+
+            @pl.when((slot >= 0) & (slot < n))
+            def _(piece=piece):
+                self.copy(slot, step, side, piece).wait_recv()
+
+            if forward is not False:
+                self.send(step + 1, side, piece, where=forward)
 
     def drain(self, source=None):
         for step in range(1, self.n):
             for side in range(2):
                 slot, valid = self.sends(step, side)
-
-                @pl.when(valid)
-                def _(slot=slot, step=step, side=side):
-                    self.copy(slot, step, side, source if step == 1 else None).wait_send()
+                for piece in range(self.pieces):
+
+                    @pl.when(valid)
+                    def _(slot=slot, step=step, side=side, piece=piece):
+                        self.copy(
+                            slot, step, side, piece, source if step == 1 else None
+                        ).wait_send()
 
 
 class Scatter:
     def __init__(self, n, buffer, send_sem, recv_sem):
         self.n, self.buffer, self.send_sem, self.recv_sem = n, buffer, send_sem, recv_sem
         self.z = lax.axis_index("tensor")
-
-    def copy(self, step, side):
+        self.pieces = send_sem.shape[-1]
+        self.size = buffer.shape[2] // self.pieces
+
+    def rows(self, piece):
+        return pl.ds(piece * self.size, self.size)
+
+    def copy(self, step, side, piece):
         return pltpu.make_async_remote_copy(
-            src_ref=self.buffer.at[side, step - 1],
-            dst_ref=self.buffer.at[side, step],
-            send_sem=self.send_sem.at[side, step],
-            recv_sem=self.recv_sem.at[side, step],
+            src_ref=self.buffer.at[side, step - 1, self.rows(piece)],
+            dst_ref=self.buffer.at[side, step, self.rows(piece)],
+            send_sem=self.send_sem.at[side, step, piece],
+            recv_sem=self.recv_sem.at[side, step, piece],
             device_id={"tensor": self.z + 1 - 2 * side},
             device_id_type=MESH,
         )
@@ -147,41 +173,49 @@
         source = self.z - (1 - 2 * side)
         return (source >= 0) & (source < self.n)
 
-    def push(self, step, side, part):
-        slot = self.buffer.at[side, step - 1]
+    def push(self, step, side, part, first=0):
         has_source = self.has_source(side)
-
-        @pl.when(has_source)
-        def _():
-            self.copy(step - 1, side).wait_recv()
-            slot[...] = (part() + slot[...].astype(F32)).astype(BF)
-
-        @pl.when(jnp.logical_not(has_source))
-        def _():
-            slot[...] = part().astype(BF)
-
-        self.copy(step, side).start()
-
-    def settle(self, total_ref):
-        for side in range(2):
-
-            @pl.when(self.has_source(side))
-            def _(side=side):
-                self.copy(self.n - 1, side).wait_recv()
-                total_ref[...] += self.buffer[side, self.n - 1].astype(F32)
+        for piece in range(self.pieces):
+            slot = self.buffer.at[side, step - 1, self.rows(piece)]
+            rows = pl.ds(pl.multiple_of(first + piece * self.size, self.size), self.size)
+
+            @pl.when(has_source)
+            def _(piece=piece, slot=slot, rows=rows):
+                self.copy(step - 1, side, piece).wait_recv()
+                slot[...] = (part[rows, :] + slot[...].astype(F32)).astype(BF)
+
+            @pl.when(jnp.logical_not(has_source))
+            def _(slot=slot, rows=rows):
+                slot[...] = part[rows, :].astype(BF)
+
+            self.copy(step, side, piece).start()
+
+    def settle(self, total_ref, then=None):
+        for piece in range(self.pieces):
+            for side in range(2):
+
+                @pl.when(self.has_source(side))
+                def _(side=side, piece=piece):
+                    rows = self.rows(piece)
+                    self.copy(self.n - 1, side, piece).wait_recv()
+                    total_ref[rows, :] += self.buffer[side, self.n - 1, rows, :].astype(F32)
+
+            if then is not None:
+                then(piece, piece * self.size, self.size)
 
     def drain(self):
         for step in range(1, self.n):
             for side in range(2):
-
-                @pl.when(self.turn(step, side)[1])
-                def _(step=step, side=side):
-                    self.copy(step, side).wait_send()
-
-
-def by_rows(rows, body, block=32):
+                for piece in range(self.pieces):
+
+                    @pl.when(self.turn(step, side)[1])
+                    def _(step=step, side=side, piece=piece):
+                        self.copy(step, side, piece).wait_send()
+
+
+def by_rows(rows, body, first=0, block=32):
     def step(index, carry):
-        body(rows_at(index, block))
+        body(pl.ds(pl.multiple_of(first + index * block, block), block))
         return carry
 
     lax.fori_loop(0, rows // block, step, 0)
@@ -401,9 +435,11 @@
     high_hbm,
     prob_hbm,
     gf_all,
+    m_hbm,
+    n2_hbm,
+    stat_ref,
     m_ref,
     n2_ref,
-    stat_ref,
     g1,
     wqkv,
     wout,
@@ -426,6 +462,7 @@
     sums,
     load_sem,
     out_sem,
+    piece_sem,
     prob_sem,
     own_sem,
     n1_send,
@@ -446,6 +483,8 @@
     half_head = HEAD_WIDTH // 2
     dp_bits = dp.bit_length() - 1
     gain_one, gain_two = gains_ref[0, 0:1, :], gains_ref[0, 1:2, :]
+    others = [{"dp": across(me, bit)} for bit in range(dp_bits)]
+    greet(n, others)
     first_row = pl.multiple_of(z * tokens, tokens)
 
     def normalize(rows):
@@ -453,13 +492,7 @@
         g1[place, :] = norm_rows(x_ref[rows, :], gain_one)[0].astype(BF)
 
     by_rows(tokens, normalize)
-    for padded, shard in ((own_qkv, wq_ref), (own_out, wo_ref)):
-        padded[...] = jnp.zeros_like(padded)
-        for head in range(padded.shape[1] // LANES):
-            padded[:, head * LANES : head * LANES + HEAD_WIDTH] = shard[
-                0, :, head * HEAD_WIDTH : (head + 1) * HEAD_WIDTH
-            ]
-    entry_barrier(n, [{"dp": across(me, bit)} for bit in range(dp_bits)])
+    greeted(n, others)
     spread = Gather(n, lambda slot: g1.at[rows_at(slot, tokens)], n1_send, n1_recv)
     spread.begin()
     shards = [
@@ -474,6 +507,12 @@
         )
     ]
     early, late = shards[:2], shards[2:]
+    for padded, shard in ((own_qkv, wq_ref), (own_out, wo_ref)):
+        padded[...] = jnp.zeros_like(padded)
+        for head in range(padded.shape[1] // LANES):
+            padded[:, head * LANES : head * LANES + HEAD_WIDTH] = shard[
+                0, :, head * HEAD_WIDTH : (head + 1) * HEAD_WIDTH
+            ]
     for shard in early:
         shard.begin()
     own_gu[:, :ff] = wgu_ref[0, :, 0, :]
@@ -499,11 +538,14 @@
     lax.fori_loop(0, n, tables, 0)
     for shard in early:
         shard.advance(0)
-    for shard in late:
-        shard.begin()
+    for side in range(2):
+        spread.arrive(1, side, n > 2)
     for stage in range(1, dp_bits):
         for shard in early:
             shard.advance(stage)
+        if stage == max(dp_bits - 2, 1):
+            for shard in late:
+                shard.begin()
     for shard in early:
         shard.own().wait()
     loads = [
@@ -543,13 +585,9 @@
         came, near = (index + 1) // 2, (index + 1) % 2
         slot = z - (1 - 2 * near) * came
 
-        @pl.when(index > 0)
+        @pl.when(came > 1)
         def _():
-            spread.arrive(came, near, forward=None)
-
-        @pl.when((index > 0) & (came < n - 1))
-        def _():
-            spread.send(came + 1, near)
+            spread.arrive(came, near, came < n - 1)
 
         @pl.when(index == 2 * (n - 2))
         def _():
@@ -630,7 +668,7 @@
 
             @pl.when(step < n)
             def _():
-                scatter.push(step, side, lambda: part[...])
+                scatter.push(step, side, part)
 
         for stage in range(2, dp_bits):
 
@@ -641,17 +679,12 @@
 
         @pl.when(step < n)
         def _():
-            gather.arrive(step, side, forward=None)
-
-        @pl.when(step < n - 1)
-        def _():
-            gather.send(step + 1, side)
+            gather.arrive(step, side, step < n - 1)
 
         return carry
 
     lax.fori_loop(0, 2 * (n - 1) + 1, turn_of, 0)
     outs[-1].start()
-    scatter.settle(part)
     stat_ref[...] = jnp.zeros_like(stat_ref)
 
     def finish(rows):
@@ -662,7 +695,23 @@
         stat_ref[0:1, :] += jnp.sum(middle * middle, axis=0, keepdims=True)
         stat_ref[1:2, :] += jnp.sum(branch * branch, axis=0, keepdims=True)
 
-    by_rows(tokens, finish)
+    def piece_out(piece):
+        size = tokens // PIECES
+        rows = pl.ds(piece * size, size)
+        return [
+            pltpu.make_async_copy(source.at[rows], target.at[rows], piece_sem.at[k, piece])
+            for k, (source, target) in enumerate([(n2_ref, n2_hbm), (m_ref, m_hbm)])
+        ]
+
+    def settled(piece, first, rows):
+        by_rows(rows, finish, first)
+        for out in piece_out(piece):
+            out.start()
+
+    scatter.settle(part, settled)
+    for piece in range(PIECES):
+        for out in piece_out(piece):
+            out.wait()
     keep.wait()
     for out in outs:
         out.wait()
@@ -712,8 +761,10 @@
             jax.ShapeDtypeStruct((8, width), F32),
         ),
         in_specs=[vmem] * 10,
-        out_specs=(hbm,) * 14 + (vmem,) * 3,
+        out_specs=(hbm,) * 16 + (vmem,),
         scratch_shapes=[
+            pltpu.VMEM((tokens, width), F32),
+            pltpu.VMEM((tokens, width), BF),
             pltpu.VMEM((group_len, width), BF),
             pltpu.VMEM((width, lanes), BF),
             pltpu.VMEM((width, out_lanes), BF),
@@ -730,9 +781,10 @@
             pltpu.VMEM((2, n, tokens, width), BF),
             pltpu.SemaphoreType.DMA((2,)),
             pltpu.SemaphoreType.DMA((8,)),
+            pltpu.SemaphoreType.DMA((2, PIECES)),
             pltpu.SemaphoreType.DMA,
             pltpu.SemaphoreType.DMA,
-            *[pltpu.SemaphoreType.DMA((2, n))] * 6,
+            *[pltpu.SemaphoreType.DMA((2, n, PIECES))] * 6,
             pltpu.SemaphoreType.DMA((4,)),
             pltpu.SemaphoreType.DMA((4, 2, dp)),
             pltpu.SemaphoreType.DMA((4, 2, dp)),
@@ -750,18 +802,20 @@
 def feed_kernel(
     n,
     chunks,
-    n2_ref,
+    n2_hbm,
     gf_hbm,
     wgu_hbm,
     wd_hbm,
-    m_ref,
+    m_hbm,
     gain_ref,
-    cot_ref,
+    cot_hbm,
     z_hbm,
     dm_ref,
     ga_ref,
     dgain_ref,
     dwgu_hbm,
+    m_ref,
+    cot_ref,
     dwgu_ref,
     n2_all,
     gf_all,
@@ -773,6 +827,7 @@
     dn2,
     sums,
     load_sem,
+    n2_sem,
     gf_sem,
     z_sem,
     dw_sem,
@@ -782,7 +837,8 @@
     rs_recv,
 ):
     z = lax.axis_index("tensor")
-    tokens, width = n2_ref.shape
+    greet(n)
+    tokens, width = n2_hbm.shape
     ff = wd_hbm.shape[1]
     piece = tokens // chunks
     rows_chunk = n * piece
@@ -796,15 +852,28 @@
             gf_sem.at[chunk, slot],
         )
 
+
+    def load_n2(chunk):
+        return pltpu.make_async_copy(
+            n2_hbm.at[chunk * piece : (chunk + 1) * piece],
+            n2_all.at[pl.ds(pl.multiple_of(chunk * rows_chunk + z * piece, piece), piece)],
+            n2_sem.at[chunk],
+        )
+
+    for chunk in range(chunks):
+        load_n2(chunk).start()
     load_gu.start()
     load_d.start()
     for chunk in range(chunks):
         for slot in range(n):
             load_gf(chunk, slot).start()
-        n2_all[pl.ds(pl.multiple_of(chunk * rows_chunk + z * piece, piece), piece), :] = n2_ref[
-            chunk * piece : (chunk + 1) * piece, :
-        ]
-    entry_barrier(n)
+    load_m = pltpu.make_async_copy(m_hbm, m_ref, load_sem.at[2])
+    load_cot = pltpu.make_async_copy(cot_hbm, cot_ref, load_sem.at[3])
+    load_m.start()
+    load_cot.start()
+    greeted(n)
+    for chunk in range(chunks):
+        load_n2(chunk).wait()
 
     def gather_of(chunk):
         return Gather(
@@ -819,7 +888,9 @@
     def scatter_of(chunk):
         return Scatter(n, sums.at[chunk], rs_send.at[chunk], rs_recv.at[chunk])
 
-    gather_of(0).begin()
+    gather_of(0).begin_where(True)
+    for chunk in range(chunks):
+        gather_of(chunk).begin_where(False)
 
     def scatter_end(chunk):
         own = dn2.at[rows_at(chunk, piece)]
@@ -890,33 +961,34 @@
             @pl.when(within(chunk))
             def _(step=step, chunk=chunk):
                 for side in range(2):
-                    gather_of(chunk).arrive(step, side, forward=step < n - 1)
+                    gather_of(chunk).arrive(step, side, step < n - 1)
 
         @pl.when(index + 1 < chunks)
         def _():
-            gather_of(index + 1).begin()
+            gather_of(index + 1).begin_where(True)
 
         ready = index - (n - 2)
 
-        @pl.when(within(ready - (n - 1)))
-        def _():
-            scatter_end(ready - (n - 1))
-
-        def push(chunk, step):
+        def push(chunk, step, starts):
             scatter = scatter_of(chunk)
             for side in range(2):
                 target, valid = scatter.turn(step, side)
-
-                @pl.when(valid)
+                other = scatter.has_source(side)
+
+                @pl.when(valid & (jnp.logical_not(other) if starts else other))
                 def _(side=side, target=target):
-                    scatter.push(step, side, lambda: part[chunk, rows_at(target, piece), :])
+                    scatter.push(step, side, part.at[chunk], target * piece)
 
         for step in range(n - 1, 1, -1):
-            chunk = ready - (step - 1)
+            chunk = ready - LAG * (step - 1)
 
             @pl.when(within(chunk))
             def _(step=step, chunk=chunk):
-                push(chunk, step)
+                push(chunk, step, False)
+
+        @pl.when(within(ready - LAG * (n - 1)))
+        def _():
+            scatter_end(ready - LAG * (n - 1))
 
         @pl.when(ready == 0)
         def _():
@@ -926,16 +998,20 @@
         @pl.when(within(ready))
         def _():
             compute(ready)
-            push(ready, 1)
-
-        @pl.when(ready >= chunks)
+            for step in range(1, n):
+                push(ready, step, True)
+
+        late, turns = ready - chunks, LAG * (n - 1)
+
+        @pl.when((late >= 0) & (late < turns))
         def _():
-            late = ready - chunks
-            lax.fori_loop(blocks * late // (n - 1), blocks * (late + 1) // (n - 1), grad_gu, 0)
+            lax.fori_loop(blocks * late // turns, blocks * (late + 1) // turns, grad_gu, 0)
 
         return carry
 
-    lax.fori_loop(0, chunks + 2 * n - 3, stage, 0)
+    lax.fori_loop(0, chunks + n - 2 + LAG * (n - 1), stage, 0)
+    load_m.wait()
+    load_cot.wait()
     gain = gain_ref[0, 1:2, :]
     dgain_ref[...] = jnp.zeros_like(dgain_ref)
 
@@ -977,9 +1053,11 @@
             jax.ShapeDtypeStruct((8, width), F32),
             jax.ShapeDtypeStruct((width, 2 * ff), BF),
         ),
-        in_specs=[vmem, hbm, hbm, hbm, vmem, vmem, vmem],
+        in_specs=[hbm] * 5 + [vmem, hbm],
         out_specs=(hbm, vmem, vmem, vmem, hbm),
         scratch_shapes=[
+            pltpu.VMEM((tokens, width), F32),
+            pltpu.VMEM((tokens, width), BF),
             pltpu.VMEM((width, 2 * ff), BF),
             pltpu.VMEM((group_len, width), BF),
             pltpu.VMEM((group_len, width), BF),
@@ -990,14 +1068,15 @@
             pltpu.VMEM((chunks, group_len // chunks, width), F32),
             pltpu.VMEM((tokens, width), F32),
             pltpu.VMEM((chunks, 2, n, tokens // chunks, width), BF),
-            pltpu.SemaphoreType.DMA((2,)),
+            pltpu.SemaphoreType.DMA((4,)),
+            pltpu.SemaphoreType.DMA((chunks,)),
             pltpu.SemaphoreType.DMA((chunks, n)),
             pltpu.SemaphoreType.DMA((chunks,)),
             pltpu.SemaphoreType.DMA((2 * ff // 256,)),
-            pltpu.SemaphoreType.DMA((chunks, 2, n)),
-            pltpu.SemaphoreType.DMA((chunks, 2, n)),
-            pltpu.SemaphoreType.DMA((chunks, 2, n)),
-            pltpu.SemaphoreType.DMA((chunks, 2, n)),
+            pltpu.SemaphoreType.DMA((chunks, 2, n, 1)),
+            pltpu.SemaphoreType.DMA((chunks, 2, n, 1)),
+            pltpu.SemaphoreType.DMA((chunks, 2, n, 1)),
+            pltpu.SemaphoreType.DMA((chunks, 2, n, 1)),
         ],
         compiler_params=pltpu.CompilerParams(
             collective_id=3, has_side_effects=True, vmem_limit_bytes=VMEM_LIMIT
@@ -1014,14 +1093,28 @@
     dp,
     kv_local,
     chunks,
-    ga_ref,
+    ga_hbm,
     wout_hbm,
     wd_hbm,
     z_hbm,
     prob_hbm,
-    g1_hbm,
     gf_hbm,
     dwgu_hbm,
+    m_hbm,
+    q_hbm,
+    k_hbm,
+    v_hbm,
+    o_hbm,
+    cos_hbm,
+    low_hbm,
+    high_hbm,
+    out_hbm,
+    stat_ref,
+    dqkv_hbm,
+    dwd_hbm,
+    ga_out,
+    grad_gu_hbm,
+    out_ref,
     m_ref,
     q_ref,
     k_ref,
@@ -1030,16 +1123,12 @@
     cos_ref,
     sin_low_ref,
     sin_high_ref,
-    out_ref,
-    stat_ref,
     dqkv_ref,
-    dw_hbm,
+    dwd_ref,
     grad_gu_ref,
-    dw_ref,
     keep,
     held,
     ga_all,
-    g1,
     gf,
     wout,
     wd,
@@ -1054,7 +1143,8 @@
     load_sem,
     gf_sem,
     prob_sem,
-    dw_sem,
+    out_sem,
+    piece_sem,
     ag_send,
     ag_recv,
     rs_send,
@@ -1064,7 +1154,11 @@
     dp_recv,
 ):
     z = lax.axis_index("tensor")
-    tokens, width = ga_ref.shape
+    me = lax.axis_index("dp")
+    dp_bits = dp.bit_length() - 1
+    others = [{"dp": across(me, bit)} for bit in range(dp_bits)]
+    greet(n, others)
+    tokens, width = ga_hbm.shape
     heads = REPEAT * kv_local
     group_len = n * tokens
     piece = tokens // chunks
@@ -1072,12 +1166,24 @@
     loads = [
         pltpu.make_async_copy(source, target, load_sem.at[index])
         for index, (source, target) in enumerate(
-            [(wout_hbm, wout), (z_hbm, z_all), (wd_hbm, wd), (g1_hbm, g1)]
+            [
+                (ga_hbm, ga_all.at[rows_at(z, tokens)]),
+                (wout_hbm, wout),
+                (k_hbm, k_ref),
+                (v_hbm, v_ref),
+                (q_hbm, q_ref),
+                (o_hbm, o_ref),
+                (cos_hbm, cos_ref),
+                (low_hbm, sin_low_ref),
+                (high_hbm, sin_high_ref),
+                (z_hbm, z_all),
+                (wd_hbm, wd),
+                (m_hbm, m_ref),
+            ]
         )
     ]
     for load in loads:
         load.start()
-    load_out, load_z, load_d, load_g1 = loads
 
     def load_gf(chunk, slot):
         return pltpu.make_async_copy(
@@ -1093,24 +1199,21 @@
     def load_prob(slot):
         return pltpu.make_async_copy(prob_hbm.at[slot], prob, prob_sem)
 
-    ga_all[rows_at(z, tokens), :] = ga_ref[...]
-    me = lax.axis_index("dp")
-    dp_bits = dp.bit_length() - 1
-    entry_barrier(n, [{"dp": across(me, bit)} for bit in range(dp_bits)])
+    greeted(n, others)
     gather = Gather(n, lambda slot: ga_all.at[rows_at(slot, tokens)], ag_send, ag_recv)
+    loads[0].wait()
     gather.begin()
     halving = Halving(
         dp, grad_gu_ref.shape[0], dwgu_hbm, keep, held, keep_sem, dp_send, dp_recv
     )
     halving.begin()
     scatter = Scatter(n, sums, rs_send, rs_recv)
+    for load in loads[1:-1]:
+        load.wait()
     for group in range(kv_local):
         k_t[group] = k_ref[group].astype(F32).T.astype(BF)
     dk[...] = jnp.zeros_like(dk)
     dv[...] = jnp.zeros_like(dv)
-    load_out.wait()
-    load_z.wait()
-    load_d.wait()
     group_lanes = (REPEAT + 2) * LANES
 
     def turn_back(values, rows):
@@ -1168,11 +1271,7 @@
 
         @pl.when(index > 0)
         def _():
-            gather.arrive(came, near, forward=None)
-
-        @pl.when((index > 0) & (came < n - 1))
-        def _():
-            gather.send(came + 1, near)
+            gather.arrive(came, near, came < n - 1)
 
         step, side = index // 2 + 1, index % 2
         target, sends = scatter.turn(step, side)
@@ -1180,7 +1279,7 @@
         @pl.when(sends & (step < n))
         def _():
             feed_rows(target)
-            scatter.push(step, side, lambda: part[...])
+            scatter.push(step, side, part)
 
         @pl.when(valid)
         def _():
@@ -1194,13 +1293,11 @@
             load_gf(chunk, slot).wait()
     ff = wd_hbm.shape[1]
     down_blocks = ff // 256
-    down_first = heads * LANES + dqkv_ref.shape[1]
 
     def grad_down(first, last):
         def body(index, carry):
             cols = rows_at(index, 256)
-            place = pl.ds(pl.multiple_of(down_first + index * 256, 256), 256)
-            dw_ref[:, place] = tn(gf[...], z_all[:, cols]).astype(BF)
+            dwd_ref[:, cols] = tn(gf[...], z_all[:, cols]).astype(BF)
             return carry
 
         lax.fori_loop(first, last, body, 0)
@@ -1231,40 +1328,19 @@
         return carry
 
     lax.fori_loop(0, n, finish_keys, 0)
-    load_g1.wait()
-    out_lanes = heads * LANES
-
-    def dw_out(which):
-        first, size = (
-            (down_first, ff),
-            (out_lanes, dqkv_ref.shape[1]),
-            (0, out_lanes),
-        )[which]
-        cols = slice(first, first + size)
-        return pltpu.make_async_copy(dw_ref.at[:, cols], dw_hbm.at[:, cols], dw_sem.at[which])
-
-    dw_out(0).start()
-
-    def grad_qkv(index, carry):
-        cols = rows_at(index, 256)
-        place = pl.ds(pl.multiple_of(out_lanes + index * 256, 256), 256)
-        dw_ref[:, place] = tn(g1[...], dqkv_ref[:, cols]).astype(BF)
-        return carry
-
-    lax.fori_loop(0, dqkv_ref.shape[1] // 256, grad_qkv, 0)
-    dw_out(1).start()
-
-    def grad_out(index, carry):
-        cols = rows_at(index, 256)
-        dw_ref[:, cols] = tn(ga_all[...], o_ref[:, cols]).astype(BF)
-        return carry
-
-    lax.fori_loop(0, out_lanes // 256, grad_out, 0)
-    dw_out(2).start()
+    outs = [
+        pltpu.make_async_copy(source, target, out_sem.at[index])
+        for index, (source, target) in enumerate(
+            [(dqkv_ref, dqkv_hbm), (dwd_ref, dwd_hbm), (ga_all, ga_out), (grad_gu_ref, grad_gu_hbm)]
+        )
+    ]
+    for out in outs[:3]:
+        out.start()
     for half in range(2):
         grad_gu_ref[:, half, :] = halving.result(half)
+    outs[3].start()
     feed_rows(z)
-    scatter.settle(part)
+    loads[-1].wait()
     stat_ref[...] = jnp.zeros_like(stat_ref)
 
     def finish(rows):
@@ -1274,15 +1350,26 @@
         stat_ref[0:1, :] += jnp.sum(result * result, axis=0, keepdims=True)
         stat_ref[1:2, :] += jnp.sum(branch * branch, axis=0, keepdims=True)
 
-    by_rows(tokens, finish)
-    for which in range(3):
-        dw_out(which).wait()
+    def piece_out(piece):
+        size = tokens // PIECES
+        rows = pl.ds(piece * size, size)
+        return pltpu.make_async_copy(out_ref.at[rows], out_hbm.at[rows], piece_sem.at[piece])
+
+    def settled(piece, first, rows):
+        by_rows(rows, finish, first)
+        piece_out(piece).start()
+
+    scatter.settle(part, settled)
+    for piece in range(PIECES):
+        piece_out(piece).wait()
+    for out in outs:
+        out.wait()
     gather.drain()
     scatter.drain()
     halving.drain()
 
 
-def attend_back(n, dp, kv_local, chunks, ga, wout, wd, z_all, prob, g1, gf, dwgu, m, q, k, v, o, tables):
+def attend_back(n, dp, kv_local, chunks, ga, wout, wd, z_all, prob, gf, dwgu, m, q, k, v, o, tables):
     tokens, width = ga.shape
     group_len = n * tokens
     heads = REPEAT * kv_local
@@ -1297,16 +1384,25 @@
             jax.ShapeDtypeStruct((tokens, width), F32),
             jax.ShapeDtypeStruct((8, width), F32),
             jax.ShapeDtypeStruct((group_len, lanes), BF),
-            jax.ShapeDtypeStruct((width, heads * LANES + lanes + ff), BF),
+            jax.ShapeDtypeStruct((width, ff), BF),
+            jax.ShapeDtypeStruct((group_len, width), BF),
             jax.ShapeDtypeStruct((owned, 2, ff), F32),
         ),
-        in_specs=[vmem] + [hbm] * 7 + [vmem] * 8,
-        out_specs=(vmem, vmem, vmem, hbm, vmem),
+        in_specs=[hbm] * 15,
+        out_specs=(hbm, vmem, hbm, hbm, hbm, hbm),
         scratch_shapes=[
-            pltpu.VMEM((width, heads * LANES + lanes + ff), BF),
+            pltpu.VMEM((tokens, width), F32),
+            pltpu.VMEM((tokens, width), F32),
+            pltpu.VMEM(q.shape, BF),
+            pltpu.VMEM(k.shape, BF),
+            pltpu.VMEM(v.shape, BF),
+            pltpu.VMEM(o.shape, BF),
+            *[pltpu.VMEM((group_len, LANES), F32)] * 3,
+            pltpu.VMEM((group_len, lanes), BF),
+            pltpu.VMEM((width, ff), BF),
+            pltpu.VMEM((owned, 2, ff), F32),
             pltpu.VMEM((2, dp // 2, owned, ff), BF),
             pltpu.VMEM((2, dp - 1, owned, ff), BF),
-            pltpu.VMEM((group_len, width), BF),
             pltpu.VMEM((group_len, width), BF),
             pltpu.VMEM((group_len, width), BF),
             pltpu.VMEM(wout.shape, BF),
@@ -1319,14 +1415,15 @@
             pltpu.VMEM((kv_local, group_len, LANES), F32),
             pltpu.VMEM((tokens, width), F32),
             pltpu.VMEM((2, n, tokens, width), BF),
-            pltpu.SemaphoreType.DMA((4,)),
+            pltpu.SemaphoreType.DMA((12,)),
             pltpu.SemaphoreType.DMA((chunks, n)),
             pltpu.SemaphoreType.DMA,
-            pltpu.SemaphoreType.DMA((3,)),
-            pltpu.SemaphoreType.DMA((2, n)),
-            pltpu.SemaphoreType.DMA((2, n)),
-            pltpu.SemaphoreType.DMA((2, n)),
-            pltpu.SemaphoreType.DMA((2, n)),
+            pltpu.SemaphoreType.DMA((4,)),
+            pltpu.SemaphoreType.DMA((PIECES,)),
+            pltpu.SemaphoreType.DMA((2, n, PIECES)),
+            pltpu.SemaphoreType.DMA((2, n, PIECES)),
+            pltpu.SemaphoreType.DMA((2, n, PIECES)),
+            pltpu.SemaphoreType.DMA((2, n, PIECES)),
             pltpu.SemaphoreType.DMA((2, dp // 2)),
             pltpu.SemaphoreType.DMA((2, dp)),
             pltpu.SemaphoreType.DMA((2, dp)),
@@ -1338,7 +1435,7 @@
             flops=8 * group_len * width * ff, bytes_accessed=200 * tokens * width * 2, transcendentals=0
         ),
         name="attend_backward",
-    )(ga, wout, wd, z_all, prob, g1, gf, dwgu, m, q, k, v, o, *tables)
+    )(ga, wout, wd, z_all, prob, gf, dwgu, m, q, k, v, o, *tables)
 
 
 def last_kernel(
@@ -1346,50 +1443,83 @@
     dp,
     cells,
     out_heads,
-    qkv_heads,
-    dqkv_ref,
-    wqkv_ref,
-    x_ref,
-    dm_ref,
+    dqkv_hbm,
+    wqkv_hbm,
+    x_hbm,
+    dm_hbm,
     gain_ref,
     dgain_two_ref,
     stat_one_ref,
     stat_two_ref,
     g1_hbm,
-    dw_hbm,
-    dx_ref,
+    ga_hbm,
+    o_hbm,
+    dwd_hbm,
+    dx_hbm,
     gains_ref,
     rms_ref,
     grad_out_ref,
     grad_qkv_ref,
     grad_down_ref,
+    dx_ref,
+    dqkv,
+    wqkv,
+    x,
+    dm,
     g1,
+    ga,
+    o,
+    dw,
     part,
     sums,
-    keep,
-    blocks,
+    down_keep,
+    down_held,
+    head_keep,
+    head_held,
     vector,
     vectors,
+    load_sem,
+    piece_sem,
     rs_send,
     rs_recv,
-    g1_sem,
-    keep_sem,
-    dp_send,
-    dp_recv,
+    down_keep_sem,
+    down_send,
+    down_recv,
+    head_keep_sem,
+    head_send,
+    head_recv,
     all_send,
     all_recv,
 ):
     z = lax.axis_index("tensor")
     me = lax.axis_index("dp")
-    tokens, width = x_ref.shape
-    load_g1 = pltpu.make_async_copy(g1_hbm, g1, g1_sem)
-    load_g1.start()
+    tokens, width = x.shape
     dp_bits, z_bits = dp.bit_length() - 1, n.bit_length() - 1
     partners = [{"dp": across(me, bit)} for bit in range(dp_bits)]
     partners += [{"tensor": across(z, bit)} for bit in range(z_bits)]
-    entry_barrier(n, partners[:dp_bits] + partners[dp_bits + 1 :])
-    halving = Halving(dp, grad_out_ref.shape[0], dw_hbm, keep, blocks, keep_sem, dp_send, dp_recv)
-    halving.begin()
+    others = partners[:dp_bits] + partners[dp_bits + 1 :]
+    greet(n, others)
+    owned = grad_out_ref.shape[0]
+    loads = [
+        pltpu.make_async_copy(source, target, load_sem.at[index])
+        for index, (source, target) in enumerate(
+            [
+                (wqkv_hbm, wqkv),
+                (dqkv_hbm, dqkv),
+                (g1_hbm, g1),
+                (ga_hbm, ga),
+                (o_hbm, o),
+                (x_hbm, x),
+                (dm_hbm, dm),
+            ]
+        )
+    ]
+    for load in loads:
+        load.start()
+    greeted(n, others)
+    down = Halving(dp, owned, dwd_hbm, down_keep, down_held, down_keep_sem, down_send, down_recv)
+    down.begin()
+    halving = Halving(dp, owned, dw, head_keep, head_held, head_keep_sem, head_send, head_recv)
     scatter = Scatter(n, sums, rs_send, rs_recv)
     gain = gain_ref[0, 0:1, :]
     vector[...] = jnp.zeros_like(vector)
@@ -1398,7 +1528,8 @@
     vector[3:4, :] = stat_two_ref[0:1, :]
     vector[4:5, :] = stat_one_ref[1:2, :]
     vector[5:6, :] = stat_two_ref[1:2, :]
-    load_g1.wait()
+    for load in loads[:3]:
+        load.wait()
 
     def compute(index, carry):
         step, side = index // 2 + 1, index % 2
@@ -1410,7 +1541,7 @@
 
             def block(number, carry):
                 cols = rows_at(number, 256)
-                values = nt(dqkv_ref[rows, :], wqkv_ref[cols, :])
+                values = nt(dqkv[rows, :], wqkv[cols, :])
                 part[rows, cols] = values
                 vector[0:1, cols] += jnp.sum(
                     values * g1[rows, cols].astype(F32), axis=0, keepdims=True
@@ -1421,7 +1552,7 @@
 
             @pl.when((step < n) & jnp.logical_not(scatter.has_source(side)))
             def _():
-                scatter.push(step, side, lambda: part[rows, :])
+                scatter.push(step, side, part, target * tokens)
 
         return carry
 
@@ -1446,38 +1577,64 @@
             exchange(index + 1).start()
 
     exchange(0).start()
-    stages = max(len(partners), dp_bits)
-    for step in range(1, n):
+    down.advance(0)
+    out_lanes = o.shape[1]
+
+    def grad_qkv(index, carry):
+        place = pl.ds(pl.multiple_of(out_lanes + index * 256, 256), 256)
+        dw[:, place] = tn(g1[...], dqkv[:, rows_at(index, 256)]).astype(BF)
+        return carry
+
+    def grad_out(index, carry):
+        cols = rows_at(index, 256)
+        dw[:, cols] = tn(ga[...], o[:, cols]).astype(BF)
+        return carry
+
+    def grads():
+        for load in loads[3:]:
+            load.wait()
+        lax.fori_loop(0, dqkv.shape[1] // 256, grad_qkv, 0)
+        lax.fori_loop(0, out_lanes // 256, grad_out, 0)
+        halving.begin()
+
+    def push_came(step):
         for side in range(2):
             target, sends = scatter.turn(step, side)
 
             @pl.when(sends & scatter.has_source(side))
-            def _(step=step, side=side, target=target):
-                rows = rows_at(target, tokens)
-                scatter.push(step, side, lambda: part[rows, :])
-
-        for index in range(stages * (step - 1) // (n - 1), stages * step // (n - 1)):
-            if index < len(partners):
-                meet(index)
-        for index in range(dp_bits * (step - 1) // (n - 1), dp_bits * step // (n - 1)):
-            halving.advance(index)
+            def _(side=side, target=target):
+                scatter.push(step, side, part, target * tokens)
+
+    work = [grads]
+    for index in range(max(len(partners), dp_bits + 1)):
+        if index < len(partners):
+            work.append(functools.partial(meet, index))
+        if index + 1 < dp_bits:
+            work.append(functools.partial(down.advance, index + 1))
+        if 1 <= index <= dp_bits:
+            work.append(functools.partial(halving.advance, index - 1))
+    done = 0
+    for step in range(2, n):
+        push_came(step)
+        until = len(work) * (step - 1) // (n - 2)
+        for item in work[done:until]:
+            item()
+        done = until
+    for item in work[done:]:
+        item()
+    for half in range(2):
+        columns = down.columns(half)
+        grad_down_ref[:, columns] = down.result(half)
     place = 0
     for half in range(2):
         block = halving.result(half)
         for index in range(block.shape[1] // LANES):
-            values = block[:, index * LANES : (index + 1) * LANES]
+            values = block[:, index * LANES : index * LANES + HEAD_WIDTH]
             if place < out_heads:
-                grad_out_ref[:, place * HEAD_WIDTH : (place + 1) * HEAD_WIDTH] = values[
-                    :, :HEAD_WIDTH
-                ]
-            elif place < out_heads + qkv_heads:
+                grad_out_ref[:, place * HEAD_WIDTH : (place + 1) * HEAD_WIDTH] = values
+            else:
                 head = place - out_heads
-                grad_qkv_ref[:, head * HEAD_WIDTH : (head + 1) * HEAD_WIDTH] = values[
-                    :, :HEAD_WIDTH
-                ]
-            else:
-                first = (place - out_heads - qkv_heads) * LANES
-                grad_down_ref[:, first : first + LANES] = values
+                grad_qkv_ref[:, head * HEAD_WIDTH : (head + 1) * HEAD_WIDTH] = values
             place += 1
     total = vectors[len(partners) - 1]
     gains_ref[0] = total[0:2, :]
@@ -1486,43 +1643,48 @@
     column = lax.broadcasted_iota(jnp.int32, (8, 4), 1)
     rms_ref[...] = jnp.sum(jnp.where(row == column + 2, squares, 0.0), axis=0, keepdims=True)
     own = part.at[rows_at(z, tokens)]
-    scatter.settle(own)
 
     def finish(rows):
-        values = x_ref[rows, :]
+        values = x[rows, :]
         dn = own[rows, :]
         inverse = lax.rsqrt(jnp.mean(values * values, axis=-1, keepdims=True) + norm_eps)
         scaled = dn * gain
         dx_ref[rows, :] = (
             inverse * scaled
             - values * inverse**3 * jnp.mean(scaled * values, axis=-1, keepdims=True)
-            + dm_ref[rows, :]
-        )
-
-    by_rows(tokens, finish)
+            + dm[rows, :]
+        )
+
+    def piece_out(piece):
+        size = tokens // PIECES
+        rows = pl.ds(piece * size, size)
+        return pltpu.make_async_copy(dx_ref.at[rows], dx_hbm.at[rows], piece_sem.at[piece])
+
+    def settled(piece, first, rows):
+        by_rows(rows, finish, first)
+        piece_out(piece).start()
+
+    scatter.settle(own, settled)
+    for piece in range(PIECES):
+        piece_out(piece).wait()
     for index in range(len(partners)):
         exchange(index).wait_send()
+    down.drain()
     halving.drain()
     scatter.drain()
 
 
-def last(n, dqkv, wqkv, x, dm, gain, dgain_two, stat_one, stat_two, g1, dw, out_columns, qkv_columns, ff):
+def last(n, dqkv, wqkv, x, dm, gain, dgain_two, stat_one, stat_two, g1, ga, o, dwd, out_columns, qkv_columns):
     tokens, width = x.shape
     dp = lax.axis_size("dp")
     owned = width // dp
     stages = (dp.bit_length() - 1) + (n.bit_length() - 1)
-    half = dw.shape[1] // 2
+    ff = dwd.shape[1]
+    columns = o.shape[1] + dqkv.shape[1]
     vmem = pl.BlockSpec(memory_space=pltpu.VMEM)
     hbm = pl.BlockSpec(memory_space=pl.ANY)
     return pl.pallas_call(
-        functools.partial(
-            last_kernel,
-            n,
-            dp,
-            tokens * width * dp * n,
-            out_columns // HEAD_WIDTH,
-            qkv_columns // HEAD_WIDTH,
-        ),
+        functools.partial(last_kernel, n, dp, tokens * width * dp * n, out_columns // HEAD_WIDTH),
         out_shape=(
             jax.ShapeDtypeStruct((tokens, width), F32),
             jax.ShapeDtypeStruct((1, 2, width), F32),
@@ -1531,22 +1693,36 @@
             jax.ShapeDtypeStruct((owned, qkv_columns), F32),
             jax.ShapeDtypeStruct((owned, ff), F32),
         ),
-        in_specs=[vmem] * 8 + [hbm] * 2,
-        out_specs=(vmem,) * 6,
+        in_specs=[hbm] * 4 + [vmem] * 4 + [hbm] * 4,
+        out_specs=(hbm,) + (vmem,) * 5,
         scratch_shapes=[
-            pltpu.VMEM((n * tokens, width), BF),
+            pltpu.VMEM(x.shape, F32),
+            pltpu.VMEM(dqkv.shape, BF),
+            pltpu.VMEM(wqkv.shape, BF),
+            pltpu.VMEM(x.shape, F32),
+            pltpu.VMEM(dm.shape, F32),
+            pltpu.VMEM(g1.shape, BF),
+            pltpu.VMEM(ga.shape, BF),
+            pltpu.VMEM(o.shape, BF),
+            pltpu.VMEM((width, columns), BF),
             pltpu.VMEM((n * tokens, width), F32),
             pltpu.VMEM((2, n, tokens, width), BF),
-            pltpu.VMEM((2, dp // 2, owned, half), BF),
-            pltpu.VMEM((2, dp - 1, owned, half), BF),
+            pltpu.VMEM((2, dp // 2, owned, ff // 2), BF),
+            pltpu.VMEM((2, dp - 1, owned, ff // 2), BF),
+            pltpu.VMEM((2, dp // 2, owned, columns // 2), BF),
+            pltpu.VMEM((2, dp - 1, owned, columns // 2), BF),
             pltpu.VMEM((8, width), F32),
             pltpu.VMEM((stages, 8, width), F32),
-            pltpu.SemaphoreType.DMA((2, n)),
-            pltpu.SemaphoreType.DMA((2, n)),
-            pltpu.SemaphoreType.DMA,
-            pltpu.SemaphoreType.DMA((2, dp // 2)),
-            pltpu.SemaphoreType.DMA((2, dp)),
-            pltpu.SemaphoreType.DMA((2, dp)),
+            pltpu.SemaphoreType.DMA((7,)),
+            pltpu.SemaphoreType.DMA((PIECES,)),
+            pltpu.SemaphoreType.DMA((2, n, PIECES)),
+            pltpu.SemaphoreType.DMA((2, n, PIECES)),
+            *[
+                pltpu.SemaphoreType.DMA((2, dp // 2)),
+                pltpu.SemaphoreType.DMA((2, dp)),
+                pltpu.SemaphoreType.DMA((2, dp)),
+            ]
+            * 2,
             pltpu.SemaphoreType.DMA((stages,)),
             pltpu.SemaphoreType.DMA((stages,)),
         ],
@@ -1557,15 +1733,51 @@
             flops=2 * dqkv.size * width, bytes_accessed=150 * tokens * width * 2, transcendentals=0
         ),
         name="input_gradient",
-    )(dqkv, wqkv, x, dm, gain, dgain_two, stat_one, stat_two, g1, dw)
+    )(dqkv, wqkv, x, dm, gain, dgain_two, stat_one, stat_two, g1, ga, o, dwd)
+
+
+def deliver_kernel(*refs):
+    count = len(refs) // 3
+    sources, targets, held = refs[:count], refs[count : 2 * count], refs[2 * count : 3 * count]
+    sem = refs[-1]
+    ins = [
+        pltpu.make_async_copy(source, place, sem.at[0, index])
+        for index, (source, place) in enumerate(zip(sources, held, strict=True))
+    ]
+    outs = [
+        pltpu.make_async_copy(place, target, sem.at[1, index])
+        for index, (place, target) in enumerate(zip(held, targets, strict=True))
+    ]
+    for copy in ins:
+        copy.start()
+    for copy, out in zip(ins, outs, strict=True):
+        copy.wait()
+        out.start()
+    for out in outs:
+        out.wait()
+
+
+def deliver(*arrays):
+    hbm = pl.BlockSpec(memory_space=pl.ANY)
+    return pl.pallas_call(
+        deliver_kernel,
+        out_shape=[jax.ShapeDtypeStruct(array.shape, array.dtype) for array in arrays],
+        in_specs=[hbm] * len(arrays),
+        out_specs=[hbm] * len(arrays),
+        scratch_shapes=[
+            *[pltpu.VMEM(array.shape, array.dtype) for array in arrays],
+            pltpu.SemaphoreType.DMA((2, len(arrays))),
+        ],
+        compiler_params=pltpu.CompilerParams(vmem_limit_bytes=VMEM_LIMIT),
+        name="deliver",
+    )(*arrays)
 
 
 def per_device(inputs, norm_gains, w_qkv, w_gate_up, w_out, w_down, segments, positions, cotangent):
     n, dp = lax.axis_size("tensor"), lax.axis_size("dp")
     tokens, width = inputs.shape
     kv_local = w_out.shape[2] // (REPEAT * HEAD_WIDTH)
-    ff_local = w_down.shape[2]
-    chunks = 4
+    chunks = 8
     half = HEAD_WIDTH // 2
     freq_steps = jnp.arange(half, dtype=F32) * (2.0 / HEAD_WIDTH)
     inverse = jnp.power(rope_base, -freq_steps)
@@ -1605,7 +1817,7 @@
         freq,
     )
     z_all, dm, ga, dgain_two, dwgu = feed(n, chunks, n2, gf_all, wgu, wd, m, norm_gains, cotangent)
-    output, stat_two, dqkv, dw, grad_gu = attend_back(
+    output, stat_two, dqkv, dwd, ga_all, grad_gu = attend_back(
         n,
         dp,
         kv_local,
@@ -1615,7 +1827,6 @@
         wd,
         z_all,
         prob,
-        g1,
         gf_all,
         dwgu,
         m,
@@ -1636,10 +1847,14 @@
         stat_one,
         stat_two,
         g1,
-        dw,
+        ga_all,
+        o,
+        dwd,
         w_out.shape[2],
         w_qkv.shape[2],
-        ff_local,
+    )
+    output, input_grad, grad_qkv, grad_gu, grad_out, grad_down, gain_total, rms = deliver(
+        output, input_grad, grad_qkv, grad_gu, grad_out, grad_down, gain_total, rms
     )
     return (
         output,

time: 415 us -> 376 us (0.906)
  Pallas kernels: 405 us -> 372 us
  local copies, waits for them, and re-layouts: 8.09 us -> 0.01 us
    pallas_call x1, Pallas kernels: 152 us -> 133 us  [forward(): pl.pallas_call(functools.partial(forward_kernel, n, dp, kv_local), out_sh...]
    pallas_call x1, Pallas kernels: 103 us -> 91.8 us  [feed(): pl.pallas_call(functools.partial(feed_kernel, n, chunks), out_shape=(jax....]
    unnamed x24 -> x0, local copies, waits for them, and re-layouts: 8.08 us -> none
    pallas_call x0 -> x1, Pallas kernels: none -> 5.02 us  [deliver(): pl.pallas_call(deliver_kernel, out_shape=[jax.ShapeDtypeStruct(array.shap...]
    pallas_call x1, Pallas kernels: 83.4 us -> 78.9 us  [attend_back(): pl.pallas_call(functools.partial(attend_back_kernel, n, dp, kv_local, chu...]
where the time goes in v3:
time: 376 us; the launch traced here: 374 us
  Pallas kernels  372 us (99%)
    pallas_call x1, Pallas kernels, forward(): pl.pallas_call(functools.partial(forward_kernel, n, dp, kv_local), out_sh...  133 us
    pallas_call x1, Pallas kernels, feed(): pl.pallas_call(functools.partial(feed_kernel, n, chunks), out_shape=(jax....  91.8 us
    pallas_call x1, Pallas kernels, attend_back(): pl.pallas_call(functools.partial(attend_back_kernel, n, dp, kv_local, chu...  78.9 us
    pallas_call x1, Pallas kernels, last(): pl.pallas_call(functools.partial(last_kernel, n, dp, tokens * width * dp...  64.2 us

profile of v3, /device:TPU:0, one launch (start us, length us, event | category | flops | bytes accessed | tf_op | source)
XLA Modules:
  0.0 373.9 jit_solution(775347592668569984)
XLA Ops:
  0.7 0.6 maximum_bitcast_fusion.freq_ref
  1.2 132.5 %attend_forward.1 = (bf16[1536,1024]{1,0:T(8,128)(2,1)}, bf16[1536,512]{1,0:T(8,128)(2,1)}, bf16[1536,2048]{1,0:T(8,128)(2,1)}, bf16[1536,1024]{1,0:T(8,128)(2,1...) custom-call(f32[256,1536]{1,0:T(8,128)} %x_hbm.1, ...), custom_call_target="tpu_custom_call" | custom-call | flops 6979321856 | bytes 157286400 | tf_op jit(solution)/shard_map/attend_forward/pallas_call | solution.py:748
  133.8 91.8 %feed_both.1 = (bf16[1024,1024]{1,0:T(8,128)(2,1)}, f32[256,1536]{1,0:T(8,128)}, bf16[256,1536]{1,0:T(8,128)(2,1)}, f32[8,1536]{1,0:T(8,128)}, bf16[1536,2048]{1,0:T(8,128)(2,1)}) custom-call(bf16[256,1536]{1,0:T(8,128)(2,1)} %get-tuple-element.50.n2_hbm, bf16[1024,1536]{1,0:T(8,128)(2,1)} %get-tuple-element.51.gf_hbm, ...), custom_call_target="tpu_custom_call" | custom-call | flops 28991029248 | bytes 196608000 | tf_op jit(solution)/shard_map/feed_both/pallas_call | solution.py:1047
  225.6 78.9 %attend_backward.1 = (f32[256,1536]{1,0:T(8,128)}, f32[8,1536]{1,0:T(8,128)}, bf16[1024,1024]{1,0:T(8,128)(2,1)}, bf16[1536,1024]{1,0:T(8,128)(2,1)}, bf16[1024,...) custom-call(bf16[256,1536]{1,0:T(8,128)(2,1)} %get-tuple-element.55.ga_hbm, bf16[1536,512]{1,0:T(8,128)(2,1)} %get-tuple-element.56.wout_hbm, ...), custom_call_target="tpu_custom_call" | custom-call | flops 12884901888 | bytes 157286400 | tf_op jit(solution)/shard_map/attend_backward/pallas_call | solution.py:1381
  304.5 64.2 %input_gradient.1 = (f32[256,1536]{1,0:T(8,128)}, f32[1,2,1536]{2,1,0:T(2,128)}, f32[1,4]{1,0:T(1,128)}, f32[192,384]{1,0:T(8,128)}, f32[192,768]{1,0:T(8,128)}, /*index=5*/f32[192,1024]{1,0:T(8,128)}) custom-call(bf16[1024,1024]{1,0:T(8,128)(2,1)} %get-tuple-element.68.dqkv_hbm, bf16[1536,1024]{1,0:T(8,128)(2,1)} %get-tuple-element.69.wqkv_hbm, ...), custom_call_target="tpu_custom_call" | custom-call | flops 3221225472 | bytes 117964800 | tf_op jit(solution)/shard_map/input_gradient/pallas_call | solution.py:1686
  368.7 5.0 %deliver.1 = (f32[256,1536]{1,0:T(8,128)}, f32[256,1536]{1,0:T(8,128)}, f32[192,768]{1,0:T(8,128)}, f32[192,2,1024]{2,1,0:T(2,128)}, f32[192,384]{1,0:T(8,128)},...) custom-call(f32[256,1536]{1,0:T(8,128)} %get-tuple-element.67.refs_0_, ...), custom_call_target="tpu_custom_call" | custom-call | tf_op jit(solution)/shard_map/deliver/pallas_call | solution.py:1762
  (2 shorter events, 0.0 us)

commit v4 on v3

--- a/solution.py
+++ b/solution.py
@@ -19,7 +19,7 @@
 BF = jnp.bfloat16
 F32 = jnp.float32
 VMEM_LIMIT = 60 * 2**20
-PIECES = 1
+PIECES = 2
 LAG = 2
 
 
@@ -1438,6 +1438,51 @@
     )(ga, wout, wd, z_all, prob, gf, dwgu, m, q, k, v, o, *tables)
 
 
+class Sharing:
+    def __init__(self, axis, size, source, slots, send_sem, recv_sem):
+        self.axis, self.size, self.source, self.slots = axis, size, source, slots
+        self.send_sem, self.recv_sem = send_sem, recv_sem
+        self.me = lax.axis_index(axis)
+
+    def copy(self, offset):
+        return pltpu.make_async_remote_copy(
+            src_ref=self.source,
+            dst_ref=self.slots.at[self.me],
+            send_sem=self.send_sem.at[offset],
+            recv_sem=self.recv_sem.at[offset],
+            device_id={self.axis: (self.me + offset) % self.size},
+            device_id_type=MESH,
+        )
+
+    def arrival(self, offset):
+        place = self.slots.at[(self.me + self.size - offset) % self.size]
+        return pltpu.make_async_remote_copy(
+            src_ref=place,
+            dst_ref=place,
+            send_sem=self.send_sem.at[offset],
+            recv_sem=self.recv_sem.at[offset],
+            device_id={self.axis: (self.me + self.size - offset) % self.size},
+            device_id_type=MESH,
+        )
+
+    def begin(self):
+        for offset in range(1, self.size):
+            self.copy(offset).start()
+        self.slots[self.me] = self.source[...]
+
+    def total(self):
+        for offset in range(1, self.size):
+            self.arrival(offset).wait_recv()
+        total = self.slots[0]
+        for index in range(1, self.size):
+            total = total + self.slots[index]
+        return total
+
+    def drain(self):
+        for offset in range(1, self.size):
+            self.copy(offset).wait_send()
+
+
 def last_kernel(
     n,
     dp,
@@ -1477,7 +1522,10 @@
     head_keep,
     head_held,
     vector,
-    vectors,
+    packed,
+    group_sum,
+    dp_slots,
+    z_slots,
     load_sem,
     piece_sem,
     rs_send,
@@ -1488,17 +1536,20 @@
     head_keep_sem,
     head_send,
     head_recv,
-    all_send,
-    all_recv,
+    dp_slot_send,
+    dp_slot_recv,
+    z_slot_send,
+    z_slot_recv,
 ):
     z = lax.axis_index("tensor")
     me = lax.axis_index("dp")
     tokens, width = x.shape
-    dp_bits, z_bits = dp.bit_length() - 1, n.bit_length() - 1
-    partners = [{"dp": across(me, bit)} for bit in range(dp_bits)]
-    partners += [{"tensor": across(z, bit)} for bit in range(z_bits)]
-    others = partners[:dp_bits] + partners[dp_bits + 1 :]
-    greet(n, others)
+    dp_bits = dp.bit_length() - 1
+    others = [{"dp": (me + offset) % dp} for offset in range(1, dp)]
+    others += [{"tensor": (z + offset) % n} for offset in range(1, n)]
+    barrier = pltpu.get_barrier_semaphore()
+    for other in others:
+        pl.semaphore_signal(barrier, inc=1, device_id=other, device_id_type=MESH)
     owned = grad_out_ref.shape[0]
     loads = [
         pltpu.make_async_copy(source, target, load_sem.at[index])
@@ -1516,7 +1567,7 @@
     ]
     for load in loads:
         load.start()
-    greeted(n, others)
+    pl.semaphore_wait(barrier, len(others))
     down = Halving(dp, owned, dwd_hbm, down_keep, down_held, down_keep_sem, down_send, down_recv)
     down.begin()
     halving = Halving(dp, owned, dw, head_keep, head_held, head_keep_sem, head_send, head_recv)
@@ -1530,6 +1581,17 @@
     vector[5:6, :] = stat_two_ref[1:2, :]
     for load in loads[:3]:
         load.wait()
+    out_lanes = o.shape[1]
+
+    def grad_qkv(index, carry):
+        place = pl.ds(pl.multiple_of(out_lanes + index * 256, 256), 256)
+        dw[:, place] = tn(g1[...], dqkv[:, rows_at(index, 256)]).astype(BF)
+        return carry
+
+    def grad_out(index, carry):
+        cols = rows_at(index, 256)
+        dw[:, cols] = tn(ga[...], o[:, cols]).astype(BF)
+        return carry
 
     def compute(index, carry):
         step, side = index // 2 + 1, index % 2
@@ -1550,52 +1612,45 @@
 
             lax.fori_loop(0, width // 256, block, 0)
 
-            @pl.when((step < n) & jnp.logical_not(scatter.has_source(side)))
+            @pl.when((step < n - 1) & jnp.logical_not(scatter.has_source(side)))
             def _():
                 scatter.push(step, side, part, target * tokens)
 
         return carry
 
-    lax.fori_loop(0, 2 * n - 1, compute, 0)
+    def compute_and_grads(index, carry):
+        compute(index, 0)
+
+        @pl.when(index == 1)
+        def _():
+            for load in loads[3:]:
+                load.wait()
+            lax.fori_loop(0, dqkv.shape[1] // 256, grad_qkv, 0)
+            lax.fori_loop(0, out_lanes // 256, grad_out, 0)
+            halving.begin()
+
+        return carry
+
+    lax.fori_loop(0, 2 * n - 1, compute_and_grads, 0)
     vector[0:1, :] = vector[0:1, :] / gain
 
-    def exchange(index):
-        return pltpu.make_async_remote_copy(
-            src_ref=vector if index == 0 else vectors.at[index - 1],
-            dst_ref=vectors.at[index],
-            send_sem=all_send.at[index],
-            recv_sem=all_recv.at[index],
-            device_id=partners[index],
-            device_id_type=MESH,
-        )
-
-    def meet(index):
-        exchange(index).wait_recv()
-        held = vector[...] if index == 0 else vectors[index - 1]
-        vectors[index] += held
-        if index + 1 < len(partners):
-            exchange(index + 1).start()
-
-    exchange(0).start()
+    blocks = width // LANES
+    packed[...] = jnp.zeros_like(packed)
+    for row in range(6):
+        parts = [
+            vector[row : row + 1, index * LANES : (index + 1) * LANES] for index in range(blocks)
+        ]
+        if row < 2:
+            for index, values in enumerate(parts):
+                packed[row * blocks + index : row * blocks + index + 1, :] = values
+        else:
+            place = 2 * blocks + row - 2
+            packed[place : place + 1, :] = functools.reduce(jnp.add, parts)
+    near = Sharing("dp", dp, packed, dp_slots, dp_slot_send, dp_slot_recv)
+    far = Sharing("tensor", n, group_sum, z_slots, z_slot_send, z_slot_recv)
+    near.begin()
     down.advance(0)
-    out_lanes = o.shape[1]
-
-    def grad_qkv(index, carry):
-        place = pl.ds(pl.multiple_of(out_lanes + index * 256, 256), 256)
-        dw[:, place] = tn(g1[...], dqkv[:, rows_at(index, 256)]).astype(BF)
-        return carry
-
-    def grad_out(index, carry):
-        cols = rows_at(index, 256)
-        dw[:, cols] = tn(ga[...], o[:, cols]).astype(BF)
-        return carry
-
-    def grads():
-        for load in loads[3:]:
-            load.wait()
-        lax.fori_loop(0, dqkv.shape[1] // 256, grad_qkv, 0)
-        lax.fori_loop(0, out_lanes // 256, grad_out, 0)
-        halving.begin()
+    halving.advance(0)
 
     def push_came(step):
         for side in range(2):
@@ -1605,23 +1660,29 @@
             def _(side=side, target=target):
                 scatter.push(step, side, part, target * tokens)
 
-    work = [grads]
-    for index in range(max(len(partners), dp_bits + 1)):
-        if index < len(partners):
-            work.append(functools.partial(meet, index))
-        if index + 1 < dp_bits:
-            work.append(functools.partial(down.advance, index + 1))
-        if 1 <= index <= dp_bits:
-            work.append(functools.partial(halving.advance, index - 1))
-    done = 0
+    def push_last_start():
+        for side in range(2):
+            target, sends = scatter.turn(n - 1, side)
+
+            @pl.when(sends & jnp.logical_not(scatter.has_source(side)))
+            def _(side=side, target=target):
+                scatter.push(n - 1, side, part, target * tokens)
+
+    done = 1
     for step in range(2, n):
         push_came(step)
-        until = len(work) * (step - 1) // (n - 2)
-        for item in work[done:until]:
-            item()
+        if step == 2:
+            group_sum[...] = near.total()
+            far.begin()
+            push_last_start()
+        until = 1 + (dp_bits - 1) * (step - 1) // (n - 1)
+        for stage in range(done, until):
+            down.advance(stage)
+            halving.advance(stage)
         done = until
-    for item in work[done:]:
-        item()
+    for stage in range(done, dp_bits):
+        down.advance(stage)
+        halving.advance(stage)
     for half in range(2):
         columns = down.columns(half)
         grad_down_ref[:, columns] = down.result(half)
@@ -1636,12 +1697,16 @@
                 head = place - out_heads
                 grad_qkv_ref[:, head * HEAD_WIDTH : (head + 1) * HEAD_WIDTH] = values
             place += 1
-    total = vectors[len(partners) - 1]
-    gains_ref[0] = total[0:2, :]
+    total = far.total()
+    for which in range(2):
+        for index in range(blocks):
+            gains_ref[0, which : which + 1, index * LANES : (index + 1) * LANES] = total[
+                which * blocks + index : which * blocks + index + 1, :
+            ]
     squares = jnp.sqrt(jnp.sum(total, axis=1, keepdims=True) * (1.0 / cells))
-    row = lax.broadcasted_iota(jnp.int32, (8, 4), 0)
-    column = lax.broadcasted_iota(jnp.int32, (8, 4), 1)
-    rms_ref[...] = jnp.sum(jnp.where(row == column + 2, squares, 0.0), axis=0, keepdims=True)
+    row = lax.broadcasted_iota(jnp.int32, (total.shape[0], 4), 0)
+    column = lax.broadcasted_iota(jnp.int32, (total.shape[0], 4), 1)
+    rms_ref[...] = jnp.sum(jnp.where(row == column + 2 * blocks, squares, 0.0), axis=0, keepdims=True)
     own = part.at[rows_at(z, tokens)]
 
     def finish(rows):
@@ -1667,8 +1732,8 @@
     scatter.settle(own, settled)
     for piece in range(PIECES):
         piece_out(piece).wait()
-    for index in range(len(partners)):
-        exchange(index).wait_send()
+    near.drain()
+    far.drain()
     down.drain()
     halving.drain()
     scatter.drain()
@@ -1678,9 +1743,9 @@
     tokens, width = x.shape
     dp = lax.axis_size("dp")
     owned = width // dp
-    stages = (dp.bit_length() - 1) + (n.bit_length() - 1)
     ff = dwd.shape[1]
     columns = o.shape[1] + dqkv.shape[1]
+    small = -(-(2 * width // LANES + 4) // 8) * 8
     vmem = pl.BlockSpec(memory_space=pltpu.VMEM)
     hbm = pl.BlockSpec(memory_space=pl.ANY)
     return pl.pallas_call(
@@ -1712,7 +1777,10 @@
             pltpu.VMEM((2, dp // 2, owned, columns // 2), BF),
             pltpu.VMEM((2, dp - 1, owned, columns // 2), BF),
             pltpu.VMEM((8, width), F32),
-            pltpu.VMEM((stages, 8, width), F32),
+            pltpu.VMEM((small, LANES), F32),
+            pltpu.VMEM((small, LANES), F32),
+            pltpu.VMEM((dp, small, LANES), F32),
+            pltpu.VMEM((n, small, LANES), F32),
             pltpu.SemaphoreType.DMA((7,)),
             pltpu.SemaphoreType.DMA((PIECES,)),
             pltpu.SemaphoreType.DMA((2, n, PIECES)),
@@ -1723,8 +1791,10 @@
                 pltpu.SemaphoreType.DMA((2, dp)),
             ]
             * 2,
-            pltpu.SemaphoreType.DMA((stages,)),
-            pltpu.SemaphoreType.DMA((stages,)),
+            pltpu.SemaphoreType.DMA((dp,)),
+            pltpu.SemaphoreType.DMA((dp,)),
+            pltpu.SemaphoreType.DMA((n,)),
+            pltpu.SemaphoreType.DMA((n,)),
         ],
         compiler_params=pltpu.CompilerParams(
             collective_id=5, has_side_effects=True, vmem_limit_bytes=VMEM_LIMIT

time: 376 us -> 373 us (level)
  no operation moved by 1% of the time
where the time goes in v4:
time: 373 us
  Pallas kernels  371 us (99%)
    pallas_call x1, Pallas kernels, forward(): pl.pallas_call(functools.partial(forward_kernel, n, dp, kv_local), out_sh...  132 us
    pallas_call x1, Pallas kernels, feed(): pl.pallas_call(functools.partial(feed_kernel, n, chunks), out_shape=(jax....  93.6 us
    pallas_call x1, Pallas kernels, attend_back(): pl.pallas_call(functools.partial(attend_back_kernel, n, dp, kv_local, chu...  78.6 us
    pallas_call x1, Pallas kernels, last(): pl.pallas_call(functools.partial(last_kernel, n, dp, tokens * width * dp...  62.3 us

profile of v4, /device:TPU:0, one launch (start us, length us, event | category | flops | bytes accessed | tf_op | source)
XLA Modules:
  0.0 372.9 jit_solution(14094702730109436198)
XLA Ops:
  0.7 0.6 maximum_bitcast_fusion.freq_ref
  1.2 131.9 %attend_forward.1 = (bf16[1536,1024]{1,0:T(8,128)(2,1)}, bf16[1536,512]{1,0:T(8,128)(2,1)}, bf16[1536,2048]{1,0:T(8,128)(2,1)}, bf16[1536,1024]{1,0:T(8,128)(2,1...) custom-call(f32[256,1536]{1,0:T(8,128)} %x_hbm.1, ...), custom_call_target="tpu_custom_call" | custom-call | flops 6979321856 | bytes 157286400 | tf_op jit(solution)/shard_map/attend_forward/pallas_call | solution.py:748
  133.2 93.6 %feed_both.1 = (bf16[1024,1024]{1,0:T(8,128)(2,1)}, f32[256,1536]{1,0:T(8,128)}, bf16[256,1536]{1,0:T(8,128)(2,1)}, f32[8,1536]{1,0:T(8,128)}, bf16[1536,2048]{1,0:T(8,128)(2,1)}) custom-call(bf16[256,1536]{1,0:T(8,128)(2,1)} %get-tuple-element.50.n2_hbm, bf16[1024,1536]{1,0:T(8,128)(2,1)} %get-tuple-element.51.gf_hbm, ...), custom_call_target="tpu_custom_call" | custom-call | flops 28991029248 | bytes 196608000 | tf_op jit(solution)/shard_map/feed_both/pallas_call | solution.py:1047
  226.8 78.6 %attend_backward.1 = (f32[256,1536]{1,0:T(8,128)}, f32[8,1536]{1,0:T(8,128)}, bf16[1024,1024]{1,0:T(8,128)(2,1)}, bf16[1536,1024]{1,0:T(8,128)(2,1)}, bf16[1024,...) custom-call(bf16[256,1536]{1,0:T(8,128)(2,1)} %get-tuple-element.55.ga_hbm, bf16[1536,512]{1,0:T(8,128)(2,1)} %get-tuple-element.56.wout_hbm, ...), custom_call_target="tpu_custom_call" | custom-call | flops 12884901888 | bytes 157286400 | tf_op jit(solution)/shard_map/attend_backward/pallas_call | solution.py:1381
  305.4 62.3 %input_gradient.1 = (f32[256,1536]{1,0:T(8,128)}, f32[1,2,1536]{2,1,0:T(2,128)}, f32[1,4]{1,0:T(1,128)}, f32[192,384]{1,0:T(8,128)}, f32[192,768]{1,0:T(8,128)}, /*index=5*/f32[192,1024]{1,0:T(8,128)}) custom-call(bf16[1024,1024]{1,0:T(8,128)(2,1)} %get-tuple-element.68.dqkv_hbm, bf16[1536,1024]{1,0:T(8,128)(2,1)} %get-tuple-element.69.wqkv_hbm, ...), custom_call_target="tpu_custom_call" | custom-call | flops 3221225472 | bytes 117964800 | tf_op jit(solution)/shard_map/input_gradient/pallas_call | solution.py:1751
  367.7 5.0 %deliver.1 = (f32[256,1536]{1,0:T(8,128)}, f32[256,1536]{1,0:T(8,128)}, f32[192,768]{1,0:T(8,128)}, f32[192,2,1024]{2,1,0:T(2,128)}, f32[192,384]{1,0:T(8,128)},...) custom-call(f32[256,1536]{1,0:T(8,128)} %get-tuple-element.67.refs_0_, ...), custom_call_target="tpu_custom_call" | custom-call | tf_op jit(solution)/shard_map/deliver/pallas_call | solution.py:1832
  (2 shorter events, 0.0 us)

commit v5 on v4

--- a/solution.py
+++ b/solution.py
@@ -889,6 +889,8 @@
         return Scatter(n, sums.at[chunk], rs_send.at[chunk], rs_recv.at[chunk])
 
     gather_of(0).begin_where(True)
+    if chunks > 1:
+        gather_of(1).begin_where(True)
     for chunk in range(chunks):
         gather_of(chunk).begin_where(False)
 
@@ -963,9 +965,9 @@
                 for side in range(2):
                     gather_of(chunk).arrive(step, side, step < n - 1)
 
-        @pl.when(index + 1 < chunks)
+        @pl.when(index + 2 < chunks)
         def _():
-            gather_of(index + 1).begin_where(True)
+            gather_of(index + 2).begin_where(True)
 
         ready = index - (n - 2)
 
@@ -979,17 +981,6 @@
                 def _(side=side, target=target):
                     scatter.push(step, side, part.at[chunk], target * piece)
 
-        for step in range(n - 1, 1, -1):
-            chunk = ready - LAG * (step - 1)
-
-            @pl.when(within(chunk))
-            def _(step=step, chunk=chunk):
-                push(chunk, step, False)
-
-        @pl.when(within(ready - LAG * (n - 1)))
-        def _():
-            scatter_end(ready - LAG * (n - 1))
-
         @pl.when(ready == 0)
         def _():
             load_gu.wait()
@@ -1000,6 +991,17 @@
             compute(ready)
             for step in range(1, n):
                 push(ready, step, True)
+
+        for step in range(n - 1, 1, -1):
+            chunk = ready - LAG * (step - 1)
+
+            @pl.when(within(chunk))
+            def _(step=step, chunk=chunk):
+                push(chunk, step, False)
+
+        @pl.when(within(ready - LAG * (n - 1)))
+        def _():
+            scatter_end(ready - LAG * (n - 1))
 
         late, turns = ready - chunks, LAG * (n - 1)
 

time: 373 us -> 373 us (level)
  no operation moved by 1% of the time
where the time goes in v5:
time: 373 us
  Pallas kernels  371 us (99%)
    pallas_call x1, Pallas kernels, forward(): pl.pallas_call(functools.partial(forward_kernel, n, dp, kv_local), out_sh...  132 us
    pallas_call x1, Pallas kernels, feed(): pl.pallas_call(functools.partial(feed_kernel, n, chunks), out_shape=(jax....  93 us
    pallas_call x1, Pallas kernels, attend_back(): pl.pallas_call(functools.partial(attend_back_kernel, n, dp, kv_local, chu...  78.6 us
    pallas_call x1, Pallas kernels, last(): pl.pallas_call(functools.partial(last_kernel, n, dp, tokens * width * dp...  62.8 us

profile of v5, /device:TPU:0, one launch (start us, length us, event | category | flops | bytes accessed | tf_op | source)
XLA Modules:
  0.0 372.8 jit_solution(14146001297515155530)
XLA Ops:
  0.7 0.6 maximum_bitcast_fusion.freq_ref
  1.2 131.9 %attend_forward.1 = (bf16[1536,1024]{1,0:T(8,128)(2,1)}, bf16[1536,512]{1,0:T(8,128)(2,1)}, bf16[1536,2048]{1,0:T(8,128)(2,1)}, bf16[1536,1024]{1,0:T(8,128)(2,1...) custom-call(f32[256,1536]{1,0:T(8,128)} %x_hbm.1, ...), custom_call_target="tpu_custom_call" | custom-call | flops 6979321856 | bytes 157286400 | tf_op jit(solution)/shard_map/attend_forward/pallas_call | solution.py:748
  133.2 93.0 %feed_both.1 = (bf16[1024,1024]{1,0:T(8,128)(2,1)}, f32[256,1536]{1,0:T(8,128)}, bf16[256,1536]{1,0:T(8,128)(2,1)}, f32[8,1536]{1,0:T(8,128)}, bf16[1536,2048]{1,0:T(8,128)(2,1)}) custom-call(bf16[256,1536]{1,0:T(8,128)(2,1)} %get-tuple-element.50.n2_hbm, bf16[1024,1536]{1,0:T(8,128)(2,1)} %get-tuple-element.51.gf_hbm, ...), custom_call_target="tpu_custom_call" | custom-call | flops 28991029248 | bytes 196608000 | tf_op jit(solution)/shard_map/feed_both/pallas_call | solution.py:1049
  226.1 78.6 %attend_backward.1 = (f32[256,1536]{1,0:T(8,128)}, f32[8,1536]{1,0:T(8,128)}, bf16[1024,1024]{1,0:T(8,128)(2,1)}, bf16[1536,1024]{1,0:T(8,128)(2,1)}, bf16[1024,...) custom-call(bf16[256,1536]{1,0:T(8,128)(2,1)} %get-tuple-element.55.ga_hbm, bf16[1536,512]{1,0:T(8,128)(2,1)} %get-tuple-element.56.wout_hbm, ...), custom_call_target="tpu_custom_call" | custom-call | flops 12884901888 | bytes 157286400 | tf_op jit(solution)/shard_map/attend_backward/pallas_call | solution.py:1383
  304.8 62.8 %input_gradient.1 = (f32[256,1536]{1,0:T(8,128)}, f32[1,2,1536]{2,1,0:T(2,128)}, f32[1,4]{1,0:T(1,128)}, f32[192,384]{1,0:T(8,128)}, f32[192,768]{1,0:T(8,128)}, /*index=5*/f32[192,1024]{1,0:T(8,128)}) custom-call(bf16[1024,1024]{1,0:T(8,128)(2,1)} %get-tuple-element.68.dqkv_hbm, bf16[1536,1024]{1,0:T(8,128)(2,1)} %get-tuple-element.69.wqkv_hbm, ...), custom_call_target="tpu_custom_call" | custom-call | flops 3221225472 | bytes 117964800 | tf_op jit(solution)/shard_map/input_gradient/pallas_call | solution.py:1753
  367.6 5.0 %deliver.1 = (f32[256,1536]{1,0:T(8,128)}, f32[256,1536]{1,0:T(8,128)}, f32[192,768]{1,0:T(8,128)}, f32[192,2,1024]{2,1,0:T(2,128)}, f32[192,384]{1,0:T(8,128)},...) custom-call(f32[256,1536]{1,0:T(8,128)} %get-tuple-element.67.refs_0_, ...), custom_call_target="tpu_custom_call" | custom-call | tf_op jit(solution)/shard_map/deliver/pallas_call | solution.py:1834
  (2 shorter events, 0.0 us)

commit v6 on v4

--- a/solution.py
+++ b/solution.py
@@ -889,6 +889,8 @@
         return Scatter(n, sums.at[chunk], rs_send.at[chunk], rs_recv.at[chunk])
 
     gather_of(0).begin_where(True)
+    if chunks > 1:
+        gather_of(1).begin_where(True)
     for chunk in range(chunks):
         gather_of(chunk).begin_where(False)
 
@@ -963,9 +965,9 @@
                 for side in range(2):
                     gather_of(chunk).arrive(step, side, step < n - 1)
 
-        @pl.when(index + 1 < chunks)
+        @pl.when(index + 2 < chunks)
         def _():
-            gather_of(index + 1).begin_where(True)
+            gather_of(index + 2).begin_where(True)
 
         ready = index - (n - 2)
 

time: 373 us -> 372 us (level)
  no operation moved by 1% of the time
where the time goes in v6:
time: 372 us
  Pallas kernels  371 us (100%)
    pallas_call x1, Pallas kernels, forward(): pl.pallas_call(functools.partial(forward_kernel, n, dp, kv_local), out_sh...  132 us
    pallas_call x1, Pallas kernels, feed(): pl.pallas_call(functools.partial(feed_kernel, n, chunks), out_shape=(jax....  92.4 us
    pallas_call x1, Pallas kernels, attend_back(): pl.pallas_call(functools.partial(attend_back_kernel, n, dp, kv_local, chu...  78.6 us
    pallas_call x1, Pallas kernels, last(): pl.pallas_call(functools.partial(last_kernel, n, dp, tokens * width * dp...  62.8 us

profile of v6, /device:TPU:0, one launch (start us, length us, event | category | flops | bytes accessed | tf_op | source)
XLA Modules:
  0.0 372.2 jit_solution(13457222395177016153)
XLA Ops:
  0.7 0.6 maximum_bitcast_fusion.freq_ref
  1.2 131.9 %attend_forward.1 = (bf16[1536,1024]{1,0:T(8,128)(2,1)}, bf16[1536,512]{1,0:T(8,128)(2,1)}, bf16[1536,2048]{1,0:T(8,128)(2,1)}, bf16[1536,1024]{1,0:T(8,128)(2,1...) custom-call(f32[256,1536]{1,0:T(8,128)} %x_hbm.1, ...), custom_call_target="tpu_custom_call" | custom-call | flops 6979321856 | bytes 157286400 | tf_op jit(solution)/shard_map/attend_forward/pallas_call | solution.py:748
  133.2 92.4 %feed_both.1 = (bf16[1024,1024]{1,0:T(8,128)(2,1)}, f32[256,1536]{1,0:T(8,128)}, bf16[256,1536]{1,0:T(8,128)(2,1)}, f32[8,1536]{1,0:T(8,128)}, bf16[1536,2048]{1,0:T(8,128)(2,1)}) custom-call(bf16[256,1536]{1,0:T(8,128)(2,1)} %get-tuple-element.50.n2_hbm, bf16[1024,1536]{1,0:T(8,128)(2,1)} %get-tuple-element.51.gf_hbm, ...), custom_call_target="tpu_custom_call" | custom-call | flops 28991029248 | bytes 196608000 | tf_op jit(solution)/shard_map/feed_both/pallas_call | solution.py:1049
  225.6 78.6 %attend_backward.1 = (f32[256,1536]{1,0:T(8,128)}, f32[8,1536]{1,0:T(8,128)}, bf16[1024,1024]{1,0:T(8,128)(2,1)}, bf16[1536,1024]{1,0:T(8,128)(2,1)}, bf16[1024,...) custom-call(bf16[256,1536]{1,0:T(8,128)(2,1)} %get-tuple-element.55.ga_hbm, bf16[1536,512]{1,0:T(8,128)(2,1)} %get-tuple-element.56.wout_hbm, ...), custom_call_target="tpu_custom_call" | custom-call | flops 12884901888 | bytes 157286400 | tf_op jit(solution)/shard_map/attend_backward/pallas_call | solution.py:1383
  304.2 62.8 %input_gradient.1 = (f32[256,1536]{1,0:T(8,128)}, f32[1,2,1536]{2,1,0:T(2,128)}, f32[1,4]{1,0:T(1,128)}, f32[192,384]{1,0:T(8,128)}, f32[192,768]{1,0:T(8,128)}, /*index=5*/f32[192,1024]{1,0:T(8,128)}) custom-call(bf16[1024,1024]{1,0:T(8,128)(2,1)} %get-tuple-element.68.dqkv_hbm, bf16[1536,1024]{1,0:T(8,128)(2,1)} %get-tuple-element.69.wqkv_hbm, ...), custom_call_target="tpu_custom_call" | custom-call | flops 3221225472 | bytes 117964800 | tf_op jit(solution)/shard_map/input_gradient/pallas_call | solution.py:1753
  367.0 5.0 %deliver.1 = (f32[256,1536]{1,0:T(8,128)}, f32[256,1536]{1,0:T(8,128)}, f32[192,768]{1,0:T(8,128)}, f32[192,2,1024]{2,1,0:T(2,128)}, f32[192,384]{1,0:T(8,128)},...) custom-call(f32[256,1536]{1,0:T(8,128)} %get-tuple-element.67.refs_0_, ...), custom_call_target="tpu_custom_call" | custom-call | tf_op jit(solution)/shard_map/deliver/pallas_call | solution.py:1834
  (2 shorter events, 0.0 us)
